TPU v7x, 256 devices: a whole 4x4x8 slice. The times are simulated.
256 devices in a mesh: blk: 64 (over z, y, x_lo), pix: 4 (over x_hi, core).
Axes of the slice: x: 4 (x_hi: 2, x_lo: 2; x = x_hi * 2 + x_lo), y: 4, z: 8, core: 2. Of those that a mesh axis runs over, the one named last changes fastest.
Arguments:
- pixels: bfloat16 [262144, 224], P(('blk', 'pix')), may hold values from -6 to 6
- bundles: bfloat16 [128, 224, 64], P('blk'), may hold values from -0.375 to 0.375
- assign: int32 [262144, 1], P(('blk', 'pix')), may hold values from 0 to 127; in each aligned block of 1024 rows (0 to 1023, 1024 to 2047, ...) at most 16 rows name the same one
Outputs:
- abundances: float32 [262144, 64], P(('blk', 'pix'))
- residual_energy: float32 [64, 128], P('blk')
Inputs may be any that keep to these rules, and one draw needn't show every extreme that they name: `assign`: among the 1024 rows of one device no bundle is named more than 16 times; in every draw some device names some bundle exactly 16 times; every bundle is named somewhere.
All inputs are finite; a program needn't handle non-finite values. Where the computation divides by a largest or mean magnitude, that divisor is 1e-20 or more.
Results may differ from a plain program's by a relative error of at most 0.0003.
Values may be sent and summed in bfloat16 or wider, within the bound.
No kernel may reach another device: no remote copies, remote signals or barrier semaphores. Data moves between devices by JAX's collectives and lax.ppermute only.
A program may use at most 64 MiB of HBM per device.

v0:
```python
import math

import jax
import jax.numpy as jnp
from jax import lax
from jax.sharding import PartitionSpec as P

ITERS = 8


sum_weight = 0.015625


def sent_together(arrays, axis, split_dim, concat_dim, along):
    widths = [math.prod(a.shape[along:]) for a in arrays]
    both = jnp.concatenate(
        [a.reshape(*a.shape[:along], w) for a, w in zip(arrays, widths)], axis=along
    )
    filled = lax.all_to_all(both, axis, split_axis=split_dim, concat_axis=concat_dim, tiled=True)
    tiles = jnp.split(filled, [sum(widths[:k]) for k in range(1, len(widths))], axis=along)
    return tuple(
        (b.reshape(*filled.shape[:along], *a.shape[along:]) for a, b in zip(arrays, tiles))
    )


def from_everyone(array, axis):
    copies = jnp.broadcast_to(array, (lax.axis_size(axis), *array.shape))
    return lax.all_to_all(copies, axis, split_axis=0, concat_axis=0, tiled=True)


def taken_together(array, axis):
    everything = from_everyone(array, axis)
    return jnp.sum(everything, axis=0)


def make_slots(assign, count, cap):
    labels = assign[:, 0]
    onehot = (labels[:, None] == jnp.arange(count, dtype=jnp.int32)[None, :]).astype(jnp.int32)
    ranked = jnp.sum(jnp.cumsum(onehot, axis=0) * onehot, axis=1) - 1
    return labels * cap + ranked


def gram_of(spectra):
    gram = (
        jnp.einsum("nbm,nbk->nmk", spectra, spectra, preferred_element_type=jnp.float32)
        + sum_weight
    )
    step = 1.0 / jnp.max(jnp.sum(jnp.abs(gram), axis=2), axis=1)
    return (gram, step)


def solve(blocks, spectra, gram, step):
    target = (
        jnp.einsum("nsb,nbm->nsm", blocks, spectra, preferred_element_type=jnp.float32) + sum_weight
    )

    def sweep(index, state):
        grad = jnp.einsum("nsm,nmk->nsk", state, gram, precision=lax.Precision.HIGHEST)
        return jnp.maximum(state - step[:, None, None] * (grad - target), 0.0)

    state = lax.fori_loop(0, ITERS, sweep, jnp.zeros_like(target))
    fitted = jnp.einsum(
        "nsm,nbm->nsb", state, spectra.astype(jnp.float32), precision=lax.Precision.HIGHEST
    )
    misfit = blocks.astype(jnp.float32) - fitted
    return (state, jnp.sum(misfit * misfit, axis=-1))


def per_device(pixels, bundles, assign):
    rows, bands = pixels.shape
    width = bundles.shape[2]
    owned = bundles.shape[0]
    count = lax.axis_size("blk") * owned
    cap = 2 * rows // count
    slots = make_slots(assign, count, cap)
    flat = jnp.zeros((count * cap, bands), jnp.bfloat16).at[slots].set(pixels)
    buckets = flat.reshape(count, cap, bands)
    valid = jnp.zeros((count * cap,), jnp.float32).at[slots].set(1.0).reshape(count, cap)
    gram, step = gram_of(bundles)
    received = lax.all_to_all(buckets, "blk", split_axis=0, concat_axis=0, tiled=True)
    sources = received.shape[0] // owned
    held = received.shape[1]
    grouped = received.reshape(sources, owned, held, bands).transpose(1, 0, 2, 3)
    state, misfit = solve(grouped.reshape(owned, sources * held, bands), bundles, gram, step)
    state = state.reshape(owned, sources, held, width).transpose(1, 0, 2, 3)
    misfit = misfit.reshape(owned, sources, held).transpose(1, 0, 2)
    states_out = state.reshape(sources * owned, held, width)
    misfit_out = misfit.reshape(sources * owned, held)
    states, misfits = sent_together((states_out, misfit_out), "blk", 0, 0, 2)
    chosen = states.reshape(count * cap, width)[slots]
    scale = bands * rows * lax.axis_size("pix") / count
    energy = jnp.sum(misfits * valid / scale, axis=1)
    total = taken_together(energy, "pix")
    return (chosen, total[None, :])


def solution(mesh):
    placed = (P(("blk", "pix"), None), P("blk", None, None), P(("blk", "pix"), None))
    return jax.shard_map(
        per_device,
        mesh=mesh,
        in_specs=placed,
        out_specs=(P(("blk", "pix"), None), P("blk", None)),
        check_vma=False,
    )
```

profile of v0, /device:TPU:1, one launch (start us, length us, event | category | flops | bytes accessed | tf_op | source)
XLA Modules:
  0.0 108.1 jit_solution(12076767840613863527)
XLA Ops:
  0.6 0.8 copy.46
  3.0 6.0 %scatter_custom_fusion = bf16[2048,224]{1,0:T(8,128)(2,1)} fusion(s32[1024]{0:T(1024)S(1)} %bitcast.52, bf16[1024,224]{1,0:T(8,128)(2,1)S(1)} %copy.48, bf16[]{:T(256)} %constant.21.clone.1), kind=kCustom, calls=%fused_computation.21 | custom fusion | bytes 917506 | tf_op jit(solution)/shard_map/scatter | solution.py:76
  9.1 13.6 %all-to-all-start = ((bf16[128,16,224]{2,1,0:T(8,128)(2,1)}), bf16[128,16,224]{2,1,0:T(8,128)(2,1)S(1)}, u32[]{:S(2)}, u32[]{:S(2)}) async-start(bf16[128,16,224]{2,1,0:T(8,128)(2,1)} %bitcast.7), calls=%async_computation | async-start | bytes 2097152 | tf_op jit(solution)/shard_map/all_to_all | solution.py:80
  23.0 25.8 %all-to-all-done = bf16[128,16,224]{2,1,0:T(8,128)(2,1)S(1)} async-done(((bf16[128,16,224]{2,1,0:T(8,128)(2,1)}), bf16[128,16,224]{2,1,0:T(8,128)(2,1)S(1)}, u32[]{:S(2)}, u32[]{:S(2)}) %all-to-all-start) | async-done | bytes 917536 | tf_op jit(solution)/shard_map/all_to_all | solution.py:80
  49.8 6.0 %while.11 = (s32[]{:T(128)}, f32[2,1024,64]{1,2,0:T(8,128)S(1)}, f32[2]{0:T(128)S(1)}, f32[2,64,64]{1,2,0:T(8,128)S(1)}, f32[2,1024,64]{1,2,0:T(8,128)S(1)}, /*index=5*/s32[]{:T(128)}, s32[]{:T(128)}) while((s32[]{:T(128)}, f32[2,1024,64]{1,2,0:T(8,128)S(1)}, f32[2]{0:T(128)S(1)}, f32[2,64,64]{1,2,0:T(8,128)S(1)}, ...), condition=%wide.region_7.8_spmd.clone, body=%wide.region_6.7_spmd.clone.sunk | while | flops 101449728 | bytes 2654303 | solution.py:61
  49.8 0.7 fusion.29
  50.6 0.7 fusion.29
  51.3 0.7 fusion.29
  52.1 0.7 fusion.29
  52.8 0.7 fusion.29
  53.6 0.7 fusion.29
  54.3 0.7 fusion.29
  55.1 0.7 fusion.29
  56.1 1.0 multiply_reduce_fusion
  57.3 0.8 copy.55
  58.3 1.3 %pad_maximum_fusion = f32[128,16,65]{2,1,0:T(8,128)} fusion(f32[128,16,1]{2,1,0:T(8,128)S(1)} %copy.55, f32[128,16,64]{2,1,0:T(8,128)S(1)} %bitcast.45), kind=kLoop, calls=%fused_computation.14 | loop fusion | flops 133120 | bytes 1064960 | tf_op jit(solution)/shard_map/concatenate | solution.py:16
  59.6 8.0 %all-to-all-start.1 = ((f32[128,16,65]{2,1,0:T(8,128)}), f32[128,16,65]{2,1,0:T(8,128)S(1)}, u32[]{:S(2)}, u32[]{:S(2)}) async-start(f32[128,16,65]{2,1,0:T(8,128)} %pad_maximum_fusion), calls=%async_computation.1 | async-start | bytes 2097152 | tf_op jit(solution)/shard_map/all_to_all | solution.py:19
  67.6 4.3 %scatter_custom_fusion.1 = f32[2048]{0:T(1024)S(1)} fusion(s32[1024]{0:T(1024)S(1)} %bitcast.53, f32[1024]{0:T(1024)S(1)} %broadcast.56, f32[]{:T(128)} %constant.17.clone.1), kind=kCustom, calls=%fused_computation.31 | custom fusion | bytes 8196 | tf_op jit(solution)/shard_map/scatter | solution.py:78
  72.0 21.4 %all-to-all-done.1 = f32[128,16,65]{2,1,0:T(8,128)S(1)} async-done(((f32[128,16,65]{2,1,0:T(8,128)}), f32[128,16,65]{2,1,0:T(8,128)S(1)}, u32[]{:S(2)}, u32[]{:S(2)}) %all-to-all-start.1) | async-done | bytes 532512 | tf_op jit(solution)/shard_map/all_to_all | solution.py:19
  94.2 0.6 broadcast_in_dim.23
  94.8 8.2 %all-to-all-start.2 = ((f32[4,1,128]{2,1,0:T(1,128)}), f32[4,1,128]{2,1,0:T(1,128)S(1)}, u32[]{:S(2)}, u32[]{:S(2)}) async-start(f32[4,1,128]{2,1,0:T(1,128)} %broadcast_in_dim.23), calls=%async_computation.2 | async-start | bytes 4096 | tf_op jit(solution)/shard_map/all_to_all | solution.py:28
  103.0 2.8 %gather_fusion = f32[1024,64]{1,0:T(8,128)S(1)} fusion(f32[2048,64]{1,0:T(8,128)S(1)} %bitcast.42, s32[1024]{0:T(1024)S(1)} %broadcast_clamp_fusion), kind=kCustom, calls=%fused_computation | custom fusion | bytes 528384 | tf_op jit(solution)/shard_map/gather | solution.py:90
  105.8 0.9 copy.59
  106.7 0.9 all-to-all-done.2
  (43 shorter events, 5.2 us)
Async XLA Ops:
  0.6 22.0 %copy-start = (bf16[2,224,64]{1,2,0:T(8,128)(2,1)S(1)}, bf16[2,224,64]{1,2,0:T(8,128)(2,1)}, u32[]{:S(2)}) copy-start(bf16[2,224,64]{1,2,0:T(8,128)(2,1)} %param.6) | copy-start | bytes 172036
  1.7 0.7 copy-start.2
  1.8 1.0 copy-start.1
  9.1 39.7 %all-to-all-start = ((bf16[128,16,224]{2,1,0:T(8,128)(2,1)}), bf16[128,16,224]{2,1,0:T(8,128)(2,1)S(1)}, u32[]{:S(2)}, u32[]{:S(2)}) async-start(bf16[128,16,224]{2,1,0:T(8,128)(2,1)} %bitcast.7), calls=%async_computation | async-start | bytes 2097152 | tf_op jit(solution)/shard_map/all_to_all | solution.py:80
  59.6 33.8 %all-to-all-start.1 = ((f32[128,16,65]{2,1,0:T(8,128)}), f32[128,16,65]{2,1,0:T(8,128)S(1)}, u32[]{:S(2)}, u32[]{:S(2)}) async-start(f32[128,16,65]{2,1,0:T(8,128)} %pad_maximum_fusion), calls=%async_computation.1 | async-start | bytes 2097152 | tf_op jit(solution)/shard_map/all_to_all | solution.py:19
  94.8 12.8 %all-to-all-start.2 = ((f32[4,1,128]{2,1,0:T(1,128)}), f32[4,1,128]{2,1,0:T(1,128)S(1)}, u32[]{:S(2)}, u32[]{:S(2)}) async-start(f32[4,1,128]{2,1,0:T(1,128)} %broadcast_in_dim.23), calls=%async_computation.2 | async-start | bytes 4096 | tf_op jit(solution)/shard_map/all_to_all | solution.py:28
where the time goes:
time: 109 us; the launch traced here: 108 us
  waiting for transfers between devices  48 us (44%)
  starting transfers between devices  29.7 us (27%)
  local copies, waits for them, and re-layouts  19.5 us (18%)
  matrix products  7.09 us (7%)
  other arithmetic  2.67 us (2%)
    all_to_all x1, waiting for transfers between devices, per_device(): lax.all_to_all(buckets, 'blk', split_axis=0, concat_axis=0, tiled=True)  25.8 us
    all_to_all x1, waiting for transfers between devices, sent_together(): lax.all_to_all(both, axis, split_axis=split_dim, concat_axis=concat_dim,...  21.4 us
    all_to_all x1, starting transfers between devices, per_device(): lax.all_to_all(buckets, 'blk', split_axis=0, concat_axis=0, tiled=True)  13.6 us
    all_to_all x1, starting transfers between devices, from_everyone(): return lax.all_to_all(copies, axis, split_axis=0, concat_axis=0, tiled=True)  8.2 us
    all_to_all x1, starting transfers between devices, sent_together(): lax.all_to_all(both, axis, split_axis=split_dim, concat_axis=concat_dim,...  7.96 us
    scatter x1, local copies, waits for them, and re-layouts, per_device(): flat = jnp.zeros((count * cap, bands), jnp.bfloat16).at[slots].set(pixels)  6.03 us
    dot_general x8, matrix products, sweep(): jnp.einsum('nsm,nmk->nsk', state, gram, precision=lax.Precision.HIGHEST)  5.44 us
    scatter x1, local copies, waits for them, and re-layouts, per_device(): jnp.zeros((count * cap,), jnp.float32).at[slots].set(1.0)  4.32 us
  transfers between devices with their start and end apart: 3, of which 3 were waited for; matrix products, arithmetic and copies ran while one was open for 8% of the time, Pallas kernels for 0%

commit v1 on v0

v1 whole, which is shorter than its diff:
```python
import jax
import jax.numpy as jnp
from jax import lax
from jax.experimental import pallas as pl
from jax.experimental.pallas import tpu as pltpu
from jax.sharding import PartitionSpec as P

ITERS = 8
CAP = 16
LANES = 256
ROOT = 0.125
PACK = 4
ALL = ("blk", "pix")
f32, bf16 = jnp.float32, jnp.bfloat16
NT = (((1,), (1,)), ((), ()))


def iota(shape, dim):
    return lax.broadcasted_iota(jnp.int32, shape, dim)


def split(x):
    high = x.astype(bf16)
    return high, (x - high.astype(f32)).astype(bf16)


def dot(a, b):
    return jnp.dot(a, b, preferred_element_type=f32)


def dot_nt(a, b):
    return lax.dot_general(a, b, NT, preferred_element_type=f32)


def prep_kernel(place, bundles, out, wide):
    bands, width = bundles.shape[1:]
    rows = out.shape[1]
    wide[:bands] = bundles[place[0]]
    added = iota((LANES - bands, width), 0) == 0
    wide[bands:] = jnp.where(added, ROOT, 0.0).astype(bf16)
    pick = iota((rows, width), 1) == iota((rows, width), 0) + place[1] * rows
    piece = dot_nt(pick.astype(f32).astype(bf16), wide[...]).astype(bf16)
    for i in range(out.shape[0]):
        out[i] = piece


def slots_kernel(place, labels, pixels, keep, send, code, wide, ranks):
    rows, bands = pixels.shape
    count = rows // (CAP // 2)
    wide[...] = jnp.where(iota(wide.shape, 1) == bands, ROOT, 0.0).astype(bf16)
    wide[:, :bands] = pixels[...]
    label = labels[...]
    chunk = 256
    upper = (iota((chunk, chunk), 0) <= iota((chunk, chunk), 1)).astype(f32).astype(bf16)
    carry = jnp.zeros((count, 1), f32)
    for q in range(rows // chunk):
        part = slice(q * chunk, (q + 1) * chunk)
        named = (iota((count, chunk), 0) == label[:, part]).astype(f32)
        running = dot(named.astype(bf16), upper) + carry
        ranks[:, part] = jnp.sum(named * running, axis=0, keepdims=True) - 1.0
        carry = running[:, chunk - 1 :]
    rank = ranks[...].astype(jnp.int32)
    away = (label & 1) ^ place[0]
    local = ((label >> 1) & 7) * 8 + (label >> 4)
    slot = local * CAP + rank
    kept = jnp.where(away == 0, slot, -1)
    sent = jnp.where(away == 1, slot, -1)
    for key, out in ((kept, keep), (sent, send)):
        for q in range(out.shape[0] // chunk):
            pick = (iota((chunk, rows), 0) + q * chunk == key).astype(f32).astype(bf16)
            out[q * chunk : (q + 1) * chunk] = dot(pick, wide[...]).astype(bf16)
    codes = away * 1024 + (local & 3) * 256 + (local >> 2) * CAP + rank
    code[...] = jnp.broadcast_to(codes.astype(f32), (8, rows)).T


def gathered(bundles, group):
    z = bundles.shape[2]
    tiles = []
    for i in range(PACK * group, PACK * group + PACK):
        tiles += [bundles[i // z, 0, i % z], bundles[i // z, 1, i % z]]
    return jnp.concatenate(tiles, axis=0)


def solve_kernel(place, bundles, mine, theirs, mine_out, theirs_out, energy, high, low, goal, state, steps, sums, parts, scale):
    groups = state.shape[0]
    wide = LANES // PACK
    block = iota((1, LANES), 1) // wide
    same = iota((LANES, LANES), 0) // wide == iota((LANES, LANES), 1) // wide
    for g in range(groups):
        basis = gathered(bundles, g)
        gram = jnp.where(same, dot_nt(basis, basis), 0.0)
        sums[g : g + 1] = jnp.sum(jnp.abs(gram), axis=0, keepdims=True)
        high[g], low[g] = split(gram)
        rows = []
        for i in range(PACK * g, PACK * g + PACK):
            rows += [mine[i * CAP : (i + 1) * CAP], theirs[i * CAP : (i + 1) * CAP]]
        found = dot_nt(jnp.concatenate(rows, axis=0), basis)
        goal[g] = sum(jnp.where(block == i, found[i * 2 * CAP : (i + 1) * 2 * CAP], 0.0) for i in range(PACK))
    total = sums[...]
    largest = jnp.zeros_like(total)
    for i in range(PACK):
        inside = block == i
        largest = jnp.where(inside, jnp.max(jnp.where(inside, total, 0.0), axis=1, keepdims=True), largest)
    steps[...] = 1.0 / largest
    for g in range(groups):
        state[g] = jnp.maximum(steps[g : g + 1] * goal[g], 0.0)

    def sweep(index, carry):
        for g in range(groups):
            a = state[g]
            first, second = split(a)
            both = dot(jnp.concatenate([first, second], axis=0), high[g])
            grad = both[: 2 * CAP] + both[2 * CAP :] + dot(first, low[g])
            state[g] = jnp.maximum(a - steps[g : g + 1] * (grad - goal[g]), 0.0)
        return carry

    lax.fori_loop(1, ITERS, sweep, 0)
    z = bundles.shape[2]
    for g in range(groups):
        a = state[g]
        mine_out[g * CAP : (g + 1) * CAP] = a[:CAP]
        theirs_out[g * CAP : (g + 1) * CAP] = a[CAP:]
        basis = gathered(bundles, g)
        spread = jnp.concatenate([jnp.where(block == i, a, 0.0) for i in range(PACK)], axis=0)
        both = dot(jnp.concatenate(split(spread), axis=0), basis)
        fitted = both[: PACK * 2 * CAP] + both[PACK * 2 * CAP :]
        for i in range(PACK):
            local = PACK * g + i
            rows = slice(local * CAP, (local + 1) * CAP)
            x = jnp.concatenate([mine[rows], theirs[rows]], axis=0).astype(f32)
            misfit = x - fitted[i * 2 * CAP : (i + 1) * 2 * CAP]
            line = jnp.sum(misfit * misfit, axis=0, keepdims=True)
            spot = 2 * (8 * (local % z) + local // z)
            parts[spot : spot + 2] = jnp.broadcast_to(line, (2, LANES))
    bands = LANES - 32
    held = (iota(parts.shape, 1) < bands) & (iota(parts.shape, 0) % 2 == place[0])
    energy[...] = jnp.sum(jnp.where(held, parts[...], 0.0).T, axis=0, keepdims=True) / scale


def return_kernel(code, mine, back, out):
    rows = code.shape[0]
    held = mine.shape[0]
    codes = code[:, :1].astype(jnp.int32)
    place = codes & 255
    pick = iota((rows, 2 * held), 1) == place + (codes >> 10) * held
    pick = pick.astype(f32).astype(bf16)
    table = jnp.concatenate([mine[...], back[...]], axis=0)
    first = table.astype(bf16)
    rest = table - first.astype(f32)
    second, third = split(rest)
    found = dot(pick, first) + dot(pick, second) + dot(pick, third)
    found = jnp.where(iota(found.shape, 1) // 64 == (codes >> 8) & 3, found, 0.0)
    half = found[:, :128] + found[:, 128:]
    out[...] = half[:, :64] + half[:, 64:]


def vmem(shape, dtype):
    return pltpu.VMEM(shape, dtype)


def call(kernel, place, args, outs, scratch):
    spec = pl.BlockSpec(memory_space=pltpu.VMEM)
    smem = [pl.BlockSpec(memory_space=pltpu.SMEM)] if place is not None else []
    head = [place] if place is not None else []
    return pl.pallas_call(
        kernel,
        out_shape=outs,
        in_specs=smem + [spec] * len(args),
        out_specs=jax.tree.map(lambda _: spec, outs),
        scratch_shapes=scratch,
        compiler_params=pltpu.CompilerParams(vmem_limit_bytes=48 << 20),
    )(*head, *args)


def positions(mesh_pix, along_blk):
    spots = []
    for blk in range(along_blk):
        for pix in range(mesh_pix):
            spots.append((blk // 8, blk // 2 % 4, pix // 2, blk % 2, pix % 2))
    return spots


def grouped(spots, key):
    groups = {}
    for index, spot in enumerate(spots):
        groups.setdefault(key(*spot), []).append(index)
    return list(groups.values())


def copies_from(array, groups):
    return lax.all_to_all(array, ALL, 0, 0, tiled=True, axis_index_groups=groups)


def per_device(pixels, bundles, assign):
    rows, bands = pixels.shape
    owned, _, width = bundles.shape
    n_blk, n_pix = lax.axis_size("blk"), lax.axis_size("pix")
    spots = positions(n_pix, n_blk)
    along_z = grouped(spots, lambda z, y, xh, xl, c: (y, xh, xl, c))
    along_yx = grouped(spots, lambda z, y, xh, xl, c: (z, c))
    pix = lax.axis_index("pix")
    place = jnp.stack([pix % 2, pix // 2]).astype(jnp.int32)
    sds = jax.ShapeDtypeStruct
    half = width // 2
    nz, nyx = len(along_z[0]), len(along_yx[0])

    piece = call(prep_kernel, place, [bundles], sds((nz, half, LANES), bf16), [vmem((LANES, width), bf16)])
    column = copies_from(piece, along_z)
    plane = copies_from(jnp.broadcast_to(column[None], (nyx, nz, half, LANES)), along_yx)

    held = (n_blk * owned // 2) * CAP
    keep, send, code = call(
        slots_kernel,
        place,
        [assign.reshape(1, rows), pixels],
        (sds((held, LANES), bf16), sds((held, LANES), bf16), sds((rows, 8), f32)),
        [vmem((rows, LANES), bf16), vmem((1, rows), f32)],
    )
    sibling = [(i, i ^ 1) for i in range(n_pix)]
    theirs = lax.ppermute(send, "pix", sibling)

    groups = held // CAP // PACK
    scale = bands * rows * n_pix / (n_blk * owned)
    mine_out, theirs_out, energy = call(
        lambda *refs: solve_kernel(*refs, scale=scale),
        place,
        [plane.reshape(nyx // 2, 2, nz, half, LANES), keep, theirs],
        (sds((groups * CAP, LANES), f32), sds((groups * CAP, LANES), f32), sds((1, n_blk * owned), f32)),
        [
            vmem((groups, LANES, LANES), bf16),
            vmem((groups, LANES, LANES), bf16),
            vmem((groups, 2 * CAP, LANES), f32),
            vmem((groups, 2 * CAP, LANES), f32),
            vmem((groups, LANES), f32),
            vmem((groups, LANES), f32),
            vmem((n_blk * owned, LANES), f32),
        ],
    )
    back = lax.ppermute(theirs_out, "pix", sibling)
    total = energy
    for flip in range(1, n_pix):
        total = total + lax.ppermute(energy, "pix", [(i, i ^ flip) for i in range(n_pix)])
    chosen = call(return_kernel, None, [code, mine_out, back], sds((rows, width), f32), [])
    return chosen, total


def solution(mesh):
    placed = (P(("blk", "pix"), None), P("blk", None, None), P(("blk", "pix"), None))
    return jax.shard_map(
        per_device,
        mesh=mesh,
        in_specs=placed,
        out_specs=(P(("blk", "pix"), None), P("blk", None)),
        check_vma=False,
    )
```

time: 109 us -> 76.7 us (0.70)
  waiting for transfers between devices: 48 us -> 22.1 us
  blocking collectives: 0 us -> 16.6 us
  starting transfers between devices: 29.7 us -> 16.5 us
  Pallas kernels: 0 us -> 12.5 us
  local copies, waits for them, and re-layouts: 19.5 us -> 7.33 us
  matrix products: 7.09 us -> 0 us
  other arithmetic: 2.67 us -> 0.59 us
    all_to_all x3 -> x1, waiting for transfers between devices: 48 us -> 17.2 us  [copies_from(): lax.all_to_all(array, ALL, 0, 0, tiled=True, axis_index_groups=groups)]
    all_to_all x3 -> x1, starting transfers between devices: 29.7 us -> 6.89 us  [copies_from(): lax.all_to_all(array, ALL, 0, 0, tiled=True, axis_index_groups=groups)]
    all_to_all x0 -> x1, blocking collectives: none -> 16.6 us  [copies_from(): lax.all_to_all(array, ALL, 0, 0, tiled=True, axis_index_groups=groups)]
    pallas_call x0 -> x4, Pallas kernels: none -> 12.5 us  [call(): pl.pallas_call(kernel, out_shape=outs, in_specs=smem + [spec] * len(args)...]
    scatter x2 -> x0, local copies, waits for them, and re-layouts: 10.4 us -> none  [the longest x1 6.03 us: per_device(): flat = jnp.zeros((count * cap, bands), jnp.bfloat16).at[slots].set(pixels)]
    ppermute x0 -> x5, starting transfers between devices: none -> 9.66 us  [the longest x3 4.38 us: per_device(): lax.ppermute(energy, 'pix', [(i, i ^ flip) for i in range(n_pix)])]
    dot_general x11 -> x0, matrix products: 7.09 us -> none  [the longest x8 5.44 us: sweep(): jnp.einsum('nsm,nmk->nsk', state, gram, precision=lax.Precision.HIGHEST)]
    ppermute x0 -> x5, waiting for transfers between devices: none -> 4.94 us  [the longest x3 3.4 us: per_device(): lax.ppermute(energy, 'pix', [(i, i ^ flip) for i in range(n_pix)])]
  transfers between devices with their start and end apart: 3 -> 6, of which waited for: 3 -> 4; matrix products, arithmetic and copies ran while one was open for 8% -> 1% of each run, Pallas kernels for 0% -> 3%
where the time goes in v1:
time: 76.7 us; the launch traced here: 76.4 us
  waiting for transfers between devices  22.1 us (29%)
  blocking collectives  16.6 us (22%)
  starting transfers between devices  16.5 us (22%)
  Pallas kernels  12.5 us (16%)
  local copies, waits for them, and re-layouts  7.33 us (10%)
    all_to_all x1, waiting for transfers between devices, copies_from(): lax.all_to_all(array, ALL, 0, 0, tiled=True, axis_index_groups=groups)  17.2 us
    all_to_all x1, blocking collectives, copies_from(): lax.all_to_all(array, ALL, 0, 0, tiled=True, axis_index_groups=groups)  16.6 us
    pallas_call x4, Pallas kernels, call(): pl.pallas_call(kernel, out_shape=outs, in_specs=smem + [spec] * len(args)...  12.5 us
    all_to_all x1, starting transfers between devices, copies_from(): lax.all_to_all(array, ALL, 0, 0, tiled=True, axis_index_groups=groups)  6.89 us
    unnamed x15, local copies, waits for them, and re-layouts  5.73 us
    ppermute x3, starting transfers between devices, per_device(): lax.ppermute(energy, 'pix', [(i, i ^ flip) for i in range(n_pix)])  4.38 us
    ppermute x3, waiting for transfers between devices, per_device(): lax.ppermute(energy, 'pix', [(i, i ^ flip) for i in range(n_pix)])  3.4 us
    ppermute x1, starting transfers between devices, per_device(): back = lax.ppermute(theirs_out, 'pix', sibling)  2.71 us
  transfers between devices with their start and end apart: 6, of which 4 were waited for; matrix products, arithmetic and copies ran while one was open for 1% of the time, Pallas kernels for 3%

profile of v1, /device:TPU:1, one launch (start us, length us, event | category | flops | bytes accessed | tf_op | source)
XLA Modules:
  0.0 76.4 jit_solution(5286548390495911215)
XLA Ops:
  0.6 1.0 %copy.6.bundles = bf16[2,224,64]{2,1,0:T(8,128)(2,1)S(1)} copy(bf16[2,224,64]{1,2,0:T(8,128)(2,1)} %param.4) | data formatting | bytes 114688 | tf_op args[1]
  1.6 0.1 pad_add_fusion.place.refs_0_
  1.7 0.7 shard_map.51
  2.4 16.6 %all_to_all.10 = bf16[8,32,256]{2,1,0:T(8,128)(2,1)S(1)} all-to-all(bf16[8,32,256]{2,1,0:T(8,128)(2,1)S(1)} %shard_map.51), channel_id=1, replica_groups={{0,32,64,96,128,160,192,224},{1,33,65,97,129,161,193,225},{2,34,66,98,1..., dimensions={0} | all-to-all | bytes 262144 | tf_op jit(solution)/shard_map/all_to_all | solution.py:191
  19.0 1.6 %broadcast_in_dim.2 = bf16[16,8,32,256]{3,2,1,0:T(8,128)(2,1)} broadcast(bf16[8,32,256]{2,1,0:T(8,128)(2,1)S(1)} %all_to_all.10), dimensions={1,2,3} | broadcast | bytes 2228224 | tf_op jit(solution)/shard_map/broadcast_in_dim | solution.py:209
  20.6 6.9 %all-to-all-start.1 = ((bf16[16,8,32,256]{3,2,1,0:T(8,128)(2,1)}), bf16[16,8,32,256]{3,2,1,0:T(8,128)(2,1)S(1)}, u32[]{:S(2)}, u32[]{:S(2)}) async-start(bf16[16,8,32,256]{3,2,1,0:T(8,128)(2,1)} %broadcast_in_dim.2), calls=%async_computation.1 | async-start | bytes 4194304 | tf_op jit(solution)/shard_map/all_to_all | solution.py:191
  27.5 0.2 copy.5.pixels
  27.7 2.2 %shard_map.50 = (bf16[1024,256]{1,0:T(8,128)(2,1)S(1)}, bf16[1024,256]{1,0:T(8,128)(2,1)S(1)}, f32[1024,8]{1,0:T(8,128)S(1)}) custom-call(s32[2]{0:T(128)S(1)} %pad_add_fusion.place.refs_0_, s32[1,1024]{1,0:T(1,128)S(1)} %bitcast.5, bf16[1024,224]{1,0:T(8,128)(2,1)S(1)} %copy.5.pixels), custom_call_target="tpu_custom_call" | custom-call | tf_op jit(solution)/shard_map/pallas_call | solution.py:165
  30.0 0.8 %copy-done = bf16[1024,256]{1,0:T(8,128)(2,1)} copy-done((bf16[1024,256]{1,0:T(8,128)(2,1)}, bf16[1024,256]{1,0:T(8,128)(2,1)S(1)}, u32[]{:S(2)}) %copy-start) | copy-done | bytes 524312
  30.7 2.6 %collective-permute-start = (bf16[1024,256]{1,0:T(8,128)(2,1)S(1)}, bf16[1024,256]{1,0:T(8,128)(2,1)S(1)}, u32[]{:S(2)}, u32[]{:S(2)}) collective-permute-start(bf16[1024,256]{1,0:T(8,128)(2,1)S(1)} %get-tuple-element.10), channel_id=1, source_target_pairs={{0,1},{1,0},{2,3},{3,2},{4,5},{5,4},{6,7},{7,6},{8,9},{9,8},{10,11... | collective-permute-start | bytes 1572872 | tf_op jit(solution)/shard_map/ppermute | solution.py:220
  33.3 1.5 %collective-permute-done.refs_3_ = bf16[1024,256]{1,0:T(8,128)(2,1)S(1)} collective-permute-done((bf16[1024,256]{1,0:T(8,128)(2,1)S(1)}, bf16[1024,256]{1,0:T(8,128)(2,1)S(1)}, u32[]{:S(2)}, u32[]{:S(2)}) %collective-permute-start) | collective-permute-done | bytes 524320 | tf_op jit(solution)/shard_map/ppermute | solution.py:220
  34.8 0.8 %copy-done.2 = bf16[1024,256]{1,0:T(8,128)(2,1)} copy-done((bf16[1024,256]{1,0:T(8,128)(2,1)}, bf16[1024,256]{1,0:T(8,128)(2,1)S(1)}, u32[]{:S(2)}) %copy-start.2) | copy-done | bytes 524312
  35.6 17.2 %all-to-all-done.1 = bf16[16,8,32,256]{3,2,1,0:T(8,128)(2,1)S(1)} async-done(((bf16[16,8,32,256]{3,2,1,0:T(8,128)(2,1)}), bf16[16,8,32,256]{3,2,1,0:T(8,128)(2,1)S(1)}, u32[]{:S(2)}, u32[]{:S(2)}) %all-to-all-start.1) | async-done | bytes 2097184 | tf_op jit(solution)/shard_map/all_to_all | solution.py:191
  52.8 1.0 %copy-done.1 = bf16[1024,256]{1,0:T(8,128)(2,1)S(1)} copy-done((bf16[1024,256]{1,0:T(8,128)(2,1)S(1)}, bf16[1024,256]{1,0:T(8,128)(2,1)}, u32[]{:S(2)}) %copy-start.1) | copy-done | bytes 524312
  53.8 1.0 %copy-done.3 = bf16[1024,256]{1,0:T(8,128)(2,1)S(1)} copy-done((bf16[1024,256]{1,0:T(8,128)(2,1)S(1)}, bf16[1024,256]{1,0:T(8,128)(2,1)}, u32[]{:S(2)}) %copy-start.3) | copy-done | bytes 524312
  54.9 8.4 %shard_map.52 = (f32[256,256]{1,0:T(8,128)S(1)}, f32[256,256]{1,0:T(8,128)S(1)}, f32[1,128]{1,0:T(1,128)S(1)}) custom-call(s32[2]{0:T(128)S(1)} %pad_add_fusion.place.refs_0_, bf16[8,2,8,32,256]{4,3,2,1,0:T(8,128)(2,1)S(1)} %bitcast.4, bf16[1024,256]{1,0:T(8,128)(2,1)S(1)} %copy-done.1, bf16[1024,256]{1,0:T(8,128)(2,1)S(1)} %copy-done.3), custom_call_target="tpu_custom_call" | custom-call | tf_op jit(solution)/shard_map/pallas_call | solution.py:165
  63.3 2.7 %collective-permute-start.1 = (f32[256,256]{1,0:T(8,128)S(1)}, f32[256,256]{1,0:T(8,128)S(1)}, u32[]{:S(2)}, u32[]{:S(2)}) collective-permute-start(f32[256,256]{1,0:T(8,128)S(1)} %get-tuple-element.12), channel_id=1, source_target_pairs={{0,1},{1,0},{2,3},{3,2},{4,5},{5,4},{6,7},{7,6},{8,9},{9,8},{10,11... | collective-permute-start | bytes 786440 | tf_op jit(solution)/shard_map/ppermute | solution.py:239
  66.0 3.9 %collective-permute-start.4 = (f32[1,128]{1,0:T(1,128)S(1)}, f32[1,128]{1,0:T(1,128)S(1)}, u32[]{:S(2)}, u32[]{:S(2)}) collective-permute-start(f32[1,128]{1,0:T(1,128)S(1)} %get-tuple-element.13), channel_id=1, source_target_pairs={{0,3},{1,2},{2,1},{3,0},{4,7},{5,6},{6,5},{7,4},{8,11},{9,10},{10,... | collective-permute-start | bytes 1544 | tf_op jit(solution)/shard_map/ppermute | solution.py:242
  70.0 0.4 collective-permute-start.2
  70.4 0.7 collective-permute-done.4
  71.1 2.7 %collective-permute-done.3 = f32[1,128]{1,0:T(1,128)S(1)} collective-permute-done((f32[1,128]{1,0:T(1,128)S(1)}, f32[1,128]{1,0:T(1,128)S(1)}, u32[]{:S(2)}, u32[]{:S(2)}) %collective-permute-start.3) | collective-permute-done | bytes 544 | tf_op jit(solution)/shard_map/ppermute | solution.py:242
  73.8 0.5 add_add_fusion
  74.3 1.2 %shard_map.53 = f32[1024,64]{1,0:T(8,128)S(1)} custom-call(f32[1024,8]{1,0:T(8,128)S(1)} %get-tuple-element.8.code, f32[256,256]{1,0:T(8,128)S(1)} %get-tuple-element.11.mine, f32[256,256]{1,0:T(8,128)S(1)} %collective-permute-done.1.back), custom_call_target="tpu_custom_call" | custom-call | tf_op jit(solution)/shard_map/pallas_call | solution.py:165
  75.5 0.9 %copy.7 = f32[1024,64]{0,1:T(8,128)} copy(f32[1024,64]{1,0:T(8,128)S(1)} %shard_map.53) | data formatting | bytes 524288
  (11 shorter events, 0.1 us)
Async XLA Ops:
  20.6 6.9 %copy-start.5 = (bf16[1024,224]{0,1:T(8,128)(2,1)S(1)}, bf16[1024,224]{0,1:T(8,128)(2,1)}, u32[]{:S(2)}) copy-start(bf16[1024,224]{0,1:T(8,128)(2,1)} %param.3) | copy-start | bytes 1376260
  20.6 7.1 %copy-start.4 = (s32[1024,1]{0,1:T(1,128)S(1)}, s32[1024,1]{0,1:T(1,128)}, u32[]{:S(2)}) copy-start(s32[1024,1]{0,1:T(1,128)} %param.5) | copy-start | bytes 12292
  20.6 32.2 %all-to-all-start.1 = ((bf16[16,8,32,256]{3,2,1,0:T(8,128)(2,1)}), bf16[16,8,32,256]{3,2,1,0:T(8,128)(2,1)S(1)}, u32[]{:S(2)}, u32[]{:S(2)}) async-start(bf16[16,8,32,256]{3,2,1,0:T(8,128)(2,1)} %broadcast_in_dim.2), calls=%async_computation.1 | async-start | bytes 4194304 | tf_op jit(solution)/shard_map/all_to_all | solution.py:191
  29.9 0.8 %copy-start = (bf16[1024,256]{1,0:T(8,128)(2,1)}, bf16[1024,256]{1,0:T(8,128)(2,1)S(1)}, u32[]{:S(2)}) copy-start(bf16[1024,256]{1,0:T(8,128)(2,1)S(1)} %get-tuple-element.9.refs_2_) | copy-start | bytes 1572868
  30.7 4.1 %collective-permute-start = (bf16[1024,256]{1,0:T(8,128)(2,1)S(1)}, bf16[1024,256]{1,0:T(8,128)(2,1)S(1)}, u32[]{:S(2)}, u32[]{:S(2)}) collective-permute-start(bf16[1024,256]{1,0:T(8,128)(2,1)S(1)} %get-tuple-element.10), channel_id=1, source_target_pairs={{0,1},{1,0},{2,3},{3,2},{4,5},{5,4},{6,7},{7,6},{8,9},{9,8},{10,11... | collective-permute-start | bytes 1572872 | tf_op jit(solution)/shard_map/ppermute | solution.py:220
  34.8 0.8 %copy-start.2 = (bf16[1024,256]{1,0:T(8,128)(2,1)}, bf16[1024,256]{1,0:T(8,128)(2,1)S(1)}, u32[]{:S(2)}) copy-start(bf16[1024,256]{1,0:T(8,128)(2,1)S(1)} %collective-permute-done.refs_3_) | copy-start | bytes 1572868
  52.8 1.0 %copy-start.1 = (bf16[1024,256]{1,0:T(8,128)(2,1)S(1)}, bf16[1024,256]{1,0:T(8,128)(2,1)}, u32[]{:S(2)}) copy-start(bf16[1024,256]{1,0:T(8,128)(2,1)} %copy-done) | copy-start | bytes 1572868
  53.8 1.0 %copy-start.3 = (bf16[1024,256]{1,0:T(8,128)(2,1)S(1)}, bf16[1024,256]{1,0:T(8,128)(2,1)}, u32[]{:S(2)}) copy-start(bf16[1024,256]{1,0:T(8,128)(2,1)} %copy-done.2) | copy-start | bytes 1572868
  63.3 11.0 %collective-permute-start.1 = (f32[256,256]{1,0:T(8,128)S(1)}, f32[256,256]{1,0:T(8,128)S(1)}, u32[]{:S(2)}, u32[]{:S(2)}) collective-permute-start(f32[256,256]{1,0:T(8,128)S(1)} %get-tuple-element.12), channel_id=1, source_target_pairs={{0,1},{1,0},{2,3},{3,2},{4,5},{5,4},{6,7},{7,6},{8,9},{9,8},{10,11... | collective-permute-start | bytes 786440 | tf_op jit(solution)/shard_map/ppermute | solution.py:239
  66.0 5.1 %collective-permute-start.4 = (f32[1,128]{1,0:T(1,128)S(1)}, f32[1,128]{1,0:T(1,128)S(1)}, u32[]{:S(2)}, u32[]{:S(2)}) collective-permute-start(f32[1,128]{1,0:T(1,128)S(1)} %get-tuple-element.13), channel_id=1, source_target_pairs={{0,3},{1,2},{2,1},{3,0},{4,7},{5,6},{6,5},{7,4},{8,11},{9,10},{10,... | collective-permute-start | bytes 1544 | tf_op jit(solution)/shard_map/ppermute | solution.py:242
  69.9 3.9 %collective-permute-start.3 = (f32[1,128]{1,0:T(1,128)S(1)}, f32[1,128]{1,0:T(1,128)S(1)}, u32[]{:S(2)}, u32[]{:S(2)}) collective-permute-start(f32[1,128]{1,0:T(1,128)S(1)} %get-tuple-element.13), channel_id=1, source_target_pairs={{0,2},{1,3},{2,0},{3,1},{4,6},{5,7},{6,4},{7,5},{8,10},{9,11},{10,... | collective-permute-start | bytes 1544 | tf_op jit(solution)/shard_map/ppermute | solution.py:242
  70.0 3.8 %collective-permute-start.2 = (f32[1,128]{1,0:T(1,128)S(1)}, f32[1,128]{1,0:T(1,128)S(1)}, u32[]{:S(2)}, u32[]{:S(2)}) collective-permute-start(f32[1,128]{1,0:T(1,128)S(1)} %get-tuple-element.13), channel_id=1, source_target_pairs={{0,1},{1,0},{2,3},{3,2},{4,5},{5,4},{6,7},{7,6},{8,9},{9,8},{10,11... | collective-permute-start | bytes 1544 | tf_op jit(solution)/shard_map/ppermute | solution.py:242

commit v2 on v1

v2 whole, which is shorter than its diff:
```python
import jax
import jax.numpy as jnp
from jax import lax
from jax.experimental import pallas as pl
from jax.experimental.pallas import tpu as pltpu
from jax.sharding import PartitionSpec as P

ITERS = 8
CAP = 16
LANES = 256
ROOT = 0.125
PACK = 4
ALL = ("blk", "pix")
f32, bf16 = jnp.float32, jnp.bfloat16


def iota(shape, dim):
    return lax.broadcasted_iota(jnp.int32, shape, dim)


def one_hot(where):
    return where.astype(f32).astype(bf16)


def split(x):
    high = x.astype(bf16)
    return high, (x - high.astype(f32)).astype(bf16)


def dot(a, b):
    return jnp.dot(a, b, preferred_element_type=f32)


def dot_nt(a, b):
    return lax.dot_general(a, b, (((1,), (1,)), ((), ())), preferred_element_type=f32)


def prep_kernel(place, bundles, out):
    width, bands = bundles.shape[1:]
    out[...] = jnp.where(iota(out.shape, 1) == bands, ROOT, 0.0).astype(bf16)
    out[:, :bands] = bundles[place[0]]


def slots_kernel(place, labels, pixels, send, code, wide, ranks):
    bands, rows = pixels.shape
    count = rows // (CAP // 2)
    wide[:bands] = pixels[...]
    wide[bands:] = jnp.where(iota((LANES - bands, rows), 0) == 0, ROOT, 0.0).astype(bf16)
    label = labels[...]
    chunk = 256
    upper = one_hot(iota((chunk, chunk), 0) <= iota((chunk, chunk), 1))
    carry = jnp.zeros((count, 1), f32)
    for q in range(rows // chunk):
        part = slice(q * chunk, (q + 1) * chunk)
        named = (iota((count, chunk), 0) == label[:, part]).astype(f32)
        running = dot(named.astype(bf16), upper) + carry
        ranks[:, part] = jnp.sum(named * running, axis=0, keepdims=True) - 1.0
        carry = running[:, chunk - 1 :]
    rank = ranks[...].astype(jnp.int32)
    handler = (label >> 1 & 1) * 4 + ((label >> 4) + place[2] & 1) * 2 + (label & 1)
    local = (label >> 5) * PACK + (label >> 2 & 3)
    slot = local * CAP + rank
    for d in range(send.shape[0]):
        key = jnp.where(handler == d, slot, -1)
        held = send.shape[1]
        send[d] = dot_nt(one_hot(iota((held, rows), 0) == key), wide[...]).astype(bf16)
    table_row = handler * (held // PACK) + (local >> 2) * CAP + rank
    code[...] = (local & 3) * 1024 + table_row


def solve_kernel(place, bundles, pixels, out, high, low, goal, state, steps, sums, parts, scale):
    groups = state.shape[0]
    sources = pixels.shape[0]
    slots = sources * CAP
    wide = LANES // PACK
    block = iota((1, LANES), 1) // wide
    same = iota((LANES, LANES), 0) // wide == iota((LANES, LANES), 1) // wide

    def basis_of(g):
        return jnp.concatenate([bundles[PACK * g + i] for i in range(PACK)], axis=0)

    def pixels_of(local):
        return jnp.concatenate([pixels[s, local * CAP : (local + 1) * CAP] for s in range(sources)], axis=0)

    for g in range(groups):
        basis = basis_of(g)
        gram = jnp.where(same, dot_nt(basis, basis), 0.0)
        sums[g : g + 1] = jnp.sum(jnp.abs(gram), axis=0, keepdims=True)
        high[g], low[g] = split(gram)
        found = dot_nt(jnp.concatenate([pixels_of(PACK * g + i) for i in range(PACK)], axis=0), basis)
        aim = found[:slots]
        for i in range(1, PACK):
            aim = jnp.where(block == i, found[i * slots : (i + 1) * slots], aim)
        goal[g] = aim
    total = sums[...]
    largest = jnp.zeros_like(total)
    for i in range(PACK):
        inside = block == i
        largest = jnp.where(inside, jnp.max(jnp.where(inside, total, 0.0), axis=1, keepdims=True), largest)
    steps[...] = 1.0 / largest
    for g in range(groups):
        state[g] = jnp.maximum(steps[g : g + 1] * goal[g], 0.0)

    def sweep(index, carry):
        for g in range(groups):
            a = state[g]
            first, second = split(a)
            both = dot(jnp.concatenate([first, second], axis=0), high[g])
            grad = both[:slots] + both[slots:] + dot(first, low[g])
            state[g] = jnp.maximum(a - steps[g : g + 1] * (grad - goal[g]), 0.0)
        return carry

    lax.fori_loop(1, ITERS, sweep, 0)
    parts[...] = jnp.zeros(parts.shape, f32)
    odd = place[2] + place[1] & 1
    for g in range(groups):
        a = state[g]
        for s in range(sources):
            out[s, g * CAP : (g + 1) * CAP] = a[s * CAP : (s + 1) * CAP]
        spread = jnp.concatenate([jnp.where(block == i, a, 0.0) for i in range(PACK)], axis=0)
        both = dot(jnp.concatenate(split(spread), axis=0), basis_of(g))
        fitted = both[: PACK * slots] + both[PACK * slots :]
        for i in range(PACK):
            misfit = pixels_of(PACK * g + i).astype(f32) - fitted[i * slots : (i + 1) * slots]
            square = misfit * misfit
            bundle = 16 * (2 * g + odd) + 4 * i + 2 * place[3] + place[0]
            for half in range(2):
                rows = slice(half * slots // 2, (half + 1) * slots // 2)
                parts[half, pl.ds(bundle, 1), :] = jnp.sum(square[rows], axis=0, keepdims=True)
    bands = LANES - 32
    below = groups * CAP
    for half in range(2):
        lines = parts[half].T
        lines = jnp.where(iota(lines.shape, 0) < bands, lines, 0.0)
        energy = jnp.sum(lines, axis=0, keepdims=True) / scale
        energy = jnp.concatenate([energy, jnp.zeros_like(energy)], axis=1)
        for s in range(half * sources // 2, (half + 1) * sources // 2):
            out[s, below:] = jnp.broadcast_to(energy, (8, LANES))


def return_kernel(code, back, chosen, energy):
    rows = code.shape[1]
    handlers, held, lanes = back.shape
    held -= 8
    wide = lanes // PACK
    codes = code[...]
    pick = one_hot(iota((handlers * held, rows), 0) == codes & 1023)
    table = jnp.concatenate([back[d, :held] for d in range(handlers)], axis=0).T
    first = table.astype(bf16)
    rest = table - first.astype(f32)
    second, third = split(rest)
    found = dot(jnp.concatenate([first, second, third], axis=0), pick)
    found = found[:lanes] + found[lanes : 2 * lanes] + found[2 * lanes :]
    which = codes >> 10
    result = found[:wide]
    for i in range(1, PACK):
        result = jnp.where(which == i, found[i * wide : (i + 1) * wide], result)
    chosen[...] = result
    total = back[0, held : held + 1]
    for d in range(1, handlers):
        total = total + back[d, held : held + 1]
    energy[...] = total[:, : energy.shape[1]]


def vmem(shape, dtype):
    return pltpu.VMEM(shape, dtype)


def call(kernel, place, args, outs, scratch, limit):
    spec = pl.BlockSpec(memory_space=pltpu.VMEM)
    head = [] if place is None else [place]
    return pl.pallas_call(
        kernel,
        out_shape=outs,
        in_specs=[pl.BlockSpec(memory_space=pltpu.SMEM)] * len(head) + [spec] * len(args),
        out_specs=jax.tree.map(lambda _: spec, outs),
        scratch_shapes=scratch,
        compiler_params=pltpu.CompilerParams(vmem_limit_bytes=limit << 20),
    )(*head, *args)


def spots_of(n_blk, n_pix):
    return [(b // 8, b // 2 % 4, b % 2, p // 2, p % 2) for b in range(n_blk) for p in range(n_pix)]


def grouped(spots, key):
    groups = {}
    for index, spot in enumerate(spots):
        groups.setdefault(key(*spot), []).append(index)
    return list(groups.values())


def exchanged(array, groups):
    return lax.all_to_all(array, ALL, 0, 0, tiled=True, axis_index_groups=groups)


def per_device(pixels, bundles, assign):
    rows, bands = pixels.shape
    owned, _, width = bundles.shape
    n_blk, n_pix = lax.axis_size("blk"), lax.axis_size("pix")
    spots = spots_of(n_blk, n_pix)
    column = grouped(spots, lambda z, y, xl, xh, c: (z % 2, xl, xh, c))
    row = grouped(spots, lambda z, y, xl, xh, c: (z, y))
    there = {spot: index for index, spot in enumerate(spots)}
    swap = [(there[s], there[(s[0] ^ s[3],) + s[1:]]) for s in spots]
    blk, pix = lax.axis_index("blk"), lax.axis_index("pix")
    place = jnp.stack([pix & 1, pix >> 1, blk >> 3 & 1, blk & 1]).astype(jnp.int32)
    sds = jax.ShapeDtypeStruct
    n_col, n_row = len(column[0]), len(row[0])
    count = n_blk * owned
    held = n_col * CAP
    groups = n_col // PACK

    basis = call(prep_kernel, place, [bundles.transpose(0, 2, 1)], sds((width, LANES), bf16), [], 4)
    basis = lax.ppermute(basis, ALL, swap)
    send, code = call(
        slots_kernel,
        place,
        [assign.reshape(1, rows), pixels.T],
        (sds((n_row, held, LANES), bf16), sds((1, rows), jnp.int32)),
        [vmem((LANES, rows), bf16), vmem((1, rows), f32)],
        16,
    )
    basis, send = lax.optimization_barrier((basis, send))
    gathered = exchanged(jnp.broadcast_to(basis[None], (n_col, width, LANES)), column)
    received = exchanged(send, row)

    below = groups * CAP
    slots = n_row * CAP
    scale = bands * rows * n_pix / count
    solved = call(
        lambda *refs: solve_kernel(*refs, scale=scale),
        place,
        [gathered, received],
        sds((n_row, below + 8, LANES), f32),
        [
            vmem((groups, LANES, LANES), bf16),
            vmem((groups, LANES, LANES), bf16),
            vmem((groups, slots, LANES), f32),
            vmem((groups, slots, LANES), f32),
            vmem((groups, LANES), f32),
            vmem((groups, LANES), f32),
            vmem((2, count, LANES), f32),
        ],
        16,
    )
    back = exchanged(solved, row)
    chosen, energy = call(
        return_kernel, None, [code, back], (sds((width, rows), f32), sds((1, count), f32)), [], 16
    )
    return chosen.T, energy


def solution(mesh):
    placed = (P(("blk", "pix"), None), P("blk", None, None), P(("blk", "pix"), None))
    return jax.shard_map(
        per_device,
        mesh=mesh,
        in_specs=placed,
        out_specs=(P(("blk", "pix"), None), P("blk", None)),
        check_vma=False,
    )
```

time: 76.7 us -> 77.3 us (level)
  blocking collectives: 16.6 us -> 64.3 us
  waiting for transfers between devices: 22.1 us -> 0.01 us
  starting transfers between devices: 16.5 us -> 0.66 us
  local copies, waits for them, and re-layouts: 7.33 us -> 1.9 us
  Pallas kernels: 12.5 us -> 9.31 us
    all_to_all x1 -> x3, blocking collectives: 16.6 us -> 64.3 us  [exchanged(): lax.all_to_all(array, ALL, 0, 0, tiled=True, axis_index_groups=groups)]
    all_to_all x1 -> x0, waiting for transfers between devices: 17.2 us -> none  [copies_from(): lax.all_to_all(array, ALL, 0, 0, tiled=True, axis_index_groups=groups)]
    ppermute x5 -> x1, starting transfers between devices: 9.66 us -> 0.66 us  [per_device(): basis = lax.ppermute(basis, ALL, swap)]
    all_to_all x1 -> x0, starting transfers between devices: 6.89 us -> none  [copies_from(): lax.all_to_all(array, ALL, 0, 0, tiled=True, axis_index_groups=groups)]
    ppermute x5 -> x1, waiting for transfers between devices: 4.94 us -> 0.01 us  [per_device(): basis = lax.ppermute(basis, ALL, swap)]
    unnamed x15 -> x6, local copies, waits for them, and re-layouts: 5.73 us -> 1.86 us
    pallas_call x4, Pallas kernels: 12.5 us -> 9.31 us  [call(): pl.pallas_call(kernel, out_shape=outs, in_specs=[pl.BlockSpec(memory_spac...]
    broadcast_in_dim x1, local copies, waits for them, and re-layouts: 1.6 us -> 0.04 us  [per_device(): jnp.broadcast_to(basis[None], (n_col, width, LANES))]
  transfers between devices with their start and end apart: 6 -> 1, of which waited for: 4 -> 0; matrix products, arithmetic and copies ran while one was open for 1% -> 0% of each run, Pallas kernels for 3% -> 3%
where the time goes in v2:
time: 77.3 us; the launch traced here: 77 us
  blocking collectives  64.3 us (83%)
  Pallas kernels  9.31 us (12%)
  local copies, waits for them, and re-layouts  1.9 us (2%)
    all_to_all x3, blocking collectives, exchanged(): lax.all_to_all(array, ALL, 0, 0, tiled=True, axis_index_groups=groups)  64.3 us
    pallas_call x4, Pallas kernels, call(): pl.pallas_call(kernel, out_shape=outs, in_specs=[pl.BlockSpec(memory_spac...  9.31 us
    unnamed x6, local copies, waits for them, and re-layouts  1.86 us
  transfers between devices with their start and end apart: 1, of which 0 were waited for; matrix products, arithmetic and copies ran while one was open for 0% of the time, Pallas kernels for 3%

profile of v2, /device:TPU:1, one launch (start us, length us, event | category | flops | bytes accessed | tf_op | source)
XLA Modules:
  0.0 77.0 jit_solution(3253692099845403995)
XLA Ops:
  0.6 0.1 pad_add_fusion.place.refs_0_
  0.7 0.0 copy-start.1
  0.7 0.8 %copy-done.1 = bf16[2,224,64]{1,2,0:T(8,128)(2,1)S(1)} copy-done((bf16[2,224,64]{1,2,0:T(8,128)(2,1)S(1)}, bf16[2,224,64]{1,2,0:T(8,128)(2,1)}, u32[]{:S(2)}) %copy-start.1) | copy-done | bytes 57368
  1.6 0.0 copy-start.2
  1.6 0.6 shard_map.51
  2.1 0.7 collective-permute-start
  2.8 0.0 copy-done.2
  2.8 0.0 copy-start
  2.8 1.0 %copy-done = bf16[1024,224]{0,1:T(8,128)(2,1)S(1)} copy-done((bf16[1024,224]{0,1:T(8,128)(2,1)S(1)}, bf16[1024,224]{0,1:T(8,128)(2,1)}, u32[]{:S(2)}) %copy-start) | copy-done | bytes 458776
  3.8 2.2 %shard_map.50 = (bf16[8,256,256]{2,1,0:T(8,128)(2,1)S(1)}, s32[1,1024]{1,0:T(1,128)S(1)}) custom-call(s32[4]{0:T(128)S(1)} %pad_add_fusion.place.refs_0_, s32[1,1024]{1,0:T(1,128)S(1)} %bitcast.10, bf16[224,1024]{1,0:T(8,128)(2,1)S(1)} %bitcast.8), custom_call_target="tpu_custom_call" | custom-call | tf_op jit(solution)/shard_map/pallas_call | solution.py:172
  6.0 0.0 collective-permute-done
  6.0 23.6 %all_to_all.15.refs_2_ = bf16[8,256,256]{2,1,0:T(8,128)(2,1)S(1)} all-to-all(bf16[8,256,256]{2,1,0:T(8,128)(2,1)S(1)} %get-tuple-element.11), channel_id=1, replica_groups={{0,1,2,3,4,5,6,7},{8,9,10,11,12,13,14,15},{16,17,18,19,20,21,22,23},{24..., dimensions={0} | all-to-all | bytes 2097152 | tf_op jit(solution)/shard_map/all_to_all | solution.py:194
  29.6 24.7 %all_to_all.16.refs_1_ = bf16[16,64,256]{2,1,0:T(8,128)(2,1)S(1)} all-to-all(bf16[16,64,256]{2,1,0:T(8,128)(2,1)S(1)} %broadcast_in_dim.2), channel_id=1, replica_groups={{0,8,16,24,64,72,80,88,128,136,144,152,192,200,208,216},{1,9,17,25,65,7..., dimensions={0} | all-to-all | bytes 1048576 | tf_op jit(solution)/shard_map/all_to_all | solution.py:194
  54.3 4.8 %shard_map.52 = f32[8,72,256]{2,1,0:T(8,128)S(1)} custom-call(s32[4]{0:T(128)S(1)} %pad_add_fusion.place.refs_0_, bf16[16,64,256]{2,1,0:T(8,128)(2,1)S(1)} %all_to_all.16.refs_1_, bf16[8,256,256]{2,1,0:T(8,128)(2,1)S(1)} %all_to_all.15.refs_2_), custom_call_target="tpu_custom_call" | custom-call | tf_op jit(solution)/shard_map/pallas_call | solution.py:172
  59.2 16.1 %all_to_all.17.back = f32[8,72,256]{2,1,0:T(8,128)S(1)} all-to-all(f32[8,72,256]{2,1,0:T(8,128)S(1)} %shard_map.52), channel_id=1, replica_groups={{0,1,2,3,4,5,6,7},{8,9,10,11,12,13,14,15},{16,17,18,19,20,21,22,23},{24..., dimensions={0} | all-to-all | bytes 1179648 | tf_op jit(solution)/shard_map/all_to_all | solution.py:194
  75.2 1.7 %shard_map.53 = (f32[64,1024]{1,0:T(8,128)}, f32[1,128]{1,0:T(1,128)}) custom-call(s32[1,1024]{1,0:T(1,128)S(1)} %get-tuple-element.8.code, f32[8,72,256]{2,1,0:T(8,128)S(1)} %all_to_all.17.back), custom_call_target="tpu_custom_call" | custom-call | tf_op jit(solution)/shard_map/pallas_call | solution.py:172
  (1 shorter events, 0.0 us)
Async XLA Ops:
  0.7 0.8 %copy-start.1 = (bf16[2,224,64]{1,2,0:T(8,128)(2,1)S(1)}, bf16[2,224,64]{1,2,0:T(8,128)(2,1)}, u32[]{:S(2)}) copy-start(bf16[2,224,64]{1,2,0:T(8,128)(2,1)} %param.4) | copy-start | bytes 172036
  1.6 1.2 %copy-start.2 = (s32[1024,1]{0,1:T(1,128)S(1)}, s32[1024,1]{0,1:T(1,128)}, u32[]{:S(2)}) copy-start(s32[1024,1]{0,1:T(1,128)} %param.5) | copy-start | bytes 12292
  2.1 3.9 %collective-permute-start = (bf16[64,256]{1,0:T(8,128)(2,1)S(1)}, bf16[64,256]{1,0:T(8,128)(2,1)S(1)}, u32[]{:S(2)}, u32[]{:S(2)}) collective-permute-start(bf16[64,256]{1,0:T(8,128)(2,1)S(1)} %shard_map.51), channel_id=1, source_target_pairs={{0,0},{1,1},{2,34},{3,35},{4,4},{5,5},{6,38},{7,39},{8,8},{9,9},{1... | collective-permute-start | bytes 98312 | tf_op jit(solution)/shard_map/ppermute | solution.py:215
  2.8 1.0 %copy-start = (bf16[1024,224]{0,1:T(8,128)(2,1)S(1)}, bf16[1024,224]{0,1:T(8,128)(2,1)}, u32[]{:S(2)}) copy-start(bf16[1024,224]{0,1:T(8,128)(2,1)} %param.3) | copy-start | bytes 1376260

commit v3 on v2

--- a/solution.py
+++ b/solution.py
@@ -41,7 +41,7 @@
     out[:, :bands] = bundles[place[0]]
 
 
-def slots_kernel(place, labels, pixels, send, code, wide, ranks):
+def slots_kernel(place, labels, pixels, near, away, code, wide, ranks):
     bands, rows = pixels.shape
     count = rows // (CAP // 2)
     wide[:bands] = pixels[...]
@@ -57,30 +57,33 @@
         ranks[:, part] = jnp.sum(named * running, axis=0, keepdims=True) - 1.0
         carry = running[:, chunk - 1 :]
     rank = ranks[...].astype(jnp.int32)
-    handler = (label >> 1 & 1) * 4 + ((label >> 4) + place[2] & 1) * 2 + (label & 1)
+    chip = ((label >> 4) + place[2] & 1) * 2 + (label >> 1 & 1)
+    handler = (label + place[0] & 1) * 4 + (chip - place[3] & 3)
     local = (label >> 5) * PACK + (label >> 2 & 3)
     slot = local * CAP + rank
-    for d in range(send.shape[0]):
+    chips, held = near.shape[:2]
+    for d in range(2 * chips):
+        out = near if d < chips else away
         key = jnp.where(handler == d, slot, -1)
-        held = send.shape[1]
-        send[d] = dot_nt(one_hot(iota((held, rows), 0) == key), wide[...]).astype(bf16)
+        out[d % chips] = dot_nt(one_hot(iota((held, rows), 0) == key), wide[...]).astype(bf16)
     table_row = handler * (held // PACK) + (local >> 2) * CAP + rank
     code[...] = (local & 3) * 1024 + table_row
 
 
-def solve_kernel(place, bundles, pixels, out, high, low, goal, state, steps, sums, parts, scale):
+def solve_kernel(place, bundles, near, away, moved1, moved2, moved3, *rest, scale):
+    outs, (high, low, goal, state, steps, sums, parts) = rest[:4], rest[4:]
     groups = state.shape[0]
-    sources = pixels.shape[0]
-    slots = sources * CAP
+    sources = [near.at[0], away.at[0]] + [m.at[i] for m in (moved1, moved2, moved3) for i in range(2)]
+    slots = len(sources) * CAP
     wide = LANES // PACK
     block = iota((1, LANES), 1) // wide
     same = iota((LANES, LANES), 0) // wide == iota((LANES, LANES), 1) // wide
 
     def basis_of(g):
-        return jnp.concatenate([bundles[PACK * g + i] for i in range(PACK)], axis=0)
+        return jnp.concatenate([bundles[i, g] for i in range(PACK)], axis=0)
 
     def pixels_of(local):
-        return jnp.concatenate([pixels[s, local * CAP : (local + 1) * CAP] for s in range(sources)], axis=0)
+        return jnp.concatenate([s[local * CAP : (local + 1) * CAP] for s in sources], axis=0)
 
     for g in range(groups):
         basis = basis_of(g)
@@ -115,18 +118,19 @@
     odd = place[2] + place[1] & 1
     for g in range(groups):
         a = state[g]
-        for s in range(sources):
-            out[s, g * CAP : (g + 1) * CAP] = a[s * CAP : (s + 1) * CAP]
+        for s in range(len(sources)):
+            outs[s // 2][s % 2, g * CAP : (g + 1) * CAP] = a[s * CAP : (s + 1) * CAP]
         spread = jnp.concatenate([jnp.where(block == i, a, 0.0) for i in range(PACK)], axis=0)
         both = dot(jnp.concatenate(split(spread), axis=0), basis_of(g))
         fitted = both[: PACK * slots] + both[PACK * slots :]
         for i in range(PACK):
             misfit = pixels_of(PACK * g + i).astype(f32) - fitted[i * slots : (i + 1) * slots]
             square = misfit * misfit
-            bundle = 16 * (2 * g + odd) + 4 * i + 2 * place[3] + place[0]
+            bundle = 16 * (2 * g + odd) + 4 * i + 2 * (place[3] & 1) + place[0]
             for half in range(2):
-                rows = slice(half * slots // 2, (half + 1) * slots // 2)
-                parts[half, pl.ds(bundle, 1), :] = jnp.sum(square[rows], axis=0, keepdims=True)
+                both = square[2 * half * CAP : 2 * (half + 1) * CAP]
+                both = both + square[2 * (half + 2) * CAP : 2 * (half + 3) * CAP]
+                parts[half, pl.ds(bundle, 1), :] = jnp.sum(both, axis=0, keepdims=True)
     bands = LANES - 32
     below = groups * CAP
     for half in range(2):
@@ -134,18 +138,21 @@
         lines = jnp.where(iota(lines.shape, 0) < bands, lines, 0.0)
         energy = jnp.sum(lines, axis=0, keepdims=True) / scale
         energy = jnp.concatenate([energy, jnp.zeros_like(energy)], axis=1)
-        for s in range(half * sources // 2, (half + 1) * sources // 2):
-            out[s, below:] = jnp.broadcast_to(energy, (8, LANES))
-
-
-def return_kernel(code, back, chosen, energy):
+        for r in (half, half + 2):
+            for i in range(2):
+                outs[r][i, below:] = jnp.broadcast_to(energy, (8, LANES))
+
+
+def return_kernel(code, back0, back1, back2, back3, others, chosen, energy):
     rows = code.shape[1]
-    handlers, held, lanes = back.shape
-    held -= 8
+    lanes = others.shape[2]
+    held = others.shape[1] - 8
+    tables = [b.at[0] for b in (back0, back1, back2, back3)] + [others.at[r] for r in range(others.shape[0])]
+    handlers = len(tables)
     wide = lanes // PACK
     codes = code[...]
     pick = one_hot(iota((handlers * held, rows), 0) == codes & 1023)
-    table = jnp.concatenate([back[d, :held] for d in range(handlers)], axis=0).T
+    table = jnp.concatenate([t[:held] for t in tables], axis=0).T
     first = table.astype(bf16)
     rest = table - first.astype(f32)
     second, third = split(rest)
@@ -156,9 +163,9 @@
     for i in range(1, PACK):
         result = jnp.where(which == i, found[i * wide : (i + 1) * wide], result)
     chosen[...] = result
-    total = back[0, held : held + 1]
-    for d in range(1, handlers):
-        total = total + back[d, held : held + 1]
+    total = tables[0][held : held + 1]
+    for t in tables[1:]:
+        total = total + t[held : held + 1]
     energy[...] = total[:, : energy.shape[1]]
 
 
@@ -199,40 +206,53 @@
     owned, _, width = bundles.shape
     n_blk, n_pix = lax.axis_size("blk"), lax.axis_size("pix")
     spots = spots_of(n_blk, n_pix)
-    column = grouped(spots, lambda z, y, xl, xh, c: (z % 2, xl, xh, c))
-    row = grouped(spots, lambda z, y, xl, xh, c: (z, y))
+    along_z = grouped(spots, lambda z, y, xl, xh, c: (y, xl, xh, c))
+    along_y = grouped(spots, lambda z, y, xl, xh, c: (z, xl, xh, c))
     there = {spot: index for index, spot in enumerate(spots)}
-    swap = [(there[s], there[(s[0] ^ s[3],) + s[1:]]) for s in spots]
+
+    def shifted(array, r):
+        pairs = []
+        for z, y, xl, xh, c in spots:
+            x = (2 * xh + xl + r) % 4
+            pairs.append((there[z, y, xl, xh, c], there[z, y, x % 2, x // 2, c]))
+        return lax.ppermute(array, ALL, pairs)
+
+    def to_sibling(array):
+        return lax.ppermute(array, ALL, [(i, i ^ 1) for i in range(len(spots))])
+
     blk, pix = lax.axis_index("blk"), lax.axis_index("pix")
-    place = jnp.stack([pix & 1, pix >> 1, blk >> 3 & 1, blk & 1]).astype(jnp.int32)
+    z, x_hi = blk >> 3, pix >> 1
+    place = jnp.stack([pix & 1, x_hi, z & 1, 2 * x_hi + (blk & 1)]).astype(jnp.int32)
     sds = jax.ShapeDtypeStruct
-    n_col, n_row = len(column[0]), len(row[0])
+    n_z, n_y = len(along_z[0]), len(along_y[0])
+    chips = 4
     count = n_blk * owned
-    held = n_col * CAP
-    groups = n_col // PACK
+    groups = n_z // 2
+    held = groups * n_y * CAP
 
     basis = call(prep_kernel, place, [bundles.transpose(0, 2, 1)], sds((width, LANES), bf16), [], 4)
-    basis = lax.ppermute(basis, ALL, swap)
-    send, code = call(
+    levels = exchanged(jnp.broadcast_to(basis[None], (n_z, width, LANES)), along_z)
+    near, away, code = call(
         slots_kernel,
         place,
         [assign.reshape(1, rows), pixels.T],
-        (sds((n_row, held, LANES), bf16), sds((1, rows), jnp.int32)),
+        (sds((chips, held, LANES), bf16), sds((chips, held, LANES), bf16), sds((1, rows), jnp.int32)),
         [vmem((LANES, rows), bf16), vmem((1, rows), f32)],
         16,
     )
-    basis, send = lax.optimization_barrier((basis, send))
-    gathered = exchanged(jnp.broadcast_to(basis[None], (n_col, width, LANES)), column)
-    received = exchanged(send, row)
+    theirs = to_sibling(away)
+    moved = [shifted(jnp.stack([near[r], theirs[r]]), r) for r in range(1, chips)]
+    half = lax.dynamic_index_in_dim(levels.reshape(groups, 2, width, LANES), (z + x_hi) & 1, 1, keepdims=False)
+    plane = exchanged(jnp.broadcast_to(half[None], (n_y, groups, width, LANES)), along_y)
 
     below = groups * CAP
-    slots = n_row * CAP
+    slots = 2 * chips * CAP
     scale = bands * rows * n_pix / count
     solved = call(
         lambda *refs: solve_kernel(*refs, scale=scale),
         place,
-        [gathered, received],
-        sds((n_row, below + 8, LANES), f32),
+        [plane, near, theirs, *moved],
+        (sds((2, below + 8, LANES), f32),) * chips,
         [
             vmem((groups, LANES, LANES), bf16),
             vmem((groups, LANES, LANES), bf16),
@@ -244,10 +264,10 @@
         ],
         16,
     )
-    back = exchanged(solved, row)
-    chosen, energy = call(
-        return_kernel, None, [code, back], (sds((width, rows), f32), sds((1, count), f32)), [], 16
-    )
+    back = [solved[0]] + [shifted(solved[r], -r) for r in range(1, chips)]
+    others = to_sibling(jnp.stack([b[1] for b in back]))
+    outs = (sds((width, rows), f32), sds((1, count), f32))
+    chosen, energy = call(return_kernel, None, [code, *back, others], outs, [], 16)
     return chosen.T, energy
 
 

time: 77.3 us -> 64.1 us (0.83)
  blocking collectives: 64.3 us -> 0 us
  starting transfers between devices: 0.66 us -> 28.5 us
  waiting for transfers between devices: 0.01 us -> 20.3 us
  local copies, waits for them, and re-layouts: 1.9 us -> 4.71 us
    all_to_all x3 -> x0, blocking collectives: 64.3 us -> none  [exchanged(): lax.all_to_all(array, ALL, 0, 0, tiled=True, axis_index_groups=groups)]
    ppermute x1 -> x8, starting transfers between devices: 0.66 us -> 15.1 us  [the longest x6 10.5 us: shifted(): return lax.ppermute(array, ALL, pairs)]
    all_to_all x0 -> x2, starting transfers between devices: none -> 13.3 us  [exchanged(): lax.all_to_all(array, ALL, 0, 0, tiled=True, axis_index_groups=groups)]
    ppermute x1 -> x8, waiting for transfers between devices: 0.01 us -> 13.2 us  [the longest x6 12 us: shifted(): return lax.ppermute(array, ALL, pairs)]
    all_to_all x0 -> x2, waiting for transfers between devices: none -> 7.09 us  [exchanged(): lax.all_to_all(array, ALL, 0, 0, tiled=True, axis_index_groups=groups)]
    broadcast_in_dim x1 -> x3, local copies, waits for them, and re-layouts: 0.04 us -> 1.59 us  [the longest x2 0.87 us: per_device(): jnp.broadcast_to(half[None], (n_y, groups, width, LANES))]
    slice x0 -> x8, local copies, waits for them, and re-layouts: none -> 0.93 us  [the longest x6 0.88 us: per_device(): others = to_sibling(jnp.stack([b[1] for b in back]))]
    unnamed x6 -> x14, local copies, waits for them, and re-layouts: 1.86 us -> 2.18 us
  transfers between devices with their start and end apart: 1 -> 10, of which waited for: 0 -> 8; matrix products, arithmetic and copies ran while one was open for 0% -> 2% of each run, Pallas kernels for 3% -> 3%
where the time goes in v3:
time: 64.1 us; the launch traced here: 63.7 us
  starting transfers between devices  28.5 us (44%)
  waiting for transfers between devices  20.3 us (32%)
  Pallas kernels  9.3 us (15%)
  local copies, waits for them, and re-layouts  4.71 us (7%)
  between operations  0.73 us (1%)
    all_to_all x2, starting transfers between devices, exchanged(): lax.all_to_all(array, ALL, 0, 0, tiled=True, axis_index_groups=groups)  13.3 us
    ppermute x6, waiting for transfers between devices, shifted(): return lax.ppermute(array, ALL, pairs)  12 us
    ppermute x6, starting transfers between devices, shifted(): return lax.ppermute(array, ALL, pairs)  10.5 us
    pallas_call x4, Pallas kernels, call(): pl.pallas_call(kernel, out_shape=outs, in_specs=[pl.BlockSpec(memory_spac...  9.3 us
    all_to_all x2, waiting for transfers between devices, exchanged(): lax.all_to_all(array, ALL, 0, 0, tiled=True, axis_index_groups=groups)  7.09 us
    ppermute x2, starting transfers between devices, to_sibling(): return lax.ppermute(array, ALL, [(i, i ^ 1) for i in range(len(spots))])  4.62 us
    unnamed x14, local copies, waits for them, and re-layouts  2.18 us
  transfers between devices with their start and end apart: 10, of which 8 were waited for; matrix products, arithmetic and copies ran while one was open for 2% of the time, Pallas kernels for 3%

profile of v3, /device:TPU:1, one launch (start us, length us, event | category | flops | bytes accessed | tf_op | source)
XLA Modules:
  0.0 63.7 jit_solution(17332966963934837746)
XLA Ops:
  0.7 0.8 %copy-done.5 = bf16[2,224,64]{1,2,0:T(8,128)(2,1)S(1)} copy-done((bf16[2,224,64]{1,2,0:T(8,128)(2,1)S(1)}, bf16[2,224,64]{1,2,0:T(8,128)(2,1)}, u32[]{:S(2)}) %copy-start.5) | copy-done | bytes 57368
  2.1 0.7 %broadcast_in_dim.6 = bf16[8,64,256]{2,1,0:T(8,128)(2,1)} broadcast(bf16[64,256]{1,0:T(8,128)(2,1)S(1)} %shard_map.51), dimensions={1,2} | broadcast | bytes 294912 | tf_op jit(solution)/shard_map/broadcast_in_dim | solution.py:234
  2.8 9.1 %all-to-all-start = ((bf16[8,64,256]{2,1,0:T(8,128)(2,1)}), bf16[8,64,256]{2,1,0:T(8,128)(2,1)S(1)}, u32[]{:S(2)}, u32[]{:S(2)}) async-start(bf16[8,64,256]{2,1,0:T(8,128)(2,1)} %broadcast_in_dim.6), calls=%async_computation | async-start | bytes 524288 | tf_op jit(solution)/shard_map/all_to_all | solution.py:201
  12.0 2.2 %shard_map.50 = (bf16[4,256,256]{2,1,0:T(8,128)(2,1)S(1)}, bf16[4,256,256]{2,1,0:T(8,128)(2,1)S(1)}, s32[1,1024]{1,0:T(1,128)S(1)}) custom-call(s32[4]{0:T(128)S(1)} %pad_add_fusion.place.refs_0_, s32[1,1024]{1,0:T(1,128)S(1)} %bitcast.13, bf16[224,1024]{1,0:T(8,128)(2,1)S(1)} %bitcast.11), custom_call_target="tpu_custom_call" | custom-call | tf_op jit(solution)/shard_map/pallas_call | solution.py:179
  14.2 1.0 %collective-permute-start = (bf16[4,256,256]{2,1,0:T(8,128)(2,1)S(1)}, bf16[4,256,256]{2,1,0:T(8,128)(2,1)S(1)}, u32[]{:S(2)}, u32[]{:S(2)}) collective-permute-start(bf16[4,256,256]{2,1,0:T(8,128)(2,1)S(1)} %get-tuple-element.13), channel_id=1, source_target_pairs={{0,1},{1,0},{2,3},{3,2},{4,5},{5,4},{6,7},{7,6},{8,9},{9,8},{10,11... | collective-permute-start | bytes 1572872 | tf_op jit(solution)/shard_map/ppermute | solution.py:221
  15.3 7.1 %all-to-all-done = bf16[8,64,256]{2,1,0:T(8,128)(2,1)S(1)} async-done(((bf16[8,64,256]{2,1,0:T(8,128)(2,1)}), bf16[8,64,256]{2,1,0:T(8,128)(2,1)S(1)}, u32[]{:S(2)}, u32[]{:S(2)}) %all-to-all-start) | async-done | bytes 262176 | tf_op jit(solution)/shard_map/all_to_all | solution.py:201
  22.4 0.9 %broadcast_in_dim.16 = bf16[4,4,64,256]{3,2,1,0:T(8,128)(2,1)} broadcast(bf16[4,64,256]{2,1,0:T(8,128)(2,1)S(1)} %dynamic-slice_bitcast_fusion), dimensions={1,2,3} | broadcast | bytes 655360 | tf_op jit(solution)/shard_map/broadcast_in_dim | solution.py:246
  23.2 4.2 %all-to-all-start.1 = ((bf16[4,4,64,256]{3,2,1,0:T(8,128)(2,1)}), bf16[4,4,64,256]{3,2,1,0:T(8,128)(2,1)S(1)}, u32[]{:S(2)}, u32[]{:S(2)}) async-start(bf16[4,4,64,256]{3,2,1,0:T(8,128)(2,1)} %broadcast_in_dim.16), calls=%async_computation.1 | async-start | bytes 1048576 | tf_op jit(solution)/shard_map/all_to_all | solution.py:201
  27.5 1.3 %collective-permute-start.1 = (bf16[2,256,256]{2,1,0:T(8,128)(2,1)S(1)}, bf16[2,256,256]{2,1,0:T(8,128)(2,1)S(1)}, u32[]{:S(2)}, u32[]{:S(2)}) collective-permute-start(bf16[2,256,256]{2,1,0:T(8,128)(2,1)S(1)} %pad_maximum_fusion.1), channel_id=1, source_target_pairs={{0,4},{1,5},{2,6},{3,7},{4,2},{5,3},{6,0},{7,1},{8,12},{9,13},{10,... | collective-permute-start | bytes 786440 | tf_op jit(solution)/shard_map/ppermute | solution.py:218
  28.8 2.5 %collective-permute-start.2 = (bf16[2,256,256]{2,1,0:T(8,128)(2,1)S(1)}, bf16[2,256,256]{2,1,0:T(8,128)(2,1)S(1)}, u32[]{:S(2)}, u32[]{:S(2)}) collective-permute-start(bf16[2,256,256]{2,1,0:T(8,128)(2,1)S(1)} %pad_maximum_fusion.2), channel_id=1, source_target_pairs={{0,2},{1,3},{2,0},{3,1},{4,6},{5,7},{6,4},{7,5},{8,10},{9,11},{10,... | collective-permute-start | bytes 786440 | tf_op jit(solution)/shard_map/ppermute | solution.py:218
  31.4 1.2 %collective-permute-start.3 = (bf16[2,256,256]{2,1,0:T(8,128)(2,1)S(1)}, bf16[2,256,256]{2,1,0:T(8,128)(2,1)S(1)}, u32[]{:S(2)}, u32[]{:S(2)}) collective-permute-start(bf16[2,256,256]{2,1,0:T(8,128)(2,1)S(1)} %pad_maximum_fusion.3), channel_id=1, source_target_pairs={{0,6},{1,7},{2,4},{3,5},{4,0},{5,1},{6,2},{7,3},{8,14},{9,15},{10,... | collective-permute-start | bytes 786440 | tf_op jit(solution)/shard_map/ppermute | solution.py:218
  32.6 1.4 %collective-permute-done.1.refs_4_ = bf16[2,256,256]{2,1,0:T(8,128)(2,1)S(1)} collective-permute-done((bf16[2,256,256]{2,1,0:T(8,128)(2,1)S(1)}, bf16[2,256,256]{2,1,0:T(8,128)(2,1)S(1)}, u32[]{:S(2)}, u32[]{:S(2)}) %collective-permute-start.1) | collective-permute-done | bytes 262176 | tf_op jit(solution)/shard_map/ppermute | solution.py:218
  34.0 6.1 %collective-permute-done.2.refs_5_ = bf16[2,256,256]{2,1,0:T(8,128)(2,1)S(1)} collective-permute-done((bf16[2,256,256]{2,1,0:T(8,128)(2,1)S(1)}, bf16[2,256,256]{2,1,0:T(8,128)(2,1)S(1)}, u32[]{:S(2)}, u32[]{:S(2)}) %collective-permute-start.2) | collective-permute-done | bytes 262176 | tf_op jit(solution)/shard_map/ppermute | solution.py:218
  40.4 4.8 %shard_map.52 = (f32[2,72,256]{2,1,0:T(8,128)S(1)}, f32[2,72,256]{2,1,0:T(8,128)S(1)}, f32[2,72,256]{2,1,0:T(8,128)S(1)}, f32[2,72,256]{2,1,0:T(8,128)S(1)}) custom-call(s32[4]{0:T(128)S(1)} %pad_add_fusion.place.refs_0_, bf16[4,4,64,256]{3,2,1,0:T(8,128)(2,1)S(1)} %all-to-all-done.1.refs_1_, bf16[4,256,256]{2,1,0:T(8,128)(2,1)S(1)} %get-tuple-element.12.refs_2_, ...), custom_call_target="tpu_custom_call" | custom-call | tf_op jit(solution)/shard_map/pallas_call | solution.py:179
  45.2 3.6 %collective-permute-start.4 = (f32[2,72,256]{2,1,0:T(8,128)S(1)}, f32[2,72,256]{2,1,0:T(8,128)S(1)}, u32[]{:S(2)}, u32[]{:S(2)}) collective-permute-start(f32[2,72,256]{2,1,0:T(8,128)S(1)} %get-tuple-element.15), channel_id=1, source_target_pairs={{0,6},{1,7},{2,4},{3,5},{4,0},{5,1},{6,2},{7,3},{8,14},{9,15},{10,... | collective-permute-start | bytes 442376 | tf_op jit(solution)/shard_map/ppermute | solution.py:218
  48.8 1.8 %collective-permute-start.5 = (f32[2,72,256]{2,1,0:T(8,128)S(1)}, f32[2,72,256]{2,1,0:T(8,128)S(1)}, u32[]{:S(2)}, u32[]{:S(2)}) collective-permute-start(f32[2,72,256]{2,1,0:T(8,128)S(1)} %get-tuple-element.16), channel_id=1, source_target_pairs={{0,2},{1,3},{2,0},{3,1},{4,6},{5,7},{6,4},{7,5},{8,10},{9,11},{10,... | collective-permute-start | bytes 442376 | tf_op jit(solution)/shard_map/ppermute | solution.py:218
  50.7 0.7 %collective-permute-done.4.back1 = f32[2,72,256]{2,1,0:T(8,128)S(1)} collective-permute-done((f32[2,72,256]{2,1,0:T(8,128)S(1)}, f32[2,72,256]{2,1,0:T(8,128)S(1)}, u32[]{:S(2)}, u32[]{:S(2)}) %collective-permute-start.4) | collective-permute-done | bytes 147488 | tf_op jit(solution)/shard_map/ppermute | solution.py:218
  52.1 2.3 %collective-permute-done.5.back2 = f32[2,72,256]{2,1,0:T(8,128)S(1)} collective-permute-done((f32[2,72,256]{2,1,0:T(8,128)S(1)}, f32[2,72,256]{2,1,0:T(8,128)S(1)}, u32[]{:S(2)}, u32[]{:S(2)}) %collective-permute-start.5) | collective-permute-done | bytes 147488 | tf_op jit(solution)/shard_map/ppermute | solution.py:218
  54.3 0.7 %copy-done.3 = f32[2,72,256]{2,1,0:T(8,128)} copy-done((f32[2,72,256]{2,1,0:T(8,128)}, f32[2,72,256]{2,1,0:T(8,128)S(1)}, u32[]{:S(2)}) %copy-start.3) | copy-done | bytes 147480
  55.0 1.3 %collective-permute-done.6.back3 = f32[2,72,256]{2,1,0:T(8,128)S(1)} collective-permute-done((f32[2,72,256]{2,1,0:T(8,128)S(1)}, f32[2,72,256]{2,1,0:T(8,128)S(1)}, u32[]{:S(2)}, u32[]{:S(2)}) %collective-permute-start.6) | collective-permute-done | bytes 147488 | tf_op jit(solution)/shard_map/ppermute | solution.py:218
  56.3 0.9 %slice-done.1 = f32[1,72,256]{2,1,0:T(8,128)S(1)} async-done(((f32[2,72,256]{2,1,0:T(8,128)}), f32[1,72,256]{2,1,0:T(8,128)S(1)}, s32[]{:S(2)}) %slice-start.1) | async-done | bytes 73752 | tf_op jit(solution)/shard_map/slice | solution.py:268
  57.2 3.6 %collective-permute-start.7 = (f32[4,72,256]{2,1,0:T(8,128)S(1)}, f32[4,72,256]{2,1,0:T(8,128)S(1)}, u32[]{:S(2)}, u32[]{:S(2)}) collective-permute-start(f32[4,72,256]{2,1,0:T(8,128)S(1)} %pad_maximum_fusion), channel_id=1, source_target_pairs={{0,1},{1,0},{2,3},{3,2},{4,5},{5,4},{6,7},{7,6},{8,9},{9,8},{10,11... | collective-permute-start | bytes 884744 | tf_op jit(solution)/shard_map/ppermute | solution.py:221
  60.8 1.2 %collective-permute-done.7.others = f32[4,72,256]{2,1,0:T(8,128)S(1)} collective-permute-done((f32[4,72,256]{2,1,0:T(8,128)S(1)}, f32[4,72,256]{2,1,0:T(8,128)S(1)}, u32[]{:S(2)}, u32[]{:S(2)}) %collective-permute-start.7) | collective-permute-done | bytes 294944 | tf_op jit(solution)/shard_map/ppermute | solution.py:221
  62.0 1.7 %shard_map.53 = (f32[64,1024]{1,0:T(8,128)}, f32[1,128]{1,0:T(1,128)}) custom-call(s32[1,1024]{1,0:T(1,128)S(1)} %get-tuple-element.11.code, f32[2,72,256]{2,1,0:T(8,128)S(1)} %get-tuple-element.14.back0, f32[2,72,256]{2,1,0:T(8,128)S(1)} %copy-done.2, f32[2,72,256]{2,1,0:T(8,128)S(1)} %copy-done.4, f32[2,72,256]{2,1,0:T(8,128)S(1)} %collective-permute-done.6.back3, ...), custom_call_target="tpu_custom_call" | custom-call | tf_op jit(solution)/shard_map/pallas_call | solution.py:179
  (30 shorter events, 1.7 us)
Async XLA Ops:
  0.7 0.8 %copy-start.5 = (bf16[2,224,64]{1,2,0:T(8,128)(2,1)S(1)}, bf16[2,224,64]{1,2,0:T(8,128)(2,1)}, u32[]{:S(2)}) copy-start(bf16[2,224,64]{1,2,0:T(8,128)(2,1)} %param.4) | copy-start | bytes 172036
  1.6 10.4 %copy-start = (bf16[1024,224]{0,1:T(8,128)(2,1)S(1)}, bf16[1024,224]{0,1:T(8,128)(2,1)}, u32[]{:S(2)}) copy-start(bf16[1024,224]{0,1:T(8,128)(2,1)} %param.3) | copy-start | bytes 1376260
  2.8 9.2 %copy-start.6 = (s32[1024,1]{0,1:T(1,128)S(1)}, s32[1024,1]{0,1:T(1,128)}, u32[]{:S(2)}) copy-start(s32[1024,1]{0,1:T(1,128)} %param.5) | copy-start | bytes 12292
  2.8 19.5 %all-to-all-start = ((bf16[8,64,256]{2,1,0:T(8,128)(2,1)}), bf16[8,64,256]{2,1,0:T(8,128)(2,1)S(1)}, u32[]{:S(2)}, u32[]{:S(2)}) async-start(bf16[8,64,256]{2,1,0:T(8,128)(2,1)} %broadcast_in_dim.6), calls=%async_computation | async-start | bytes 524288 | tf_op jit(solution)/shard_map/all_to_all | solution.py:201
  14.2 13.2 %collective-permute-start = (bf16[4,256,256]{2,1,0:T(8,128)(2,1)S(1)}, bf16[4,256,256]{2,1,0:T(8,128)(2,1)S(1)}, u32[]{:S(2)}, u32[]{:S(2)}) collective-permute-start(bf16[4,256,256]{2,1,0:T(8,128)(2,1)S(1)} %get-tuple-element.13), channel_id=1, source_target_pairs={{0,1},{1,0},{2,3},{3,2},{4,5},{5,4},{6,7},{7,6},{8,9},{9,8},{10,11... | collective-permute-start | bytes 1572872 | tf_op jit(solution)/shard_map/ppermute | solution.py:221
  23.2 17.1 %all-to-all-start.1 = ((bf16[4,4,64,256]{3,2,1,0:T(8,128)(2,1)}), bf16[4,4,64,256]{3,2,1,0:T(8,128)(2,1)S(1)}, u32[]{:S(2)}, u32[]{:S(2)}) async-start(bf16[4,4,64,256]{3,2,1,0:T(8,128)(2,1)} %broadcast_in_dim.16), calls=%async_computation.1 | async-start | bytes 1048576 | tf_op jit(solution)/shard_map/all_to_all | solution.py:201
  27.5 6.5 %collective-permute-start.1 = (bf16[2,256,256]{2,1,0:T(8,128)(2,1)S(1)}, bf16[2,256,256]{2,1,0:T(8,128)(2,1)S(1)}, u32[]{:S(2)}, u32[]{:S(2)}) collective-permute-start(bf16[2,256,256]{2,1,0:T(8,128)(2,1)S(1)} %pad_maximum_fusion.1), channel_id=1, source_target_pairs={{0,4},{1,5},{2,6},{3,7},{4,2},{5,3},{6,0},{7,1},{8,12},{9,13},{10,... | collective-permute-start | bytes 786440 | tf_op jit(solution)/shard_map/ppermute | solution.py:218
  28.8 11.3 %collective-permute-start.2 = (bf16[2,256,256]{2,1,0:T(8,128)(2,1)S(1)}, bf16[2,256,256]{2,1,0:T(8,128)(2,1)S(1)}, u32[]{:S(2)}, u32[]{:S(2)}) collective-permute-start(bf16[2,256,256]{2,1,0:T(8,128)(2,1)S(1)} %pad_maximum_fusion.2), channel_id=1, source_target_pairs={{0,2},{1,3},{2,0},{3,1},{4,6},{5,7},{6,4},{7,5},{8,10},{9,11},{10,... | collective-permute-start | bytes 786440 | tf_op jit(solution)/shard_map/ppermute | solution.py:218
  31.4 9.0 %collective-permute-start.3 = (bf16[2,256,256]{2,1,0:T(8,128)(2,1)S(1)}, bf16[2,256,256]{2,1,0:T(8,128)(2,1)S(1)}, u32[]{:S(2)}, u32[]{:S(2)}) collective-permute-start(bf16[2,256,256]{2,1,0:T(8,128)(2,1)S(1)} %pad_maximum_fusion.3), channel_id=1, source_target_pairs={{0,6},{1,7},{2,4},{3,5},{4,0},{5,1},{6,2},{7,3},{8,14},{9,15},{10,... | collective-permute-start | bytes 786440 | tf_op jit(solution)/shard_map/ppermute | solution.py:218
  45.2 6.2 %collective-permute-start.4 = (f32[2,72,256]{2,1,0:T(8,128)S(1)}, f32[2,72,256]{2,1,0:T(8,128)S(1)}, u32[]{:S(2)}, u32[]{:S(2)}) collective-permute-start(f32[2,72,256]{2,1,0:T(8,128)S(1)} %get-tuple-element.15), channel_id=1, source_target_pairs={{0,6},{1,7},{2,4},{3,5},{4,0},{5,1},{6,2},{7,3},{8,14},{9,15},{10,... | collective-permute-start | bytes 442376 | tf_op jit(solution)/shard_map/ppermute | solution.py:218
  48.8 5.5 %collective-permute-start.5 = (f32[2,72,256]{2,1,0:T(8,128)S(1)}, f32[2,72,256]{2,1,0:T(8,128)S(1)}, u32[]{:S(2)}, u32[]{:S(2)}) collective-permute-start(f32[2,72,256]{2,1,0:T(8,128)S(1)} %get-tuple-element.16), channel_id=1, source_target_pairs={{0,2},{1,3},{2,0},{3,1},{4,6},{5,7},{6,4},{7,5},{8,10},{9,11},{10,... | collective-permute-start | bytes 442376 | tf_op jit(solution)/shard_map/ppermute | solution.py:218
  50.7 5.6 %collective-permute-start.6 = (f32[2,72,256]{2,1,0:T(8,128)S(1)}, f32[2,72,256]{2,1,0:T(8,128)S(1)}, u32[]{:S(2)}, u32[]{:S(2)}) collective-permute-start(f32[2,72,256]{2,1,0:T(8,128)S(1)} %get-tuple-element.17), channel_id=1, source_target_pairs={{0,4},{1,5},{2,6},{3,7},{4,2},{5,3},{6,0},{7,1},{8,12},{9,13},{10,... | collective-permute-start | bytes 442376 | tf_op jit(solution)/shard_map/ppermute | solution.py:218
  51.4 0.7 %copy-start.1 = (f32[2,72,256]{2,1,0:T(8,128)}, f32[2,72,256]{2,1,0:T(8,128)S(1)}, u32[]{:S(2)}) copy-start(f32[2,72,256]{2,1,0:T(8,128)S(1)} %collective-permute-done.4.back1) | copy-start | bytes 442372
  54.3 0.7 %copy-start.3 = (f32[2,72,256]{2,1,0:T(8,128)}, f32[2,72,256]{2,1,0:T(8,128)S(1)}, u32[]{:S(2)}) copy-start(f32[2,72,256]{2,1,0:T(8,128)S(1)} %collective-permute-done.5.back2) | copy-start | bytes 442372
  55.0 1.3 %slice-start = ((f32[2,72,256]{2,1,0:T(8,128)}), f32[1,72,256]{2,1,0:T(8,128)S(1)}, s32[]{:S(2)}) async-start(f32[2,72,256]{2,1,0:T(8,128)} %copy-done.1), calls=%async_computation.2 | async-start | bytes 147456 | tf_op jit(solution)/shard_map/slice | solution.py:268
  56.3 0.9 %slice-start.1 = ((f32[2,72,256]{2,1,0:T(8,128)}), f32[1,72,256]{2,1,0:T(8,128)S(1)}, s32[]{:S(2)}) async-start(f32[2,72,256]{2,1,0:T(8,128)} %copy-done.3), calls=%async_computation.3 | async-start | bytes 147456 | tf_op jit(solution)/shard_map/slice | solution.py:268
  57.2 4.8 %copy-start.2 = (f32[2,72,256]{2,1,0:T(8,128)S(1)}, f32[2,72,256]{2,1,0:T(8,128)}, u32[]{:S(2)}) copy-start(f32[2,72,256]{2,1,0:T(8,128)} %copy-done.1) | copy-start | bytes 442372
  57.2 4.8 %copy-start.4 = (f32[2,72,256]{2,1,0:T(8,128)S(1)}, f32[2,72,256]{2,1,0:T(8,128)}, u32[]{:S(2)}) copy-start(f32[2,72,256]{2,1,0:T(8,128)} %copy-done.3) | copy-start | bytes 442372
  57.2 4.8 %collective-permute-start.7 = (f32[4,72,256]{2,1,0:T(8,128)S(1)}, f32[4,72,256]{2,1,0:T(8,128)S(1)}, u32[]{:S(2)}, u32[]{:S(2)}) collective-permute-start(f32[4,72,256]{2,1,0:T(8,128)S(1)} %pad_maximum_fusion), channel_id=1, source_target_pairs={{0,1},{1,0},{2,3},{3,2},{4,5},{5,4},{6,7},{7,6},{8,9},{9,8},{10,11... | collective-permute-start | bytes 884744 | tf_op jit(solution)/shard_map/ppermute | solution.py:221

commit v4 on v3

--- a/solution.py
+++ b/solution.py
@@ -41,7 +41,8 @@
     out[:, :bands] = bundles[place[0]]
 
 
-def slots_kernel(place, labels, pixels, near, away, code, wide, ranks):
+def slots_kernel(place, labels, pixels, *rest):
+    outs, (code, wide, ranks) = rest[:-3], rest[-3:]
     bands, rows = pixels.shape
     count = rows // (CAP // 2)
     wide[:bands] = pixels[...]
@@ -58,22 +59,30 @@
         carry = running[:, chunk - 1 :]
     rank = ranks[...].astype(jnp.int32)
     chip = ((label >> 4) + place[2] & 1) * 2 + (label >> 1 & 1)
-    handler = (label + place[0] & 1) * 4 + (chip - place[3] & 3)
+    handler = (chip - place[3] & 3) * 2 + (label + place[0] & 1)
     local = (label >> 5) * PACK + (label >> 2 & 3)
     slot = local * CAP + rank
-    chips, held = near.shape[:2]
-    for d in range(2 * chips):
-        out = near if d < chips else away
+    held = outs[0].shape[0]
+    for d in range(len(outs)):
         key = jnp.where(handler == d, slot, -1)
-        out[d % chips] = dot_nt(one_hot(iota((held, rows), 0) == key), wide[...]).astype(bf16)
+        outs[d][...] = dot_nt(one_hot(iota((held, rows), 0) == key), wide[...]).astype(bf16)
     table_row = handler * (held // PACK) + (local >> 2) * CAP + rank
     code[...] = (local & 3) * 1024 + table_row
 
 
-def solve_kernel(place, bundles, near, away, moved1, moved2, moved3, *rest, scale):
-    outs, (high, low, goal, state, steps, sums, parts) = rest[:4], rest[4:]
+def pick_kernel(place, levels, *rest):
+    out = rest[-1]
+    odd = place[2] + place[1] & 1
+    for g in range(out.shape[1]):
+        level = levels[2 * g + odd]
+        for y in range(out.shape[0]):
+            out[y, g] = level
+
+
+def solve_kernel(place, bundles, *rest, scale):
+    sources, outs = rest[:-9], rest[-9:-7]
+    high, low, goal, state, steps, sums, parts = rest[-7:]
     groups = state.shape[0]
-    sources = [near.at[0], away.at[0]] + [m.at[i] for m in (moved1, moved2, moved3) for i in range(2)]
     slots = len(sources) * CAP
     wide = LANES // PACK
     block = iota((1, LANES), 1) // wide
@@ -119,7 +128,7 @@
     for g in range(groups):
         a = state[g]
         for s in range(len(sources)):
-            outs[s // 2][s % 2, g * CAP : (g + 1) * CAP] = a[s * CAP : (s + 1) * CAP]
+            outs[s % 2][s // 2, g * CAP : (g + 1) * CAP] = a[s * CAP : (s + 1) * CAP]
         spread = jnp.concatenate([jnp.where(block == i, a, 0.0) for i in range(PACK)], axis=0)
         both = dot(jnp.concatenate(split(spread), axis=0), basis_of(g))
         fitted = both[: PACK * slots] + both[PACK * slots :]
@@ -140,14 +149,14 @@
         energy = jnp.concatenate([energy, jnp.zeros_like(energy)], axis=1)
         for r in (half, half + 2):
             for i in range(2):
-                outs[r][i, below:] = jnp.broadcast_to(energy, (8, LANES))
-
-
-def return_kernel(code, back0, back1, back2, back3, others, chosen, energy):
+                outs[i][r, below:] = jnp.broadcast_to(energy, (8, LANES))
+
+
+def return_kernel(code, mine, theirs, back1, back2, back3, chosen, energy):
     rows = code.shape[1]
-    lanes = others.shape[2]
-    held = others.shape[1] - 8
-    tables = [b.at[0] for b in (back0, back1, back2, back3)] + [others.at[r] for r in range(others.shape[0])]
+    held, lanes = mine.shape[1] - 8, mine.shape[2]
+    backs = (back1, back2, back3)
+    tables = [mine.at[0], theirs.at[0]] + [b.at[i] for b in backs for i in range(2)]
     handlers = len(tables)
     wide = lanes // PACK
     codes = code[...]
@@ -173,17 +182,17 @@
     return pltpu.VMEM(shape, dtype)
 
 
-def call(kernel, place, args, outs, scratch, limit):
+def call(kernel, place, args, outs, scratch, limit, after=()):
     spec = pl.BlockSpec(memory_space=pltpu.VMEM)
     head = [] if place is None else [place]
     return pl.pallas_call(
         kernel,
         out_shape=outs,
-        in_specs=[pl.BlockSpec(memory_space=pltpu.SMEM)] * len(head) + [spec] * len(args),
+        in_specs=[pl.BlockSpec(memory_space=pltpu.SMEM)] * len(head) + [spec] * len(args) + [pl.BlockSpec(memory_space=pl.ANY)] * len(after),
         out_specs=jax.tree.map(lambda _: spec, outs),
         scratch_shapes=scratch,
         compiler_params=pltpu.CompilerParams(vmem_limit_bytes=limit << 20),
-    )(*head, *args)
+    )(*head, *args, *after)
 
 
 def spots_of(n_blk, n_pix):
@@ -210,15 +219,12 @@
     along_y = grouped(spots, lambda z, y, xl, xh, c: (z, xl, xh, c))
     there = {spot: index for index, spot in enumerate(spots)}
 
-    def shifted(array, r):
+    def moved(array, r, other):
         pairs = []
         for z, y, xl, xh, c in spots:
             x = (2 * xh + xl + r) % 4
-            pairs.append((there[z, y, xl, xh, c], there[z, y, x % 2, x // 2, c]))
-        return lax.ppermute(array, ALL, pairs)
-
-    def to_sibling(array):
-        return lax.ppermute(array, ALL, [(i, i ^ 1) for i in range(len(spots))])
+            pairs.append((there[z, y, xl, xh, c], there[z, y, x % 2, x // 2, c ^ other]))
+        return lax.ppermute(array, ALL, pairs) if r or other else array
 
     blk, pix = lax.axis_index("blk"), lax.axis_index("pix")
     z, x_hi = blk >> 3, pix >> 1
@@ -232,18 +238,17 @@
 
     basis = call(prep_kernel, place, [bundles.transpose(0, 2, 1)], sds((width, LANES), bf16), [], 4)
     levels = exchanged(jnp.broadcast_to(basis[None], (n_z, width, LANES)), along_z)
-    near, away, code = call(
+    *sends, code = call(
         slots_kernel,
         place,
         [assign.reshape(1, rows), pixels.T],
-        (sds((chips, held, LANES), bf16), sds((chips, held, LANES), bf16), sds((1, rows), jnp.int32)),
+        (sds((held, LANES), bf16),) * (2 * chips) + (sds((1, rows), jnp.int32),),
         [vmem((LANES, rows), bf16), vmem((1, rows), f32)],
         16,
     )
-    theirs = to_sibling(away)
-    moved = [shifted(jnp.stack([near[r], theirs[r]]), r) for r in range(1, chips)]
-    half = lax.dynamic_index_in_dim(levels.reshape(groups, 2, width, LANES), (z + x_hi) & 1, 1, keepdims=False)
-    plane = exchanged(jnp.broadcast_to(half[None], (n_y, groups, width, LANES)), along_y)
+    received = [moved(send, d // 2, d % 2) for d, send in enumerate(sends)]
+    half = call(pick_kernel, place, [levels], sds((n_y, groups, width, LANES), bf16), [], 4, received[2::2])
+    plane = exchanged(half, along_y)
 
     below = groups * CAP
     slots = 2 * chips * CAP
@@ -251,8 +256,8 @@
     solved = call(
         lambda *refs: solve_kernel(*refs, scale=scale),
         place,
-        [plane, near, theirs, *moved],
-        (sds((2, below + 8, LANES), f32),) * chips,
+        [plane, *received],
+        (sds((chips, below + 8, LANES), f32),) * 2,
         [
             vmem((groups, LANES, LANES), bf16),
             vmem((groups, LANES, LANES), bf16),
@@ -264,10 +269,10 @@
         ],
         16,
     )
-    back = [solved[0]] + [shifted(solved[r], -r) for r in range(1, chips)]
-    others = to_sibling(jnp.stack([b[1] for b in back]))
+    mine, others = solved[0], moved(solved[1], 0, 1)
+    back = [moved(jnp.stack([mine[r], others[r]]), -r, 0) for r in range(1, chips)]
     outs = (sds((width, rows), f32), sds((1, count), f32))
-    chosen, energy = call(return_kernel, None, [code, *back, others], outs, [], 16)
+    chosen, energy = call(return_kernel, None, [code, mine, others, *back], outs, [], 16)
     return chosen.T, energy
 
 

time: 64.1 us -> 63 us (0.983)
  local copies, waits for them, and re-layouts: 4.71 us -> 1.6 us
  Pallas kernels: 9.3 us -> 10.7 us
    ppermute x8 -> x11, waiting for transfers between devices: 13.2 us -> 20.7 us  [moved(): return lax.ppermute(array, ALL, pairs) if r or other else array]
    all_to_all x2, waiting for transfers between devices: 7.09 us -> 0.01 us  [exchanged(): lax.all_to_all(array, ALL, 0, 0, tiled=True, axis_index_groups=groups)]
    pallas_call x4 -> x5, Pallas kernels: 9.3 us -> 10.7 us  [call(): pl.pallas_call(kernel, out_shape=outs, in_specs=[pl.BlockSpec(memory_spac...]
    unnamed x14 -> x6, local copies, waits for them, and re-layouts: 2.18 us -> 0.85 us
    slice x8 -> x2, local copies, waits for them, and re-layouts: 0.93 us -> 0.03 us  [the longest x1 0.02 us: per_device(): mine[r]]
    broadcast_in_dim x2 -> x0, local copies, waits for them, and re-layouts: 0.87 us -> none  [per_device(): jnp.broadcast_to(half[None], (n_y, groups, width, LANES))]
    ppermute x8 -> x11, starting transfers between devices: 15.1 us -> 15.5 us  [moved(): return lax.ppermute(array, ALL, pairs) if r or other else array]
  transfers between devices with their start and end apart: 10 -> 13, of which waited for: 8 -> 10; matrix products, arithmetic and copies ran while one was open for 2% -> 0% of each run, Pallas kernels for 3% -> 3%
where the time goes in v4:
time: 63 us; the launch traced here: 62.7 us
  starting transfers between devices  28.9 us (46%)
  waiting for transfers between devices  20.7 us (33%)
  Pallas kernels  10.7 us (17%)
  local copies, waits for them, and re-layouts  1.6 us (3%)
  between operations  0.71 us (1%)
    ppermute x11, waiting for transfers between devices, moved(): return lax.ppermute(array, ALL, pairs) if r or other else array  20.7 us
    ppermute x11, starting transfers between devices, moved(): return lax.ppermute(array, ALL, pairs) if r or other else array  15.5 us
    all_to_all x2, starting transfers between devices, exchanged(): lax.all_to_all(array, ALL, 0, 0, tiled=True, axis_index_groups=groups)  13.3 us
    pallas_call x5, Pallas kernels, call(): pl.pallas_call(kernel, out_shape=outs, in_specs=[pl.BlockSpec(memory_spac...  10.7 us
  transfers between devices with their start and end apart: 13, of which 10 were waited for; matrix products, arithmetic and copies ran while one was open for 0% of the time, Pallas kernels for 3%

profile of v4, /device:TPU:1, one launch (start us, length us, event | category | flops | bytes accessed | tf_op | source)
XLA Modules:
  0.0 62.7 jit_solution(662159936508669733)
XLA Ops:
  0.7 0.8 %copy-done.1 = bf16[2,224,64]{1,2,0:T(8,128)(2,1)S(1)} copy-done((bf16[2,224,64]{1,2,0:T(8,128)(2,1)S(1)}, bf16[2,224,64]{1,2,0:T(8,128)(2,1)}, u32[]{:S(2)}) %copy-start.1) | copy-done | bytes 57368
  1.6 0.6 shard_map.51
  2.1 0.7 %broadcast_in_dim.2 = bf16[8,64,256]{2,1,0:T(8,128)(2,1)} broadcast(bf16[64,256]{1,0:T(8,128)(2,1)S(1)} %shard_map.51), dimensions={1,2} | broadcast | bytes 294912 | tf_op jit(solution)/shard_map/broadcast_in_dim | solution.py:240
  2.8 9.1 %all-to-all-start = ((bf16[8,64,256]{2,1,0:T(8,128)(2,1)}), bf16[8,64,256]{2,1,0:T(8,128)(2,1)S(1)}, u32[]{:S(2)}, u32[]{:S(2)}) async-start(bf16[8,64,256]{2,1,0:T(8,128)(2,1)} %broadcast_in_dim.2), calls=%async_computation | async-start | bytes 524288 | tf_op jit(solution)/shard_map/all_to_all | solution.py:210
  12.0 2.2 %shard_map.50 = (bf16[256,256]{1,0:T(8,128)(2,1)S(1)}, bf16[256,256]{1,0:T(8,128)(2,1)S(1)}, bf16[256,256]{1,0:T(8,128)(2,1)S(1)}, bf16[256,256]{1,0:T(8,128)(2,...) custom-call(s32[4]{0:T(128)S(1)} %pad_add_fusion.place.refs_0_, ...), custom_call_target="tpu_custom_call" | custom-call | tf_op jit(solution)/shard_map/pallas_call | solution.py:188
  14.2 1.3 %collective-permute-start = (bf16[256,256]{1,0:T(8,128)(2,1)S(1)}, bf16[256,256]{1,0:T(8,128)(2,1)S(1)}, u32[]{:S(2)}, u32[]{:S(2)}) collective-permute-start(bf16[256,256]{1,0:T(8,128)(2,1)S(1)} %get-tuple-element.16), channel_id=1, source_target_pairs={{0,4},{1,5},{2,6},{3,7},{4,2},{5,3},{6,0},{7,1},{8,12},{9,13},{10,... | collective-permute-start | bytes 393224 | tf_op jit(solution)/shard_map/ppermute | solution.py:227
  15.5 2.4 %collective-permute-start.1 = (bf16[256,256]{1,0:T(8,128)(2,1)S(1)}, bf16[256,256]{1,0:T(8,128)(2,1)S(1)}, u32[]{:S(2)}, u32[]{:S(2)}) collective-permute-start(bf16[256,256]{1,0:T(8,128)(2,1)S(1)} %get-tuple-element.17), channel_id=1, source_target_pairs={{0,2},{1,3},{2,0},{3,1},{4,6},{5,7},{6,4},{7,5},{8,10},{9,11},{10,... | collective-permute-start | bytes 393224 | tf_op jit(solution)/shard_map/ppermute | solution.py:227
  17.9 1.1 %collective-permute-start.2 = (bf16[256,256]{1,0:T(8,128)(2,1)S(1)}, bf16[256,256]{1,0:T(8,128)(2,1)S(1)}, u32[]{:S(2)}, u32[]{:S(2)}) collective-permute-start(bf16[256,256]{1,0:T(8,128)(2,1)S(1)} %get-tuple-element.18), channel_id=1, source_target_pairs={{0,6},{1,7},{2,4},{3,5},{4,0},{5,1},{6,2},{7,3},{8,14},{9,15},{10,... | collective-permute-start | bytes 393224 | tf_op jit(solution)/shard_map/ppermute | solution.py:227
  19.6 3.4 %collective-permute-done.1.rest_1_.refs_6_ = bf16[256,256]{1,0:T(8,128)(2,1)S(1)} collective-permute-done((bf16[256,256]{1,0:T(8,128)(2,1)S(1)}, bf16[256,256]{1,0:T(8,128)(2,1)S(1)}, u32[]{:S(2)}, u32[]{:S(2)}) %collective-permute-start.1) | collective-permute-done | bytes 131104 | tf_op jit(solution)/shard_map/ppermute | solution.py:227
  23.5 1.4 %shard_map.52 = bf16[4,4,64,256]{3,2,1,0:T(8,128)(2,1)} custom-call(s32[4]{0:T(128)S(1)} %pad_add_fusion.place.refs_0_, bf16[8,64,256]{2,1,0:T(8,128)(2,1)S(1)} %all-to-all-done.levels, bf16[256,256]{1,0:T(8,128)(2,1)S(1)} %collective-permute-done.rest_0_.refs_4_, bf16[256,256]{1,0:T(8,128)(2,1)S(1)} %collective-permute-done.1.rest_1_.refs_6_, ...), custom_call_target="tpu_custom_call" | custom-call | tf_op jit(solution)/shard_map/pallas_call | solution.py:188
  24.8 4.2 %all-to-all-start.1 = ((bf16[4,4,64,256]{3,2,1,0:T(8,128)(2,1)}), bf16[4,4,64,256]{3,2,1,0:T(8,128)(2,1)S(1)}, u32[]{:S(2)}, u32[]{:S(2)}) async-start(bf16[4,4,64,256]{3,2,1,0:T(8,128)(2,1)} %shard_map.52), calls=%async_computation.1 | async-start | bytes 1048576 | tf_op jit(solution)/shard_map/all_to_all | solution.py:210
  29.0 2.0 %collective-permute-start.3 = (bf16[256,256]{1,0:T(8,128)(2,1)S(1)}, bf16[256,256]{1,0:T(8,128)(2,1)S(1)}, u32[]{:S(2)}, u32[]{:S(2)}) collective-permute-start(bf16[256,256]{1,0:T(8,128)(2,1)S(1)} %get-tuple-element.20), channel_id=1, source_target_pairs={{0,1},{1,0},{2,3},{3,2},{4,5},{5,4},{6,7},{7,6},{8,9},{9,8},{10,11... | collective-permute-start | bytes 393224 | tf_op jit(solution)/shard_map/ppermute | solution.py:227
  31.0 0.9 %collective-permute-start.4 = (bf16[256,256]{1,0:T(8,128)(2,1)S(1)}, bf16[256,256]{1,0:T(8,128)(2,1)S(1)}, u32[]{:S(2)}, u32[]{:S(2)}) collective-permute-start(bf16[256,256]{1,0:T(8,128)(2,1)S(1)} %get-tuple-element.21), channel_id=1, source_target_pairs={{0,5},{1,4},{2,7},{3,6},{4,3},{5,2},{6,1},{7,0},{8,13},{9,12},{10,... | collective-permute-start | bytes 393224 | tf_op jit(solution)/shard_map/ppermute | solution.py:227
  32.0 2.8 %collective-permute-start.5 = (bf16[256,256]{1,0:T(8,128)(2,1)S(1)}, bf16[256,256]{1,0:T(8,128)(2,1)S(1)}, u32[]{:S(2)}, u32[]{:S(2)}) collective-permute-start(bf16[256,256]{1,0:T(8,128)(2,1)S(1)} %get-tuple-element.22), channel_id=1, source_target_pairs={{0,3},{1,2},{2,1},{3,0},{4,7},{5,6},{6,5},{7,4},{8,11},{9,10},{10,... | collective-permute-start | bytes 393224 | tf_op jit(solution)/shard_map/ppermute | solution.py:227
  34.8 0.9 %collective-permute-start.6 = (bf16[256,256]{1,0:T(8,128)(2,1)S(1)}, bf16[256,256]{1,0:T(8,128)(2,1)S(1)}, u32[]{:S(2)}, u32[]{:S(2)}) collective-permute-start(bf16[256,256]{1,0:T(8,128)(2,1)S(1)} %get-tuple-element.23), channel_id=1, source_target_pairs={{0,7},{1,6},{2,5},{3,4},{4,1},{5,0},{6,3},{7,2},{8,15},{9,14},{10,... | collective-permute-start | bytes 393224 | tf_op jit(solution)/shard_map/ppermute | solution.py:227
  35.7 2.0 %collective-permute-done.4.refs_5_ = bf16[256,256]{1,0:T(8,128)(2,1)S(1)} collective-permute-done((bf16[256,256]{1,0:T(8,128)(2,1)S(1)}, bf16[256,256]{1,0:T(8,128)(2,1)S(1)}, u32[]{:S(2)}, u32[]{:S(2)}) %collective-permute-start.4) | collective-permute-done | bytes 131104 | tf_op jit(solution)/shard_map/ppermute | solution.py:227
  37.7 3.3 %collective-permute-done.5.refs_7_ = bf16[256,256]{1,0:T(8,128)(2,1)S(1)} collective-permute-done((bf16[256,256]{1,0:T(8,128)(2,1)S(1)}, bf16[256,256]{1,0:T(8,128)(2,1)S(1)}, u32[]{:S(2)}, u32[]{:S(2)}) %collective-permute-start.5) | collective-permute-done | bytes 131104 | tf_op jit(solution)/shard_map/ppermute | solution.py:227
  41.3 4.8 %shard_map.53 = (f32[4,72,256]{2,1,0:T(8,128)S(1)}, f32[4,72,256]{2,1,0:T(8,128)S(1)}) custom-call(s32[4]{0:T(128)S(1)} %pad_add_fusion.place.refs_0_, bf16[4,4,64,256]{3,2,1,0:T(8,128)(2,1)S(1)} %all-to-all-done.1.refs_1_, bf16[256,256]{1,0:T(8,128)(2,1)S(1)} %get-tuple-element.19.refs_2_, bf16[256,256]{1,0:T(8,128)(2,1)S(1)} %collective-permute-done.3.refs_3_, ...), custom_call_target="tpu_custom_call" | custom-call | tf_op jit(solution)/shard_map/pallas_call | solution.py:188
  46.6 1.2 %collective-permute-done.7.theirs = f32[4,72,256]{2,1,0:T(8,128)S(1)} collective-permute-done((f32[4,72,256]{2,1,0:T(8,128)S(1)}, f32[4,72,256]{2,1,0:T(8,128)S(1)}, u32[]{:S(2)}, u32[]{:S(2)}) %collective-permute-start.7) | collective-permute-done | bytes 294944 | tf_op jit(solution)/shard_map/ppermute | solution.py:227
  47.8 2.6 %collective-permute-start.8 = (f32[2,72,256]{2,1,0:T(8,128)S(1)}, f32[2,72,256]{2,1,0:T(8,128)S(1)}, u32[]{:S(2)}, u32[]{:S(2)}) collective-permute-start(f32[2,72,256]{2,1,0:T(8,128)S(1)} %pad_maximum_fusion), channel_id=1, source_target_pairs={{0,6},{1,7},{2,4},{3,5},{4,0},{5,1},{6,2},{7,3},{8,14},{9,15},{10,... | collective-permute-start | bytes 442376 | tf_op jit(solution)/shard_map/ppermute | solution.py:227
  50.4 0.6 collective-permute-start.9
  51.4 4.9 %collective-permute-done.8.back1 = f32[2,72,256]{2,1,0:T(8,128)S(1)} collective-permute-done((f32[2,72,256]{2,1,0:T(8,128)S(1)}, f32[2,72,256]{2,1,0:T(8,128)S(1)}, u32[]{:S(2)}, u32[]{:S(2)}) %collective-permute-start.8) | collective-permute-done | bytes 147488 | tf_op jit(solution)/shard_map/ppermute | solution.py:227
  56.8 4.2 %collective-permute-done.10.back3 = f32[2,72,256]{2,1,0:T(8,128)S(1)} collective-permute-done((f32[2,72,256]{2,1,0:T(8,128)S(1)}, f32[2,72,256]{2,1,0:T(8,128)S(1)}, u32[]{:S(2)}, u32[]{:S(2)}) %collective-permute-start.10) | collective-permute-done | bytes 147488 | tf_op jit(solution)/shard_map/ppermute | solution.py:227
  61.0 1.7 %shard_map.54 = (f32[64,1024]{1,0:T(8,128)}, f32[1,128]{1,0:T(1,128)}) custom-call(s32[1,1024]{1,0:T(1,128)S(1)} %get-tuple-element.15.code, f32[4,72,256]{2,1,0:T(8,128)S(1)} %get-tuple-element.24.mine, f32[4,72,256]{2,1,0:T(8,128)S(1)} %collective-permute-done.7.theirs, f32[2,72,256]{2,1,0:T(8,128)S(1)} %collective-permute-done.8.back1, ...), custom_call_target="tpu_custom_call" | custom-call | tf_op jit(solution)/shard_map/pallas_call | solution.py:188
  (20 shorter events, 2.7 us)
Async XLA Ops:
  0.7 0.8 %copy-start.1 = (bf16[2,224,64]{1,2,0:T(8,128)(2,1)S(1)}, bf16[2,224,64]{1,2,0:T(8,128)(2,1)}, u32[]{:S(2)}) copy-start(bf16[2,224,64]{1,2,0:T(8,128)(2,1)} %param.4) | copy-start | bytes 172036
  1.6 10.4 %copy-start = (bf16[1024,224]{0,1:T(8,128)(2,1)S(1)}, bf16[1024,224]{0,1:T(8,128)(2,1)}, u32[]{:S(2)}) copy-start(bf16[1024,224]{0,1:T(8,128)(2,1)} %param.3) | copy-start | bytes 1376260
  2.8 9.2 %copy-start.2 = (s32[1024,1]{0,1:T(1,128)S(1)}, s32[1024,1]{0,1:T(1,128)}, u32[]{:S(2)}) copy-start(s32[1024,1]{0,1:T(1,128)} %param.5) | copy-start | bytes 12292
  2.8 20.6 %all-to-all-start = ((bf16[8,64,256]{2,1,0:T(8,128)(2,1)}), bf16[8,64,256]{2,1,0:T(8,128)(2,1)S(1)}, u32[]{:S(2)}, u32[]{:S(2)}) async-start(bf16[8,64,256]{2,1,0:T(8,128)(2,1)} %broadcast_in_dim.2), calls=%async_computation | async-start | bytes 524288 | tf_op jit(solution)/shard_map/all_to_all | solution.py:210
  14.2 5.4 %collective-permute-start = (bf16[256,256]{1,0:T(8,128)(2,1)S(1)}, bf16[256,256]{1,0:T(8,128)(2,1)S(1)}, u32[]{:S(2)}, u32[]{:S(2)}) collective-permute-start(bf16[256,256]{1,0:T(8,128)(2,1)S(1)} %get-tuple-element.16), channel_id=1, source_target_pairs={{0,4},{1,5},{2,6},{3,7},{4,2},{5,3},{6,0},{7,1},{8,12},{9,13},{10,... | collective-permute-start | bytes 393224 | tf_op jit(solution)/shard_map/ppermute | solution.py:227
  15.5 7.5 %collective-permute-start.1 = (bf16[256,256]{1,0:T(8,128)(2,1)S(1)}, bf16[256,256]{1,0:T(8,128)(2,1)S(1)}, u32[]{:S(2)}, u32[]{:S(2)}) collective-permute-start(bf16[256,256]{1,0:T(8,128)(2,1)S(1)} %get-tuple-element.17), channel_id=1, source_target_pairs={{0,2},{1,3},{2,0},{3,1},{4,6},{5,7},{6,4},{7,5},{8,10},{9,11},{10,... | collective-permute-start | bytes 393224 | tf_op jit(solution)/shard_map/ppermute | solution.py:227
  17.9 5.5 %collective-permute-start.2 = (bf16[256,256]{1,0:T(8,128)(2,1)S(1)}, bf16[256,256]{1,0:T(8,128)(2,1)S(1)}, u32[]{:S(2)}, u32[]{:S(2)}) collective-permute-start(bf16[256,256]{1,0:T(8,128)(2,1)S(1)} %get-tuple-element.18), channel_id=1, source_target_pairs={{0,6},{1,7},{2,4},{3,5},{4,0},{5,1},{6,2},{7,3},{8,14},{9,15},{10,... | collective-permute-start | bytes 393224 | tf_op jit(solution)/shard_map/ppermute | solution.py:227
  24.8 16.4 %all-to-all-start.1 = ((bf16[4,4,64,256]{3,2,1,0:T(8,128)(2,1)}), bf16[4,4,64,256]{3,2,1,0:T(8,128)(2,1)S(1)}, u32[]{:S(2)}, u32[]{:S(2)}) async-start(bf16[4,4,64,256]{3,2,1,0:T(8,128)(2,1)} %shard_map.52), calls=%async_computation.1 | async-start | bytes 1048576 | tf_op jit(solution)/shard_map/all_to_all | solution.py:210
  29.0 6.7 %collective-permute-start.3 = (bf16[256,256]{1,0:T(8,128)(2,1)S(1)}, bf16[256,256]{1,0:T(8,128)(2,1)S(1)}, u32[]{:S(2)}, u32[]{:S(2)}) collective-permute-start(bf16[256,256]{1,0:T(8,128)(2,1)S(1)} %get-tuple-element.20), channel_id=1, source_target_pairs={{0,1},{1,0},{2,3},{3,2},{4,5},{5,4},{6,7},{7,6},{8,9},{9,8},{10,11... | collective-permute-start | bytes 393224 | tf_op jit(solution)/shard_map/ppermute | solution.py:227
  31.0 6.6 %collective-permute-start.4 = (bf16[256,256]{1,0:T(8,128)(2,1)S(1)}, bf16[256,256]{1,0:T(8,128)(2,1)S(1)}, u32[]{:S(2)}, u32[]{:S(2)}) collective-permute-start(bf16[256,256]{1,0:T(8,128)(2,1)S(1)} %get-tuple-element.21), channel_id=1, source_target_pairs={{0,5},{1,4},{2,7},{3,6},{4,3},{5,2},{6,1},{7,0},{8,13},{9,12},{10,... | collective-permute-start | bytes 393224 | tf_op jit(solution)/shard_map/ppermute | solution.py:227
  32.0 9.0 %collective-permute-start.5 = (bf16[256,256]{1,0:T(8,128)(2,1)S(1)}, bf16[256,256]{1,0:T(8,128)(2,1)S(1)}, u32[]{:S(2)}, u32[]{:S(2)}) collective-permute-start(bf16[256,256]{1,0:T(8,128)(2,1)S(1)} %get-tuple-element.22), channel_id=1, source_target_pairs={{0,3},{1,2},{2,1},{3,0},{4,7},{5,6},{6,5},{7,4},{8,11},{9,10},{10,... | collective-permute-start | bytes 393224 | tf_op jit(solution)/shard_map/ppermute | solution.py:227
  34.8 6.5 %collective-permute-start.6 = (bf16[256,256]{1,0:T(8,128)(2,1)S(1)}, bf16[256,256]{1,0:T(8,128)(2,1)S(1)}, u32[]{:S(2)}, u32[]{:S(2)}) collective-permute-start(bf16[256,256]{1,0:T(8,128)(2,1)S(1)} %get-tuple-element.23), channel_id=1, source_target_pairs={{0,7},{1,6},{2,5},{3,4},{4,1},{5,0},{6,3},{7,2},{8,15},{9,14},{10,... | collective-permute-start | bytes 393224 | tf_op jit(solution)/shard_map/ppermute | solution.py:227
  46.1 1.7 %collective-permute-start.7 = (f32[4,72,256]{2,1,0:T(8,128)S(1)}, f32[4,72,256]{2,1,0:T(8,128)S(1)}, u32[]{:S(2)}, u32[]{:S(2)}) collective-permute-start(f32[4,72,256]{2,1,0:T(8,128)S(1)} %get-tuple-element.25), channel_id=1, source_target_pairs={{0,1},{1,0},{2,3},{3,2},{4,5},{5,4},{6,7},{7,6},{8,9},{9,8},{10,11... | collective-permute-start | bytes 884744 | tf_op jit(solution)/shard_map/ppermute | solution.py:227
  47.8 8.5 %collective-permute-start.8 = (f32[2,72,256]{2,1,0:T(8,128)S(1)}, f32[2,72,256]{2,1,0:T(8,128)S(1)}, u32[]{:S(2)}, u32[]{:S(2)}) collective-permute-start(f32[2,72,256]{2,1,0:T(8,128)S(1)} %pad_maximum_fusion), channel_id=1, source_target_pairs={{0,6},{1,7},{2,4},{3,5},{4,0},{5,1},{6,2},{7,3},{8,14},{9,15},{10,... | collective-permute-start | bytes 442376 | tf_op jit(solution)/shard_map/ppermute | solution.py:227
  50.4 6.4 %collective-permute-start.9 = (f32[2,72,256]{2,1,0:T(8,128)S(1)}, f32[2,72,256]{2,1,0:T(8,128)S(1)}, u32[]{:S(2)}, u32[]{:S(2)}) collective-permute-start(f32[2,72,256]{2,1,0:T(8,128)S(1)} %pad_maximum_fusion.1), channel_id=1, source_target_pairs={{0,2},{1,3},{2,0},{3,1},{4,6},{5,7},{6,4},{7,5},{8,10},{9,11},{10,... | collective-permute-start | bytes 442376 | tf_op jit(solution)/shard_map/ppermute | solution.py:227
  51.0 9.9 %collective-permute-start.10 = (f32[2,72,256]{2,1,0:T(8,128)S(1)}, f32[2,72,256]{2,1,0:T(8,128)S(1)}, u32[]{:S(2)}, u32[]{:S(2)}) collective-permute-start(f32[2,72,256]{2,1,0:T(8,128)S(1)} %pad_maximum_fusion.2), channel_id=1, source_target_pairs={{0,4},{1,5},{2,6},{3,7},{4,2},{5,3},{6,0},{7,1},{8,12},{9,13},{10,... | collective-permute-start | bytes 442376 | tf_op jit(solution)/shard_map/ppermute | solution.py:227

commit v5 on v4

--- a/solution.py
+++ b/solution.py
@@ -58,9 +58,10 @@
         ranks[:, part] = jnp.sum(named * running, axis=0, keepdims=True) - 1.0
         carry = running[:, chunk - 1 :]
     rank = ranks[...].astype(jnp.int32)
-    chip = ((label >> 4) + place[2] & 1) * 2 + (label >> 1 & 1)
+    other = (label >> 6) ^ place[2]
+    chip = other * 2 + (label >> 1 & 1)
     handler = (chip - place[3] & 3) * 2 + (label + place[0] & 1)
-    local = (label >> 5) * PACK + (label >> 2 & 3)
+    local = ((label >> 4 & 3) ^ other * 3) * PACK + (label >> 2 & 3)
     slot = local * CAP + rank
     held = outs[0].shape[0]
     for d in range(len(outs)):
@@ -70,13 +71,10 @@
     code[...] = (local & 3) * 1024 + table_row
 
 
-def pick_kernel(place, levels, *rest):
+def repeat_kernel(basis, *rest):
     out = rest[-1]
-    odd = place[2] + place[1] & 1
-    for g in range(out.shape[1]):
-        level = levels[2 * g + odd]
-        for y in range(out.shape[0]):
-            out[y, g] = level
+    for i in range(out.shape[0]):
+        out[i] = basis[...]
 
 
 def solve_kernel(place, bundles, *rest, scale):
@@ -89,7 +87,7 @@
     same = iota((LANES, LANES), 0) // wide == iota((LANES, LANES), 1) // wide
 
     def basis_of(g):
-        return jnp.concatenate([bundles[i, g] for i in range(PACK)], axis=0)
+        return jnp.concatenate([bundles[PACK * g + i] for i in range(PACK)], axis=0)
 
     def pixels_of(local):
         return jnp.concatenate([s[local * CAP : (local + 1) * CAP] for s in sources], axis=0)
@@ -124,7 +122,6 @@
 
     lax.fori_loop(1, ITERS, sweep, 0)
     parts[...] = jnp.zeros(parts.shape, f32)
-    odd = place[2] + place[1] & 1
     for g in range(groups):
         a = state[g]
         for s in range(len(sources)):
@@ -135,7 +132,7 @@
         for i in range(PACK):
             misfit = pixels_of(PACK * g + i).astype(f32) - fitted[i * slots : (i + 1) * slots]
             square = misfit * misfit
-            bundle = 16 * (2 * g + odd) + 4 * i + 2 * (place[3] & 1) + place[0]
+            bundle = 16 * (4 * place[2] + g ^ 7 * place[1]) + 4 * i + 2 * (place[3] & 1) + place[0]
             for half in range(2):
                 both = square[2 * half * CAP : 2 * (half + 1) * CAP]
                 both = both + square[2 * (half + 2) * CAP : 2 * (half + 3) * CAP]
@@ -215,9 +212,9 @@
     owned, _, width = bundles.shape
     n_blk, n_pix = lax.axis_size("blk"), lax.axis_size("pix")
     spots = spots_of(n_blk, n_pix)
-    along_z = grouped(spots, lambda z, y, xl, xh, c: (y, xl, xh, c))
-    along_y = grouped(spots, lambda z, y, xl, xh, c: (z, xl, xh, c))
+    column = grouped(spots, lambda z, y, xl, xh, c: (z // 4, xl, xh, c))
     there = {spot: index for index, spot in enumerate(spots)}
+    swap = [(there[s], there[(s[0] ^ 7 * s[3],) + s[1:]]) for s in spots]
 
     def moved(array, r, other):
         pairs = []
@@ -228,16 +225,15 @@
 
     blk, pix = lax.axis_index("blk"), lax.axis_index("pix")
     z, x_hi = blk >> 3, pix >> 1
-    place = jnp.stack([pix & 1, x_hi, z & 1, 2 * x_hi + (blk & 1)]).astype(jnp.int32)
+    place = jnp.stack([pix & 1, x_hi, z >> 2, 2 * x_hi + (blk & 1)]).astype(jnp.int32)
     sds = jax.ShapeDtypeStruct
-    n_z, n_y = len(along_z[0]), len(along_y[0])
-    chips = 4
+    n_col, chips = len(column[0]), 4
     count = n_blk * owned
-    groups = n_z // 2
-    held = groups * n_y * CAP
+    groups = n_col // PACK
+    held = n_col * CAP
 
     basis = call(prep_kernel, place, [bundles.transpose(0, 2, 1)], sds((width, LANES), bf16), [], 4)
-    levels = exchanged(jnp.broadcast_to(basis[None], (n_z, width, LANES)), along_z)
+    basis = lax.ppermute(basis, ALL, swap)
     *sends, code = call(
         slots_kernel,
         place,
@@ -246,9 +242,9 @@
         [vmem((LANES, rows), bf16), vmem((1, rows), f32)],
         16,
     )
+    basis = call(repeat_kernel, None, [basis], sds((n_col, width, LANES), bf16), [], 4, [sends[0]])
+    gathered = exchanged(basis, column)
     received = [moved(send, d // 2, d % 2) for d, send in enumerate(sends)]
-    half = call(pick_kernel, place, [levels], sds((n_y, groups, width, LANES), bf16), [], 4, received[2::2])
-    plane = exchanged(half, along_y)
 
     below = groups * CAP
     slots = 2 * chips * CAP
@@ -256,7 +252,7 @@
     solved = call(
         lambda *refs: solve_kernel(*refs, scale=scale),
         place,
-        [plane, *received],
+        [gathered, *received],
         (sds((chips, below + 8, LANES), f32),) * 2,
         [
             vmem((groups, LANES, LANES), bf16),

time: 63 us -> 58.8 us (0.933)
  waiting for transfers between devices: 20.7 us -> 16.1 us
    ppermute x11, waiting for transfers between devices: 20.7 us -> 16.1 us  [moved(): return lax.ppermute(array, ALL, pairs) if r or other else array]
    all_to_all x2 -> x1, starting transfers between devices: 13.3 us -> 9.19 us  [exchanged(): lax.all_to_all(array, ALL, 0, 0, tiled=True, axis_index_groups=groups)]
    ppermute x11, starting transfers between devices: 15.5 us -> 19.6 us  [moved(): return lax.ppermute(array, ALL, pairs) if r or other else array]
    unnamed x6, local copies, waits for them, and re-layouts: 0.85 us -> 1.86 us
    broadcast_in_dim x1 -> x0, local copies, waits for them, and re-layouts: 0.72 us -> none  [per_device(): jnp.broadcast_to(basis[None], (n_z, width, LANES))]
    ppermute x0 -> x1, starting transfers between devices: none -> 0.66 us  [per_device(): basis = lax.ppermute(basis, ALL, swap)]
  transfers between devices with their start and end apart: 13 -> 13, of which waited for: 10 -> 9; matrix products, arithmetic and copies ran while one was open for 0% -> 0% of each run, Pallas kernels for 3% -> 4%
where the time goes in v5:
time: 58.8 us; the launch traced here: 58.5 us
  starting transfers between devices  29.5 us (50%)
  waiting for transfers between devices  16.1 us (27%)
  Pallas kernels  10.2 us (17%)
  local copies, waits for them, and re-layouts  1.89 us (3%)
  between operations  0.74 us (1%)
    ppermute x11, starting transfers between devices, moved(): return lax.ppermute(array, ALL, pairs) if r or other else array  19.6 us
    ppermute x11, waiting for transfers between devices, moved(): return lax.ppermute(array, ALL, pairs) if r or other else array  16.1 us
    pallas_call x5, Pallas kernels, call(): pl.pallas_call(kernel, out_shape=outs, in_specs=[pl.BlockSpec(memory_spac...  10.2 us
    all_to_all x1, starting transfers between devices, exchanged(): lax.all_to_all(array, ALL, 0, 0, tiled=True, axis_index_groups=groups)  9.19 us
    unnamed x6, local copies, waits for them, and re-layouts  1.86 us
  transfers between devices with their start and end apart: 13, of which 9 were waited for; matrix products, arithmetic and copies ran while one was open for 0% of the time, Pallas kernels for 4%

profile of v5, /device:TPU:1, one launch (start us, length us, event | category | flops | bytes accessed | tf_op | source)
XLA Modules:
  0.0 58.5 jit_solution(10853552919716122287)
XLA Ops:
  0.7 0.8 %copy-done.1 = bf16[2,224,64]{1,2,0:T(8,128)(2,1)S(1)} copy-done((bf16[2,224,64]{1,2,0:T(8,128)(2,1)S(1)}, bf16[2,224,64]{1,2,0:T(8,128)(2,1)}, u32[]{:S(2)}) %copy-start.1) | copy-done | bytes 57368
  1.6 0.6 shard_map.51
  2.1 0.7 %collective-permute-start = (bf16[64,256]{1,0:T(8,128)(2,1)S(1)}, bf16[64,256]{1,0:T(8,128)(2,1)S(1)}, u32[]{:S(2)}, u32[]{:S(2)}) collective-permute-start(bf16[64,256]{1,0:T(8,128)(2,1)S(1)} %shard_map.51), channel_id=1, source_target_pairs={{0,0},{1,1},{2,226},{3,227},{4,4},{5,5},{6,230},{7,231},{8,8},{9,9... | collective-permute-start | bytes 98312 | tf_op jit(solution)/shard_map/ppermute | solution.py:236
  2.8 1.0 %copy-done = bf16[1024,224]{0,1:T(8,128)(2,1)S(1)} copy-done((bf16[1024,224]{0,1:T(8,128)(2,1)S(1)}, bf16[1024,224]{0,1:T(8,128)(2,1)}, u32[]{:S(2)}) %copy-start) | copy-done | bytes 458776
  3.8 2.2 %shard_map.50 = (bf16[256,256]{1,0:T(8,128)(2,1)S(1)}, bf16[256,256]{1,0:T(8,128)(2,1)S(1)}, bf16[256,256]{1,0:T(8,128)(2,1)S(1)}, bf16[256,256]{1,0:T(8,128)(2,...) custom-call(s32[4]{0:T(128)S(1)} %pad_add_fusion.place.refs_0_, ...), custom_call_target="tpu_custom_call" | custom-call | tf_op jit(solution)/shard_map/pallas_call | solution.py:185
  6.0 0.8 %shard_map.52 = bf16[16,64,256]{2,1,0:T(8,128)(2,1)} custom-call(bf16[64,256]{1,0:T(8,128)(2,1)S(1)} %collective-permute-done.basis, bf16[256,256]{1,0:T(8,128)(2,1)S(1)} %get-tuple-element.16.rest_0_.refs_2_), custom_call_target="tpu_custom_call" | custom-call | tf_op jit(solution)/shard_map/pallas_call | solution.py:185
  6.9 9.2 %all-to-all-start = ((bf16[16,64,256]{2,1,0:T(8,128)(2,1)}), bf16[16,64,256]{2,1,0:T(8,128)(2,1)S(1)}, u32[]{:S(2)}, u32[]{:S(2)}) async-start(bf16[16,64,256]{2,1,0:T(8,128)(2,1)} %shard_map.52), calls=%async_computation | async-start | bytes 1048576 | tf_op jit(solution)/shard_map/all_to_all | solution.py:207
  16.1 1.0 %collective-permute-start.1 = (bf16[256,256]{1,0:T(8,128)(2,1)S(1)}, bf16[256,256]{1,0:T(8,128)(2,1)S(1)}, u32[]{:S(2)}, u32[]{:S(2)}) collective-permute-start(bf16[256,256]{1,0:T(8,128)(2,1)S(1)} %get-tuple-element.17), channel_id=1, source_target_pairs={{0,1},{1,0},{2,3},{3,2},{4,5},{5,4},{6,7},{7,6},{8,9},{9,8},{10,11... | collective-permute-start | bytes 393224 | tf_op jit(solution)/shard_map/ppermute | solution.py:224
  17.1 1.2 %collective-permute-start.2 = (bf16[256,256]{1,0:T(8,128)(2,1)S(1)}, bf16[256,256]{1,0:T(8,128)(2,1)S(1)}, u32[]{:S(2)}, u32[]{:S(2)}) collective-permute-start(bf16[256,256]{1,0:T(8,128)(2,1)S(1)} %get-tuple-element.18), channel_id=1, source_target_pairs={{0,4},{1,5},{2,6},{3,7},{4,2},{5,3},{6,0},{7,1},{8,12},{9,13},{10,... | collective-permute-start | bytes 393224 | tf_op jit(solution)/shard_map/ppermute | solution.py:224
  18.3 6.3 %collective-permute-start.3 = (bf16[256,256]{1,0:T(8,128)(2,1)S(1)}, bf16[256,256]{1,0:T(8,128)(2,1)S(1)}, u32[]{:S(2)}, u32[]{:S(2)}) collective-permute-start(bf16[256,256]{1,0:T(8,128)(2,1)S(1)} %get-tuple-element.19), channel_id=1, source_target_pairs={{0,5},{1,4},{2,7},{3,6},{4,3},{5,2},{6,1},{7,0},{8,13},{9,12},{10,... | collective-permute-start | bytes 393224 | tf_op jit(solution)/shard_map/ppermute | solution.py:224
  24.6 1.1 %collective-permute-start.4 = (bf16[256,256]{1,0:T(8,128)(2,1)S(1)}, bf16[256,256]{1,0:T(8,128)(2,1)S(1)}, u32[]{:S(2)}, u32[]{:S(2)}) collective-permute-start(bf16[256,256]{1,0:T(8,128)(2,1)S(1)} %get-tuple-element.20), channel_id=1, source_target_pairs={{0,2},{1,3},{2,0},{3,1},{4,6},{5,7},{6,4},{7,5},{8,10},{9,11},{10,... | collective-permute-start | bytes 393224 | tf_op jit(solution)/shard_map/ppermute | solution.py:224
  25.7 2.2 %collective-permute-start.5 = (bf16[256,256]{1,0:T(8,128)(2,1)S(1)}, bf16[256,256]{1,0:T(8,128)(2,1)S(1)}, u32[]{:S(2)}, u32[]{:S(2)}) collective-permute-start(bf16[256,256]{1,0:T(8,128)(2,1)S(1)} %get-tuple-element.21), channel_id=1, source_target_pairs={{0,3},{1,2},{2,1},{3,0},{4,7},{5,6},{6,5},{7,4},{8,11},{9,10},{10,... | collective-permute-start | bytes 393224 | tf_op jit(solution)/shard_map/ppermute | solution.py:224
  28.2 2.5 %collective-permute-start.7 = (bf16[256,256]{1,0:T(8,128)(2,1)S(1)}, bf16[256,256]{1,0:T(8,128)(2,1)S(1)}, u32[]{:S(2)}, u32[]{:S(2)}) collective-permute-start(bf16[256,256]{1,0:T(8,128)(2,1)S(1)} %get-tuple-element.23), channel_id=1, source_target_pairs={{0,7},{1,6},{2,5},{3,4},{4,1},{5,0},{6,3},{7,2},{8,15},{9,14},{10,... | collective-permute-start | bytes 393224 | tf_op jit(solution)/shard_map/ppermute | solution.py:224
  30.7 0.6 collective-permute-done.3.refs_5_
  31.3 3.5 %collective-permute-done.4.refs_6_ = bf16[256,256]{1,0:T(8,128)(2,1)S(1)} collective-permute-done((bf16[256,256]{1,0:T(8,128)(2,1)S(1)}, bf16[256,256]{1,0:T(8,128)(2,1)S(1)}, u32[]{:S(2)}, u32[]{:S(2)}) %collective-permute-start.4) | collective-permute-done | bytes 131104 | tf_op jit(solution)/shard_map/ppermute | solution.py:224
  34.8 3.0 %collective-permute-done.5.refs_7_ = bf16[256,256]{1,0:T(8,128)(2,1)S(1)} collective-permute-done((bf16[256,256]{1,0:T(8,128)(2,1)S(1)}, bf16[256,256]{1,0:T(8,128)(2,1)S(1)}, u32[]{:S(2)}, u32[]{:S(2)}) %collective-permute-start.5) | collective-permute-done | bytes 131104 | tf_op jit(solution)/shard_map/ppermute | solution.py:224
  38.3 4.8 %shard_map.53 = (f32[4,72,256]{2,1,0:T(8,128)S(1)}, f32[4,72,256]{2,1,0:T(8,128)S(1)}) custom-call(s32[4]{0:T(128)S(1)} %pad_add_fusion.place.refs_0_, bf16[16,64,256]{2,1,0:T(8,128)(2,1)S(1)} %all-to-all-done.refs_1_, bf16[256,256]{1,0:T(8,128)(2,1)S(1)} %get-tuple-element.16.rest_0_.refs_2_, bf16[256,256]{1,0:T(8,128)(2,1)S(1)} %collective-permute-done.1.refs_3_, ...), custom_call_target="tpu_custom_call" | custom-call | tf_op jit(solution)/shard_map/pallas_call | solution.py:185
  43.6 1.2 %collective-permute-done.8.theirs = f32[4,72,256]{2,1,0:T(8,128)S(1)} collective-permute-done((f32[4,72,256]{2,1,0:T(8,128)S(1)}, f32[4,72,256]{2,1,0:T(8,128)S(1)}, u32[]{:S(2)}, u32[]{:S(2)}) %collective-permute-start.8) | collective-permute-done | bytes 294944 | tf_op jit(solution)/shard_map/ppermute | solution.py:224
  44.8 1.9 %collective-permute-start.9 = (f32[2,72,256]{2,1,0:T(8,128)S(1)}, f32[2,72,256]{2,1,0:T(8,128)S(1)}, u32[]{:S(2)}, u32[]{:S(2)}) collective-permute-start(f32[2,72,256]{2,1,0:T(8,128)S(1)} %pad_maximum_fusion), channel_id=1, source_target_pairs={{0,6},{1,7},{2,4},{3,5},{4,0},{5,1},{6,2},{7,3},{8,14},{9,15},{10,... | collective-permute-start | bytes 442376 | tf_op jit(solution)/shard_map/ppermute | solution.py:224
  46.7 2.7 %collective-permute-start.10 = (f32[2,72,256]{2,1,0:T(8,128)S(1)}, f32[2,72,256]{2,1,0:T(8,128)S(1)}, u32[]{:S(2)}, u32[]{:S(2)}) collective-permute-start(f32[2,72,256]{2,1,0:T(8,128)S(1)} %pad_maximum_fusion.1), channel_id=1, source_target_pairs={{0,2},{1,3},{2,0},{3,1},{4,6},{5,7},{6,4},{7,5},{8,10},{9,11},{10,... | collective-permute-start | bytes 442376 | tf_op jit(solution)/shard_map/ppermute | solution.py:224
  49.6 1.9 %collective-permute-done.9.back1 = f32[2,72,256]{2,1,0:T(8,128)S(1)} collective-permute-done((f32[2,72,256]{2,1,0:T(8,128)S(1)}, f32[2,72,256]{2,1,0:T(8,128)S(1)}, u32[]{:S(2)}, u32[]{:S(2)}) %collective-permute-start.9) | collective-permute-done | bytes 147488 | tf_op jit(solution)/shard_map/ppermute | solution.py:224
  51.5 1.7 %collective-permute-done.10.back2 = f32[2,72,256]{2,1,0:T(8,128)S(1)} collective-permute-done((f32[2,72,256]{2,1,0:T(8,128)S(1)}, f32[2,72,256]{2,1,0:T(8,128)S(1)}, u32[]{:S(2)}, u32[]{:S(2)}) %collective-permute-start.10) | collective-permute-done | bytes 147488 | tf_op jit(solution)/shard_map/ppermute | solution.py:224
  53.2 3.5 %collective-permute-done.11.back3 = f32[2,72,256]{2,1,0:T(8,128)S(1)} collective-permute-done((f32[2,72,256]{2,1,0:T(8,128)S(1)}, f32[2,72,256]{2,1,0:T(8,128)S(1)}, u32[]{:S(2)}, u32[]{:S(2)}) %collective-permute-start.11) | collective-permute-done | bytes 147488 | tf_op jit(solution)/shard_map/ppermute | solution.py:224
  56.7 1.7 %shard_map.54 = (f32[64,1024]{1,0:T(8,128)}, f32[1,128]{1,0:T(1,128)}) custom-call(s32[1,1024]{1,0:T(1,128)S(1)} %get-tuple-element.15.code, f32[4,72,256]{2,1,0:T(8,128)S(1)} %get-tuple-element.24.mine, f32[4,72,256]{2,1,0:T(8,128)S(1)} %collective-permute-done.8.theirs, f32[2,72,256]{2,1,0:T(8,128)S(1)} %collective-permute-done.9.back1, ...), custom_call_target="tpu_custom_call" | custom-call | tf_op jit(solution)/shard_map/pallas_call | solution.py:185
  (19 shorter events, 1.5 us)
Async XLA Ops:
  0.7 0.8 %copy-start.1 = (bf16[2,224,64]{1,2,0:T(8,128)(2,1)S(1)}, bf16[2,224,64]{1,2,0:T(8,128)(2,1)}, u32[]{:S(2)}) copy-start(bf16[2,224,64]{1,2,0:T(8,128)(2,1)} %param.4) | copy-start | bytes 172036
  1.6 1.2 %copy-start.2 = (s32[1024,1]{0,1:T(1,128)S(1)}, s32[1024,1]{0,1:T(1,128)}, u32[]{:S(2)}) copy-start(s32[1024,1]{0,1:T(1,128)} %param.5) | copy-start | bytes 12292
  2.1 3.9 %collective-permute-start = (bf16[64,256]{1,0:T(8,128)(2,1)S(1)}, bf16[64,256]{1,0:T(8,128)(2,1)S(1)}, u32[]{:S(2)}, u32[]{:S(2)}) collective-permute-start(bf16[64,256]{1,0:T(8,128)(2,1)S(1)} %shard_map.51), channel_id=1, source_target_pairs={{0,0},{1,1},{2,226},{3,227},{4,4},{5,5},{6,230},{7,231},{8,8},{9,9... | collective-permute-start | bytes 98312 | tf_op jit(solution)/shard_map/ppermute | solution.py:236
  2.8 1.0 %copy-start = (bf16[1024,224]{0,1:T(8,128)(2,1)S(1)}, bf16[1024,224]{0,1:T(8,128)(2,1)}, u32[]{:S(2)}) copy-start(bf16[1024,224]{0,1:T(8,128)(2,1)} %param.3) | copy-start | bytes 1376260
  6.9 31.4 %all-to-all-start = ((bf16[16,64,256]{2,1,0:T(8,128)(2,1)}), bf16[16,64,256]{2,1,0:T(8,128)(2,1)S(1)}, u32[]{:S(2)}, u32[]{:S(2)}) async-start(bf16[16,64,256]{2,1,0:T(8,128)(2,1)} %shard_map.52), calls=%async_computation | async-start | bytes 1048576 | tf_op jit(solution)/shard_map/all_to_all | solution.py:207
  16.1 11.9 %collective-permute-start.1 = (bf16[256,256]{1,0:T(8,128)(2,1)S(1)}, bf16[256,256]{1,0:T(8,128)(2,1)S(1)}, u32[]{:S(2)}, u32[]{:S(2)}) collective-permute-start(bf16[256,256]{1,0:T(8,128)(2,1)S(1)} %get-tuple-element.17), channel_id=1, source_target_pairs={{0,1},{1,0},{2,3},{3,2},{4,5},{5,4},{6,7},{7,6},{8,9},{9,8},{10,11... | collective-permute-start | bytes 393224 | tf_op jit(solution)/shard_map/ppermute | solution.py:224
  17.1 11.1 %collective-permute-start.2 = (bf16[256,256]{1,0:T(8,128)(2,1)S(1)}, bf16[256,256]{1,0:T(8,128)(2,1)S(1)}, u32[]{:S(2)}, u32[]{:S(2)}) collective-permute-start(bf16[256,256]{1,0:T(8,128)(2,1)S(1)} %get-tuple-element.18), channel_id=1, source_target_pairs={{0,4},{1,5},{2,6},{3,7},{4,2},{5,3},{6,0},{7,1},{8,12},{9,13},{10,... | collective-permute-start | bytes 393224 | tf_op jit(solution)/shard_map/ppermute | solution.py:224
  18.3 12.9 %collective-permute-start.3 = (bf16[256,256]{1,0:T(8,128)(2,1)S(1)}, bf16[256,256]{1,0:T(8,128)(2,1)S(1)}, u32[]{:S(2)}, u32[]{:S(2)}) collective-permute-start(bf16[256,256]{1,0:T(8,128)(2,1)S(1)} %get-tuple-element.19), channel_id=1, source_target_pairs={{0,5},{1,4},{2,7},{3,6},{4,3},{5,2},{6,1},{7,0},{8,13},{9,12},{10,... | collective-permute-start | bytes 393224 | tf_op jit(solution)/shard_map/ppermute | solution.py:224
  24.6 10.2 %collective-permute-start.4 = (bf16[256,256]{1,0:T(8,128)(2,1)S(1)}, bf16[256,256]{1,0:T(8,128)(2,1)S(1)}, u32[]{:S(2)}, u32[]{:S(2)}) collective-permute-start(bf16[256,256]{1,0:T(8,128)(2,1)S(1)} %get-tuple-element.20), channel_id=1, source_target_pairs={{0,2},{1,3},{2,0},{3,1},{4,6},{5,7},{6,4},{7,5},{8,10},{9,11},{10,... | collective-permute-start | bytes 393224 | tf_op jit(solution)/shard_map/ppermute | solution.py:224
  25.7 12.1 %collective-permute-start.5 = (bf16[256,256]{1,0:T(8,128)(2,1)S(1)}, bf16[256,256]{1,0:T(8,128)(2,1)S(1)}, u32[]{:S(2)}, u32[]{:S(2)}) collective-permute-start(bf16[256,256]{1,0:T(8,128)(2,1)S(1)} %get-tuple-element.21), channel_id=1, source_target_pairs={{0,3},{1,2},{2,1},{3,0},{4,7},{5,6},{6,5},{7,4},{8,11},{9,10},{10,... | collective-permute-start | bytes 393224 | tf_op jit(solution)/shard_map/ppermute | solution.py:224
  27.9 9.9 %collective-permute-start.6 = (bf16[256,256]{1,0:T(8,128)(2,1)S(1)}, bf16[256,256]{1,0:T(8,128)(2,1)S(1)}, u32[]{:S(2)}, u32[]{:S(2)}) collective-permute-start(bf16[256,256]{1,0:T(8,128)(2,1)S(1)} %get-tuple-element.22), channel_id=1, source_target_pairs={{0,6},{1,7},{2,4},{3,5},{4,0},{5,1},{6,2},{7,3},{8,14},{9,15},{10,... | collective-permute-start | bytes 393224 | tf_op jit(solution)/shard_map/ppermute | solution.py:224
  28.2 10.1 %collective-permute-start.7 = (bf16[256,256]{1,0:T(8,128)(2,1)S(1)}, bf16[256,256]{1,0:T(8,128)(2,1)S(1)}, u32[]{:S(2)}, u32[]{:S(2)}) collective-permute-start(bf16[256,256]{1,0:T(8,128)(2,1)S(1)} %get-tuple-element.23), channel_id=1, source_target_pairs={{0,7},{1,6},{2,5},{3,4},{4,1},{5,0},{6,3},{7,2},{8,15},{9,14},{10,... | collective-permute-start | bytes 393224 | tf_op jit(solution)/shard_map/ppermute | solution.py:224
  43.1 1.7 %collective-permute-start.8 = (f32[4,72,256]{2,1,0:T(8,128)S(1)}, f32[4,72,256]{2,1,0:T(8,128)S(1)}, u32[]{:S(2)}, u32[]{:S(2)}) collective-permute-start(f32[4,72,256]{2,1,0:T(8,128)S(1)} %get-tuple-element.25), channel_id=1, source_target_pairs={{0,1},{1,0},{2,3},{3,2},{4,5},{5,4},{6,7},{7,6},{8,9},{9,8},{10,11... | collective-permute-start | bytes 884744 | tf_op jit(solution)/shard_map/ppermute | solution.py:224
  44.8 6.7 %collective-permute-start.9 = (f32[2,72,256]{2,1,0:T(8,128)S(1)}, f32[2,72,256]{2,1,0:T(8,128)S(1)}, u32[]{:S(2)}, u32[]{:S(2)}) collective-permute-start(f32[2,72,256]{2,1,0:T(8,128)S(1)} %pad_maximum_fusion), channel_id=1, source_target_pairs={{0,6},{1,7},{2,4},{3,5},{4,0},{5,1},{6,2},{7,3},{8,14},{9,15},{10,... | collective-permute-start | bytes 442376 | tf_op jit(solution)/shard_map/ppermute | solution.py:224
  46.7 6.5 %collective-permute-start.10 = (f32[2,72,256]{2,1,0:T(8,128)S(1)}, f32[2,72,256]{2,1,0:T(8,128)S(1)}, u32[]{:S(2)}, u32[]{:S(2)}) collective-permute-start(f32[2,72,256]{2,1,0:T(8,128)S(1)} %pad_maximum_fusion.1), channel_id=1, source_target_pairs={{0,2},{1,3},{2,0},{3,1},{4,6},{5,7},{6,4},{7,5},{8,10},{9,11},{10,... | collective-permute-start | bytes 442376 | tf_op jit(solution)/shard_map/ppermute | solution.py:224
  49.5 7.2 %collective-permute-start.11 = (f32[2,72,256]{2,1,0:T(8,128)S(1)}, f32[2,72,256]{2,1,0:T(8,128)S(1)}, u32[]{:S(2)}, u32[]{:S(2)}) collective-permute-start(f32[2,72,256]{2,1,0:T(8,128)S(1)} %pad_maximum_fusion.2), channel_id=1, source_target_pairs={{0,4},{1,5},{2,6},{3,7},{4,2},{5,3},{6,0},{7,1},{8,12},{9,13},{10,... | collective-permute-start | bytes 442376 | tf_op jit(solution)/shard_map/ppermute | solution.py:224

commit v6 on v5

--- a/solution.py
+++ b/solution.py
@@ -35,10 +35,13 @@
     return lax.dot_general(a, b, (((1,), (1,)), ((), ())), preferred_element_type=f32)
 
 
-def prep_kernel(place, bundles, out):
-    width, bands = bundles.shape[1:]
-    out[...] = jnp.where(iota(out.shape, 1) == bands, ROOT, 0.0).astype(bf16)
-    out[:, :bands] = bundles[place[0]]
+def spread_kernel(place, bundles, *rest):
+    out, wide = rest[-2:]
+    bands = bundles.shape[2]
+    wide[...] = jnp.where(iota(wide.shape, 1) == bands, ROOT, 0.0).astype(bf16)
+    wide[:, :bands] = bundles[place[0]]
+    for i in range(out.shape[0]):
+        out[i] = wide[...]
 
 
 def slots_kernel(place, labels, pixels, *rest):
@@ -63,22 +66,22 @@
     handler = (chip - place[3] & 3) * 2 + (label + place[0] & 1)
     local = ((label >> 4 & 3) ^ other * 3) * PACK + (label >> 2 & 3)
     slot = local * CAP + rank
-    held = outs[0].shape[0]
-    for d in range(len(outs)):
+    held = outs[0].shape[1]
+    for d in range(2 * len(outs)):
         key = jnp.where(handler == d, slot, -1)
-        outs[d][...] = dot_nt(one_hot(iota((held, rows), 0) == key), wide[...]).astype(bf16)
+        outs[d // 2][d % 2] = dot_nt(one_hot(iota((held, rows), 0) == key), wide[...]).astype(bf16)
     table_row = handler * (held // PACK) + (local >> 2) * CAP + rank
     code[...] = (local & 3) * 1024 + table_row
 
 
-def repeat_kernel(basis, *rest):
-    out = rest[-1]
-    for i in range(out.shape[0]):
-        out[i] = basis[...]
-
-
-def solve_kernel(place, bundles, *rest, scale):
-    sources, outs = rest[:-9], rest[-9:-7]
+def stack_kernel(*refs):
+    for r, m in enumerate(refs[:-1]):
+        refs[-1][r] = m[1]
+
+
+def solve_kernel(place, bundles, theirs, *rest, scale):
+    sources = [s for r, m in enumerate(rest[:-9]) for s in (m.at[0], theirs.at[r])]
+    outs = rest[-9:-7]
     high, low, goal, state, steps, sums, parts = rest[-7:]
     groups = state.shape[0]
     slots = len(sources) * CAP
@@ -159,11 +162,8 @@
     codes = code[...]
     pick = one_hot(iota((handlers * held, rows), 0) == codes & 1023)
     table = jnp.concatenate([t[:held] for t in tables], axis=0).T
-    first = table.astype(bf16)
-    rest = table - first.astype(f32)
-    second, third = split(rest)
-    found = dot(jnp.concatenate([first, second, third], axis=0), pick)
-    found = found[:lanes] + found[lanes : 2 * lanes] + found[2 * lanes :]
+    found = dot(jnp.concatenate(split(table), axis=0), pick)
+    found = found[:lanes] + found[lanes:]
     which = codes >> 10
     result = found[:wide]
     for i in range(1, PACK):
@@ -232,19 +232,21 @@
     groups = n_col // PACK
     held = n_col * CAP
 
-    basis = call(prep_kernel, place, [bundles.transpose(0, 2, 1)], sds((width, LANES), bf16), [], 4)
-    basis = lax.ppermute(basis, ALL, swap)
+    raw = lax.ppermute(bundles.transpose(0, 2, 1), ALL, swap)
     *sends, code = call(
         slots_kernel,
         place,
         [assign.reshape(1, rows), pixels.T],
-        (sds((held, LANES), bf16),) * (2 * chips) + (sds((1, rows), jnp.int32),),
+        (sds((2, held, LANES), bf16),) * chips + (sds((1, rows), jnp.int32),),
         [vmem((LANES, rows), bf16), vmem((1, rows), f32)],
         16,
     )
-    basis = call(repeat_kernel, None, [basis], sds((n_col, width, LANES), bf16), [], 4, [sends[0]])
-    gathered = exchanged(basis, column)
-    received = [moved(send, d // 2, d % 2) for d, send in enumerate(sends)]
+    copies = call(
+        spread_kernel, place, [raw], sds((n_col, width, LANES), bf16), [vmem((width, LANES), bf16)], 4, [sends[0]]
+    )
+    gathered = exchanged(copies, column)
+    received = [moved(send, r, 0) for r, send in enumerate(sends)]
+    theirs = moved(call(stack_kernel, None, received, sds((chips, held, LANES), bf16), [], 8), 0, 1)
 
     below = groups * CAP
     slots = 2 * chips * CAP
@@ -252,7 +254,7 @@
     solved = call(
         lambda *refs: solve_kernel(*refs, scale=scale),
         place,
-        [gathered, *received],
+        [gathered, theirs, *received],
         (sds((chips, below + 8, LANES), f32),) * 2,
         [
             vmem((groups, LANES, LANES), bf16),

time: 58.8 us -> 59.5 us (1.012)
  waiting for transfers between devices: 16.1 us -> 21.3 us
  starting transfers between devices: 29.5 us -> 25.5 us
    ppermute x11 -> x8, waiting for transfers between devices: 16.1 us -> 21.3 us  [moved(): return lax.ppermute(array, ALL, pairs) if r or other else array]
    ppermute x11 -> x8, starting transfers between devices: 19.6 us -> 14.8 us  [moved(): return lax.ppermute(array, ALL, pairs) if r or other else array]
    ppermute x1, starting transfers between devices: 0.66 us -> 1.5 us  [per_device(): raw = lax.ppermute(bundles.transpose(0, 2, 1), ALL, swap)]
    unnamed x6 -> x4, local copies, waits for them, and re-layouts: 1.86 us -> 1.63 us
  transfers between devices with their start and end apart: 13 -> 10, of which waited for: 9 -> 7; matrix products, arithmetic and copies ran while one was open for 0% -> 0% of each run, Pallas kernels for 4% -> 4%
where the time goes in v6:
time: 59.5 us; the launch traced here: 59.1 us
  starting transfers between devices  25.5 us (43%)
  waiting for transfers between devices  21.3 us (36%)
  Pallas kernels  9.88 us (17%)
  local copies, waits for them, and re-layouts  1.66 us (3%)
  between operations  0.7 us (1%)
    ppermute x8, waiting for transfers between devices, moved(): return lax.ppermute(array, ALL, pairs) if r or other else array  21.3 us
    ppermute x8, starting transfers between devices, moved(): return lax.ppermute(array, ALL, pairs) if r or other else array  14.8 us
    pallas_call x5, Pallas kernels, call(): pl.pallas_call(kernel, out_shape=outs, in_specs=[pl.BlockSpec(memory_spac...  9.88 us
    all_to_all x1, starting transfers between devices, exchanged(): lax.all_to_all(array, ALL, 0, 0, tiled=True, axis_index_groups=groups)  9.19 us
    unnamed x4, local copies, waits for them, and re-layouts  1.63 us
    ppermute x1, starting transfers between devices, per_device(): raw = lax.ppermute(bundles.transpose(0, 2, 1), ALL, swap)  1.5 us
  transfers between devices with their start and end apart: 10, of which 7 were waited for; matrix products, arithmetic and copies ran while one was open for 0% of the time, Pallas kernels for 4%

profile of v6, /device:TPU:1, one launch (start us, length us, event | category | flops | bytes accessed | tf_op | source)
XLA Modules:
  0.0 59.1 jit_solution(942484639705159500)
XLA Ops:
  0.6 1.5 %collective-permute-start = (bf16[2,64,224]{2,1,0:T(8,128)(2,1)}, bf16[2,64,224]{2,1,0:T(8,128)(2,1)S(1)}, u32[]{:S(2)}, u32[]{:S(2)}) collective-permute-start(bf16[2,64,224]{2,1,0:T(8,128)(2,1)} %bitcast.11), channel_id=1, source_target_pairs={{0,0},{1,1},{2,226},{3,227},{4,4},{5,5},{6,230},{7,231},{8,8},{9,9... | collective-permute-start | bytes 172040 | tf_op jit(solution)/shard_map/ppermute | solution.py:235
  2.1 0.1 pad_add_fusion.place.refs_0_
  2.2 0.6 %copy-done.1 = s32[1024,1]{0,1:T(1,128)S(1)} copy-done((s32[1024,1]{0,1:T(1,128)S(1)}, s32[1024,1]{0,1:T(1,128)}, u32[]{:S(2)}) %copy-start.1) | copy-done | bytes 4120
  2.8 1.0 %copy-done = bf16[1024,224]{0,1:T(8,128)(2,1)S(1)} copy-done((bf16[1024,224]{0,1:T(8,128)(2,1)S(1)}, bf16[1024,224]{0,1:T(8,128)(2,1)}, u32[]{:S(2)}) %copy-start) | copy-done | bytes 458776
  3.8 2.2 %shard_map.50 = (bf16[2,256,256]{2,1,0:T(8,128)(2,1)S(1)}, bf16[2,256,256]{2,1,0:T(8,128)(2,1)S(1)}, bf16[2,256,256]{2,1,0:T(8,128)(2,1)S(1)}, bf16[2,256,256]{2,1,0:T(8,128)(2,1)S(1)}, s32[1,1024]{1,0:T(1,128)S(1)}) custom-call(s32[4]{0:T(128)S(1)} %pad_add_fusion.place.refs_0_, s32[1,1024]{1,0:T(1,128)S(1)} %bitcast.9, bf16[224,1024]{1,0:T(8,128)(2,1)S(1)} %bitcast.8), custom_call_target="tpu_custom_call" | custom-call | tf_op jit(solution)/shard_map/pallas_call | solution.py:185
  6.0 1.4 %shard_map.51 = bf16[16,64,256]{2,1,0:T(8,128)(2,1)} custom-call(s32[4]{0:T(128)S(1)} %pad_add_fusion.place.refs_0_, bf16[2,64,224]{2,1,0:T(8,128)(2,1)S(1)} %collective-permute-done.bundles, bf16[2,256,256]{2,1,0:T(8,128)(2,1)S(1)} %get-tuple-element.12.rest_0_.refs_0_.refs_3_), custom_call_target="tpu_custom_call" | custom-call | tf_op jit(solution)/shard_map/pallas_call | solution.py:185
  7.4 9.2 %all-to-all-start = ((bf16[16,64,256]{2,1,0:T(8,128)(2,1)}), bf16[16,64,256]{2,1,0:T(8,128)(2,1)S(1)}, u32[]{:S(2)}, u32[]{:S(2)}) async-start(bf16[16,64,256]{2,1,0:T(8,128)(2,1)} %shard_map.51), calls=%async_computation | async-start | bytes 1048576 | tf_op jit(solution)/shard_map/all_to_all | solution.py:207
  16.6 1.3 %collective-permute-start.1 = (bf16[2,256,256]{2,1,0:T(8,128)(2,1)S(1)}, bf16[2,256,256]{2,1,0:T(8,128)(2,1)S(1)}, u32[]{:S(2)}, u32[]{:S(2)}) collective-permute-start(bf16[2,256,256]{2,1,0:T(8,128)(2,1)S(1)} %get-tuple-element.13), channel_id=1, source_target_pairs={{0,4},{1,5},{2,6},{3,7},{4,2},{5,3},{6,0},{7,1},{8,12},{9,13},{10,... | collective-permute-start | bytes 786440 | tf_op jit(solution)/shard_map/ppermute | solution.py:224
  17.9 6.2 %collective-permute-start.2 = (bf16[2,256,256]{2,1,0:T(8,128)(2,1)S(1)}, bf16[2,256,256]{2,1,0:T(8,128)(2,1)S(1)}, u32[]{:S(2)}, u32[]{:S(2)}) collective-permute-start(bf16[2,256,256]{2,1,0:T(8,128)(2,1)S(1)} %get-tuple-element.14), channel_id=1, source_target_pairs={{0,2},{1,3},{2,0},{3,1},{4,6},{5,7},{6,4},{7,5},{8,10},{9,11},{10,... | collective-permute-start | bytes 786440 | tf_op jit(solution)/shard_map/ppermute | solution.py:224
  24.1 1.1 %collective-permute-start.3 = (bf16[2,256,256]{2,1,0:T(8,128)(2,1)S(1)}, bf16[2,256,256]{2,1,0:T(8,128)(2,1)S(1)}, u32[]{:S(2)}, u32[]{:S(2)}) collective-permute-start(bf16[2,256,256]{2,1,0:T(8,128)(2,1)S(1)} %get-tuple-element.15), channel_id=1, source_target_pairs={{0,6},{1,7},{2,4},{3,5},{4,0},{5,1},{6,2},{7,3},{8,14},{9,15},{10,... | collective-permute-start | bytes 786440 | tf_op jit(solution)/shard_map/ppermute | solution.py:224
  25.2 3.1 %collective-permute-done.1.refs_1_.refs_4_ = bf16[2,256,256]{2,1,0:T(8,128)(2,1)S(1)} collective-permute-done((bf16[2,256,256]{2,1,0:T(8,128)(2,1)S(1)}, bf16[2,256,256]{2,1,0:T(8,128)(2,1)S(1)}, u32[]{:S(2)}, u32[]{:S(2)}) %collective-permute-start.1) | collective-permute-done | bytes 262176 | tf_op jit(solution)/shard_map/ppermute | solution.py:224
  28.3 6.5 %collective-permute-done.2.refs_2_.refs_5_ = bf16[2,256,256]{2,1,0:T(8,128)(2,1)S(1)} collective-permute-done((bf16[2,256,256]{2,1,0:T(8,128)(2,1)S(1)}, bf16[2,256,256]{2,1,0:T(8,128)(2,1)S(1)}, u32[]{:S(2)}, u32[]{:S(2)}) %collective-permute-start.2) | collective-permute-done | bytes 262176 | tf_op jit(solution)/shard_map/ppermute | solution.py:224
  34.9 2.2 %collective-permute-start.4 = (bf16[4,256,256]{2,1,0:T(8,128)(2,1)S(1)}, bf16[4,256,256]{2,1,0:T(8,128)(2,1)S(1)}, u32[]{:S(2)}, u32[]{:S(2)}) collective-permute-start(bf16[4,256,256]{2,1,0:T(8,128)(2,1)S(1)} %shard_map.52), channel_id=1, source_target_pairs={{0,1},{1,0},{2,3},{3,2},{4,5},{5,4},{6,7},{7,6},{8,9},{9,8},{10,11... | collective-permute-start | bytes 1572872 | tf_op jit(solution)/shard_map/ppermute | solution.py:224
  37.1 1.5 %collective-permute-done.4.refs_2_ = bf16[4,256,256]{2,1,0:T(8,128)(2,1)S(1)} collective-permute-done((bf16[4,256,256]{2,1,0:T(8,128)(2,1)S(1)}, bf16[4,256,256]{2,1,0:T(8,128)(2,1)S(1)}, u32[]{:S(2)}, u32[]{:S(2)}) %collective-permute-start.4) | collective-permute-done | bytes 524320 | tf_op jit(solution)/shard_map/ppermute | solution.py:224
  38.6 4.8 %shard_map.53 = (f32[4,72,256]{2,1,0:T(8,128)S(1)}, f32[4,72,256]{2,1,0:T(8,128)S(1)}) custom-call(s32[4]{0:T(128)S(1)} %pad_add_fusion.place.refs_0_, bf16[16,64,256]{2,1,0:T(8,128)(2,1)S(1)} %all-to-all-done.refs_1_, bf16[4,256,256]{2,1,0:T(8,128)(2,1)S(1)} %collective-permute-done.4.refs_2_, ...), custom_call_target="tpu_custom_call" | custom-call | tf_op jit(solution)/shard_map/pallas_call | solution.py:185
  43.5 0.5 collective-permute-start.5
  43.9 1.2 %collective-permute-done.5.theirs = f32[4,72,256]{2,1,0:T(8,128)S(1)} collective-permute-done((f32[4,72,256]{2,1,0:T(8,128)S(1)}, f32[4,72,256]{2,1,0:T(8,128)S(1)}, u32[]{:S(2)}, u32[]{:S(2)}) %collective-permute-start.5) | collective-permute-done | bytes 294944 | tf_op jit(solution)/shard_map/ppermute | solution.py:224
  45.2 2.0 %collective-permute-start.6 = (f32[2,72,256]{2,1,0:T(8,128)S(1)}, f32[2,72,256]{2,1,0:T(8,128)S(1)}, u32[]{:S(2)}, u32[]{:S(2)}) collective-permute-start(f32[2,72,256]{2,1,0:T(8,128)S(1)} %pad_maximum_fusion), channel_id=1, source_target_pairs={{0,6},{1,7},{2,4},{3,5},{4,0},{5,1},{6,2},{7,3},{8,14},{9,15},{10,... | collective-permute-start | bytes 442376 | tf_op jit(solution)/shard_map/ppermute | solution.py:224
  47.2 0.9 %collective-permute-start.7 = (f32[2,72,256]{2,1,0:T(8,128)S(1)}, f32[2,72,256]{2,1,0:T(8,128)S(1)}, u32[]{:S(2)}, u32[]{:S(2)}) collective-permute-start(f32[2,72,256]{2,1,0:T(8,128)S(1)} %pad_maximum_fusion.1), channel_id=1, source_target_pairs={{0,2},{1,3},{2,0},{3,1},{4,6},{5,7},{6,4},{7,5},{8,10},{9,11},{10,... | collective-permute-start | bytes 442376 | tf_op jit(solution)/shard_map/ppermute | solution.py:224
  48.1 0.6 collective-permute-start.8
  48.7 1.6 %collective-permute-done.6.back1 = f32[2,72,256]{2,1,0:T(8,128)S(1)} collective-permute-done((f32[2,72,256]{2,1,0:T(8,128)S(1)}, f32[2,72,256]{2,1,0:T(8,128)S(1)}, u32[]{:S(2)}, u32[]{:S(2)}) %collective-permute-start.6) | collective-permute-done | bytes 147488 | tf_op jit(solution)/shard_map/ppermute | solution.py:224
  50.3 3.2 %collective-permute-done.7.back2 = f32[2,72,256]{2,1,0:T(8,128)S(1)} collective-permute-done((f32[2,72,256]{2,1,0:T(8,128)S(1)}, f32[2,72,256]{2,1,0:T(8,128)S(1)}, u32[]{:S(2)}, u32[]{:S(2)}) %collective-permute-start.7) | collective-permute-done | bytes 147488 | tf_op jit(solution)/shard_map/ppermute | solution.py:224
  53.5 4.2 %collective-permute-done.8.back3 = f32[2,72,256]{2,1,0:T(8,128)S(1)} collective-permute-done((f32[2,72,256]{2,1,0:T(8,128)S(1)}, f32[2,72,256]{2,1,0:T(8,128)S(1)}, u32[]{:S(2)}, u32[]{:S(2)}) %collective-permute-start.8) | collective-permute-done | bytes 147488 | tf_op jit(solution)/shard_map/ppermute | solution.py:224
  57.7 1.5 %shard_map.54 = (f32[64,1024]{1,0:T(8,128)}, f32[1,128]{1,0:T(1,128)}) custom-call(s32[1,1024]{1,0:T(1,128)S(1)} %get-tuple-element.11.code, f32[4,72,256]{2,1,0:T(8,128)S(1)} %get-tuple-element.16.mine, f32[4,72,256]{2,1,0:T(8,128)S(1)} %collective-permute-done.5.theirs, f32[2,72,256]{2,1,0:T(8,128)S(1)} %collective-permute-done.6.back1, ...), custom_call_target="tpu_custom_call" | custom-call | tf_op jit(solution)/shard_map/pallas_call | solution.py:185
  (11 shorter events, 0.2 us)
Async XLA Ops:
  0.6 5.4 %collective-permute-start = (bf16[2,64,224]{2,1,0:T(8,128)(2,1)}, bf16[2,64,224]{2,1,0:T(8,128)(2,1)S(1)}, u32[]{:S(2)}, u32[]{:S(2)}) collective-permute-start(bf16[2,64,224]{2,1,0:T(8,128)(2,1)} %bitcast.11), channel_id=1, source_target_pairs={{0,0},{1,1},{2,226},{3,227},{4,4},{5,5},{6,230},{7,231},{8,8},{9,9... | collective-permute-start | bytes 172040 | tf_op jit(solution)/shard_map/ppermute | solution.py:235
  2.1 0.7 %copy-start.1 = (s32[1024,1]{0,1:T(1,128)S(1)}, s32[1024,1]{0,1:T(1,128)}, u32[]{:S(2)}) copy-start(s32[1024,1]{0,1:T(1,128)} %param.5) | copy-start | bytes 12292
  2.8 1.0 %copy-start = (bf16[1024,224]{0,1:T(8,128)(2,1)S(1)}, bf16[1024,224]{0,1:T(8,128)(2,1)}, u32[]{:S(2)}) copy-start(bf16[1024,224]{0,1:T(8,128)(2,1)} %param.3) | copy-start | bytes 1376260
  7.4 31.2 %all-to-all-start = ((bf16[16,64,256]{2,1,0:T(8,128)(2,1)}), bf16[16,64,256]{2,1,0:T(8,128)(2,1)S(1)}, u32[]{:S(2)}, u32[]{:S(2)}) async-start(bf16[16,64,256]{2,1,0:T(8,128)(2,1)} %shard_map.51), calls=%async_computation | async-start | bytes 1048576 | tf_op jit(solution)/shard_map/all_to_all | solution.py:207
  16.6 11.7 %collective-permute-start.1 = (bf16[2,256,256]{2,1,0:T(8,128)(2,1)S(1)}, bf16[2,256,256]{2,1,0:T(8,128)(2,1)S(1)}, u32[]{:S(2)}, u32[]{:S(2)}) collective-permute-start(bf16[2,256,256]{2,1,0:T(8,128)(2,1)S(1)} %get-tuple-element.13), channel_id=1, source_target_pairs={{0,4},{1,5},{2,6},{3,7},{4,2},{5,3},{6,0},{7,1},{8,12},{9,13},{10,... | collective-permute-start | bytes 786440 | tf_op jit(solution)/shard_map/ppermute | solution.py:224
  17.9 16.9 %collective-permute-start.2 = (bf16[2,256,256]{2,1,0:T(8,128)(2,1)S(1)}, bf16[2,256,256]{2,1,0:T(8,128)(2,1)S(1)}, u32[]{:S(2)}, u32[]{:S(2)}) collective-permute-start(bf16[2,256,256]{2,1,0:T(8,128)(2,1)S(1)} %get-tuple-element.14), channel_id=1, source_target_pairs={{0,2},{1,3},{2,0},{3,1},{4,6},{5,7},{6,4},{7,5},{8,10},{9,11},{10,... | collective-permute-start | bytes 786440 | tf_op jit(solution)/shard_map/ppermute | solution.py:224
  24.1 10.8 %collective-permute-start.3 = (bf16[2,256,256]{2,1,0:T(8,128)(2,1)S(1)}, bf16[2,256,256]{2,1,0:T(8,128)(2,1)S(1)}, u32[]{:S(2)}, u32[]{:S(2)}) collective-permute-start(bf16[2,256,256]{2,1,0:T(8,128)(2,1)S(1)} %get-tuple-element.15), channel_id=1, source_target_pairs={{0,6},{1,7},{2,4},{3,5},{4,0},{5,1},{6,2},{7,3},{8,14},{9,15},{10,... | collective-permute-start | bytes 786440 | tf_op jit(solution)/shard_map/ppermute | solution.py:224
  34.9 3.7 %collective-permute-start.4 = (bf16[4,256,256]{2,1,0:T(8,128)(2,1)S(1)}, bf16[4,256,256]{2,1,0:T(8,128)(2,1)S(1)}, u32[]{:S(2)}, u32[]{:S(2)}) collective-permute-start(bf16[4,256,256]{2,1,0:T(8,128)(2,1)S(1)} %shard_map.52), channel_id=1, source_target_pairs={{0,1},{1,0},{2,3},{3,2},{4,5},{5,4},{6,7},{7,6},{8,9},{9,8},{10,11... | collective-permute-start | bytes 1572872 | tf_op jit(solution)/shard_map/ppermute | solution.py:224
  43.5 1.7 %collective-permute-start.5 = (f32[4,72,256]{2,1,0:T(8,128)S(1)}, f32[4,72,256]{2,1,0:T(8,128)S(1)}, u32[]{:S(2)}, u32[]{:S(2)}) collective-permute-start(f32[4,72,256]{2,1,0:T(8,128)S(1)} %get-tuple-element.17), channel_id=1, source_target_pairs={{0,1},{1,0},{2,3},{3,2},{4,5},{5,4},{6,7},{7,6},{8,9},{9,8},{10,11... | collective-permute-start | bytes 884744 | tf_op jit(solution)/shard_map/ppermute | solution.py:224
  45.2 5.1 %collective-permute-start.6 = (f32[2,72,256]{2,1,0:T(8,128)S(1)}, f32[2,72,256]{2,1,0:T(8,128)S(1)}, u32[]{:S(2)}, u32[]{:S(2)}) collective-permute-start(f32[2,72,256]{2,1,0:T(8,128)S(1)} %pad_maximum_fusion), channel_id=1, source_target_pairs={{0,6},{1,7},{2,4},{3,5},{4,0},{5,1},{6,2},{7,3},{8,14},{9,15},{10,... | collective-permute-start | bytes 442376 | tf_op jit(solution)/shard_map/ppermute | solution.py:224
  47.2 6.3 %collective-permute-start.7 = (f32[2,72,256]{2,1,0:T(8,128)S(1)}, f32[2,72,256]{2,1,0:T(8,128)S(1)}, u32[]{:S(2)}, u32[]{:S(2)}) collective-permute-start(f32[2,72,256]{2,1,0:T(8,128)S(1)} %pad_maximum_fusion.1), channel_id=1, source_target_pairs={{0,2},{1,3},{2,0},{3,1},{4,6},{5,7},{6,4},{7,5},{8,10},{9,11},{10,... | collective-permute-start | bytes 442376 | tf_op jit(solution)/shard_map/ppermute | solution.py:224
  48.1 9.6 %collective-permute-start.8 = (f32[2,72,256]{2,1,0:T(8,128)S(1)}, f32[2,72,256]{2,1,0:T(8,128)S(1)}, u32[]{:S(2)}, u32[]{:S(2)}) collective-permute-start(f32[2,72,256]{2,1,0:T(8,128)S(1)} %pad_maximum_fusion.2), channel_id=1, source_target_pairs={{0,4},{1,5},{2,6},{3,7},{4,2},{5,3},{6,0},{7,1},{8,12},{9,13},{10,... | collective-permute-start | bytes 442376 | tf_op jit(solution)/shard_map/ppermute | solution.py:224

commit v7 on v6

--- a/solution.py
+++ b/solution.py
@@ -35,21 +35,31 @@
     return lax.dot_general(a, b, (((1,), (1,)), ((), ())), preferred_element_type=f32)
 
 
-def spread_kernel(place, bundles, *rest):
-    out, wide = rest[-2:]
+def spread_kernel(place, bundles, after, out, piece, wide, sems):
     bands = bundles.shape[2]
+    count = out.shape[0]
+    fetch = pltpu.make_async_copy(bundles.at[place[0]], piece, sems.at[count])
+    fetch.start()
     wide[...] = jnp.where(iota(wide.shape, 1) == bands, ROOT, 0.0).astype(bf16)
-    wide[:, :bands] = bundles[place[0]]
-    for i in range(out.shape[0]):
-        out[i] = wide[...]
-
-
-def slots_kernel(place, labels, pixels, *rest):
-    outs, (code, wide, ranks) = rest[:-3], rest[-3:]
-    bands, rows = pixels.shape
+    fetch.wait()
+    wide[:, :bands] = piece[...]
+    copies = [pltpu.make_async_copy(wide, out.at[i], sems.at[i]) for i in range(count)]
+    for copy in copies:
+        copy.start()
+    for copy in copies:
+        copy.wait()
+
+
+def slots_kernel(place, labels_from, pixels_from, *rest):
+    outs, (code, labels, wide, ranks, sems) = rest[:-5], rest[-5:]
+    bands, rows = pixels_from.shape
     count = rows // (CAP // 2)
-    wide[:bands] = pixels[...]
+    fetch = pltpu.make_async_copy(labels_from, labels, sems.at[0])
+    fetch.start()
+    pixels = pltpu.make_async_copy(pixels_from, wide.at[:bands], sems.at[1])
+    pixels.start()
     wide[bands:] = jnp.where(iota((LANES - bands, rows), 0) == 0, ROOT, 0.0).astype(bf16)
+    fetch.wait()
     label = labels[...]
     chunk = 256
     upper = one_hot(iota((chunk, chunk), 0) <= iota((chunk, chunk), 1))
@@ -67,6 +77,7 @@
     local = ((label >> 4 & 3) ^ other * 3) * PACK + (label >> 2 & 3)
     slot = local * CAP + rank
     held = outs[0].shape[1]
+    pixels.wait()
     for d in range(2 * len(outs)):
         key = jnp.where(handler == d, slot, -1)
         outs[d // 2][d % 2] = dot_nt(one_hot(iota((held, rows), 0) == key), wide[...]).astype(bf16)
@@ -79,38 +90,49 @@
         refs[-1][r] = m[1]
 
 
-def solve_kernel(place, bundles, theirs, *rest, scale):
-    sources = [s for r, m in enumerate(rest[:-9]) for s in (m.at[0], theirs.at[r])]
-    outs = rest[-9:-7]
-    high, low, goal, state, steps, sums, parts = rest[-7:]
-    groups = state.shape[0]
-    slots = len(sources) * CAP
+def blocks():
+    return iota((1, LANES), 1) // (LANES // PACK)
+
+
+def basis_of(bundles, g):
+    return jnp.concatenate([bundles[PACK * g + i] for i in range(PACK)], axis=0)
+
+
+def gram_kernel(bundles, high, low, steps, sums):
+    groups = high.shape[0]
     wide = LANES // PACK
-    block = iota((1, LANES), 1) // wide
+    block = blocks()
     same = iota((LANES, LANES), 0) // wide == iota((LANES, LANES), 1) // wide
-
-    def basis_of(g):
-        return jnp.concatenate([bundles[PACK * g + i] for i in range(PACK)], axis=0)
-
-    def pixels_of(local):
-        return jnp.concatenate([s[local * CAP : (local + 1) * CAP] for s in sources], axis=0)
-
     for g in range(groups):
-        basis = basis_of(g)
+        basis = basis_of(bundles, g)
         gram = jnp.where(same, dot_nt(basis, basis), 0.0)
         sums[g : g + 1] = jnp.sum(jnp.abs(gram), axis=0, keepdims=True)
         high[g], low[g] = split(gram)
-        found = dot_nt(jnp.concatenate([pixels_of(PACK * g + i) for i in range(PACK)], axis=0), basis)
-        aim = found[:slots]
-        for i in range(1, PACK):
-            aim = jnp.where(block == i, found[i * slots : (i + 1) * slots], aim)
-        goal[g] = aim
     total = sums[...]
     largest = jnp.zeros_like(total)
     for i in range(PACK):
         inside = block == i
         largest = jnp.where(inside, jnp.max(jnp.where(inside, total, 0.0), axis=1, keepdims=True), largest)
     steps[...] = 1.0 / largest
+
+
+def solve_kernel(place, bundles, high, low, steps, theirs, *rest, scale):
+    sources = [s for r, m in enumerate(rest[:-5]) for s in (m.at[0], theirs.at[r])]
+    outs = rest[-5:-3]
+    goal, state, parts = rest[-3:]
+    groups = state.shape[0]
+    slots = len(sources) * CAP
+    block = blocks()
+
+    def pixels_of(local):
+        return jnp.concatenate([s[local * CAP : (local + 1) * CAP] for s in sources], axis=0)
+
+    for g in range(groups):
+        found = dot_nt(jnp.concatenate([pixels_of(PACK * g + i) for i in range(PACK)], axis=0), basis_of(bundles, g))
+        aim = found[:slots]
+        for i in range(1, PACK):
+            aim = jnp.where(block == i, found[i * slots : (i + 1) * slots], aim)
+        goal[g] = aim
     for g in range(groups):
         state[g] = jnp.maximum(steps[g : g + 1] * goal[g], 0.0)
 
@@ -130,7 +152,7 @@
         for s in range(len(sources)):
             outs[s % 2][s // 2, g * CAP : (g + 1) * CAP] = a[s * CAP : (s + 1) * CAP]
         spread = jnp.concatenate([jnp.where(block == i, a, 0.0) for i in range(PACK)], axis=0)
-        both = dot(jnp.concatenate(split(spread), axis=0), basis_of(g))
+        both = dot(jnp.concatenate(split(spread), axis=0), basis_of(bundles, g))
         fitted = both[: PACK * slots] + both[PACK * slots :]
         for i in range(PACK):
             misfit = pixels_of(PACK * g + i).astype(f32) - fitted[i * slots : (i + 1) * slots]
@@ -179,17 +201,21 @@
     return pltpu.VMEM(shape, dtype)
 
 
-def call(kernel, place, args, outs, scratch, limit, after=()):
-    spec = pl.BlockSpec(memory_space=pltpu.VMEM)
+def call(kernel, place, args, outs, scratch, limit, after=(), stays=(), out_stays=False):
+    spec, lies = pl.BlockSpec(memory_space=pltpu.VMEM), pl.BlockSpec(memory_space=pl.ANY)
+    far = pl.BlockSpec(memory_space=pltpu.HBM)
     head = [] if place is None else [place]
     return pl.pallas_call(
         kernel,
         out_shape=outs,
-        in_specs=[pl.BlockSpec(memory_space=pltpu.SMEM)] * len(head) + [spec] * len(args) + [pl.BlockSpec(memory_space=pl.ANY)] * len(after),
-        out_specs=jax.tree.map(lambda _: spec, outs),
+        in_specs=[pl.BlockSpec(memory_space=pltpu.SMEM)] * len(head)
+        + [spec] * len(args)
+        + [far] * len(stays)
+        + [lies] * len(after),
+        out_specs=jax.tree.map(lambda _: far if out_stays else spec, outs),
         scratch_shapes=scratch,
         compiler_params=pltpu.CompilerParams(vmem_limit_bytes=limit << 20),
-    )(*head, *args, *after)
+    )(*head, *args, *stays, *after)
 
 
 def spots_of(n_blk, n_pix):
@@ -236,13 +262,22 @@
     *sends, code = call(
         slots_kernel,
         place,
-        [assign.reshape(1, rows), pixels.T],
+        [],
         (sds((2, held, LANES), bf16),) * chips + (sds((1, rows), jnp.int32),),
-        [vmem((LANES, rows), bf16), vmem((1, rows), f32)],
+        [vmem((1, rows), jnp.int32), vmem((LANES, rows), bf16), vmem((1, rows), f32), pltpu.SemaphoreType.DMA((2,))],
         16,
+        stays=[assign.reshape(1, rows), pixels.T],
     )
     copies = call(
-        spread_kernel, place, [raw], sds((n_col, width, LANES), bf16), [vmem((width, LANES), bf16)], 4, [sends[0]]
+        spread_kernel,
+        place,
+        [],
+        sds((n_col, width, LANES), bf16),
+        [vmem((width, bands), bf16), vmem((width, LANES), bf16), pltpu.SemaphoreType.DMA((n_col + 1,))],
+        4,
+        stays=[raw],
+        after=[sends[0]],
+        out_stays=True,
     )
     gathered = exchanged(copies, column)
     received = [moved(send, r, 0) for r, send in enumerate(sends)]
@@ -251,18 +286,23 @@
     below = groups * CAP
     slots = 2 * chips * CAP
     scale = bands * rows * n_pix / count
+    square = sds((groups, LANES, LANES), bf16)
+    grams = call(
+        gram_kernel,
+        None,
+        [gathered],
+        (square, square, sds((groups, LANES), f32)),
+        [vmem((groups, LANES), f32)],
+        16,
+    )
     solved = call(
         lambda *refs: solve_kernel(*refs, scale=scale),
         place,
-        [gathered, theirs, *received],
+        [gathered, *grams, theirs, *received],
         (sds((chips, below + 8, LANES), f32),) * 2,
         [
-            vmem((groups, LANES, LANES), bf16),
-            vmem((groups, LANES, LANES), bf16),
             vmem((groups, slots, LANES), f32),
             vmem((groups, slots, LANES), f32),
-            vmem((groups, LANES), f32),
-            vmem((groups, LANES), f32),
             vmem((2, count, LANES), f32),
         ],
         16,

time: 59.5 us -> 60 us (level)
  Pallas kernels: 9.88 us -> 10.9 us
    pallas_call x5 -> x6, Pallas kernels: 9.88 us -> 10.9 us  [call(): pl.pallas_call(kernel, out_shape=outs, in_specs=[pl.BlockSpec(memory_spac...]
  transfers between devices with their start and end apart: 10 -> 10, of which waited for: 7 -> 7; matrix products, arithmetic and copies ran while one was open for 0% -> 0% of each run, Pallas kernels for 4% -> 5%
where the time goes in v7:
time: 60 us; the launch traced here: 59.6 us
  starting transfers between devices  25.5 us (42%)
  waiting for transfers between devices  20.8 us (35%)
  Pallas kernels  10.9 us (18%)
  local copies, waits for them, and re-layouts  1.66 us (3%)
  between operations  0.7 us (1%)
    ppermute x8, waiting for transfers between devices, moved(): return lax.ppermute(array, ALL, pairs) if r or other else array  20.8 us
    ppermute x8, starting transfers between devices, moved(): return lax.ppermute(array, ALL, pairs) if r or other else array  14.8 us
    pallas_call x6, Pallas kernels, call(): pl.pallas_call(kernel, out_shape=outs, in_specs=[pl.BlockSpec(memory_spac...  10.9 us
    all_to_all x1, starting transfers between devices, exchanged(): lax.all_to_all(array, ALL, 0, 0, tiled=True, axis_index_groups=groups)  9.2 us
    unnamed x4, local copies, waits for them, and re-layouts  1.63 us
    ppermute x1, starting transfers between devices, per_device(): raw = lax.ppermute(bundles.transpose(0, 2, 1), ALL, swap)  1.5 us
  transfers between devices with their start and end apart: 10, of which 7 were waited for; matrix products, arithmetic and copies ran while one was open for 0% of the time, Pallas kernels for 5%

profile of v7, /device:TPU:1, one launch (start us, length us, event | category | flops | bytes accessed | tf_op | source)
XLA Modules:
  0.0 59.6 jit_solution(12036340410771942315)
XLA Ops:
  0.6 1.5 %collective-permute-start = (bf16[2,64,224]{2,1,0:T(8,128)(2,1)}, bf16[2,64,224]{2,1,0:T(8,128)(2,1)S(1)}, u32[]{:S(2)}, u32[]{:S(2)}) collective-permute-start(bf16[2,64,224]{2,1,0:T(8,128)(2,1)} %bitcast.11), channel_id=1, source_target_pairs={{0,0},{1,1},{2,226},{3,227},{4,4},{5,5},{6,230},{7,231},{8,8},{9,9... | collective-permute-start | bytes 172040 | tf_op jit(solution)/shard_map/ppermute | solution.py:261
  2.2 0.6 %copy-done.1 = s32[1024,1]{0,1:T(1,128)S(1)} copy-done((s32[1024,1]{0,1:T(1,128)S(1)}, s32[1024,1]{0,1:T(1,128)}, u32[]{:S(2)}) %copy-start.1) | copy-done | bytes 4120
  2.8 1.0 %copy-done = bf16[1024,224]{0,1:T(8,128)(2,1)S(1)} copy-done((bf16[1024,224]{0,1:T(8,128)(2,1)S(1)}, bf16[1024,224]{0,1:T(8,128)(2,1)}, u32[]{:S(2)}) %copy-start) | copy-done | bytes 458776
  3.8 2.5 %shard_map.50 = (bf16[2,256,256]{2,1,0:T(8,128)(2,1)S(1)}, bf16[2,256,256]{2,1,0:T(8,128)(2,1)S(1)}, bf16[2,256,256]{2,1,0:T(8,128)(2,1)S(1)}, bf16[2,256,256]{2,1,0:T(8,128)(2,1)S(1)}, s32[1,1024]{1,0:T(1,128)S(1)}) custom-call(s32[4]{0:T(128)S(1)} %pad_add_fusion.place.refs_0_, s32[1,1024]{1,0:T(1,128)S(1)} %bitcast.9, bf16[224,1024]{1,0:T(8,128)(2,1)S(1)} %bitcast.8), custom_call_target="tpu_custom_call" | custom-call | tf_op jit(solution)/shard_map/pallas_call | solution.py:208
  6.4 1.6 %shard_map.51 = bf16[16,64,256]{2,1,0:T(8,128)(2,1)} custom-call(s32[4]{0:T(128)S(1)} %pad_add_fusion.place.refs_0_, bf16[2,64,224]{2,1,0:T(8,128)(2,1)S(1)} %collective-permute-done.bundles, bf16[2,256,256]{2,1,0:T(8,128)(2,1)S(1)} %get-tuple-element.15.after.refs_0_.refs_6_), custom_call_target="tpu_custom_call" | custom-call | tf_op jit(solution)/shard_map/pallas_call | solution.py:208
  8.0 9.2 %all-to-all-start = ((bf16[16,64,256]{2,1,0:T(8,128)(2,1)}), bf16[16,64,256]{2,1,0:T(8,128)(2,1)S(1)}, u32[]{:S(2)}, u32[]{:S(2)}) async-start(bf16[16,64,256]{2,1,0:T(8,128)(2,1)} %shard_map.51), calls=%async_computation | async-start | bytes 1048576 | tf_op jit(solution)/shard_map/all_to_all | solution.py:233
  17.2 1.3 %collective-permute-start.1 = (bf16[2,256,256]{2,1,0:T(8,128)(2,1)S(1)}, bf16[2,256,256]{2,1,0:T(8,128)(2,1)S(1)}, u32[]{:S(2)}, u32[]{:S(2)}) collective-permute-start(bf16[2,256,256]{2,1,0:T(8,128)(2,1)S(1)} %get-tuple-element.19), channel_id=1, source_target_pairs={{0,4},{1,5},{2,6},{3,7},{4,2},{5,3},{6,0},{7,1},{8,12},{9,13},{10,... | collective-permute-start | bytes 786440 | tf_op jit(solution)/shard_map/ppermute | solution.py:250
  18.5 6.2 %collective-permute-start.2 = (bf16[2,256,256]{2,1,0:T(8,128)(2,1)S(1)}, bf16[2,256,256]{2,1,0:T(8,128)(2,1)S(1)}, u32[]{:S(2)}, u32[]{:S(2)}) collective-permute-start(bf16[2,256,256]{2,1,0:T(8,128)(2,1)S(1)} %get-tuple-element.20), channel_id=1, source_target_pairs={{0,2},{1,3},{2,0},{3,1},{4,6},{5,7},{6,4},{7,5},{8,10},{9,11},{10,... | collective-permute-start | bytes 786440 | tf_op jit(solution)/shard_map/ppermute | solution.py:250
  24.6 1.2 %collective-permute-start.3 = (bf16[2,256,256]{2,1,0:T(8,128)(2,1)S(1)}, bf16[2,256,256]{2,1,0:T(8,128)(2,1)S(1)}, u32[]{:S(2)}, u32[]{:S(2)}) collective-permute-start(bf16[2,256,256]{2,1,0:T(8,128)(2,1)S(1)} %get-tuple-element.21), channel_id=1, source_target_pairs={{0,6},{1,7},{2,4},{3,5},{4,0},{5,1},{6,2},{7,3},{8,14},{9,15},{10,... | collective-permute-start | bytes 786440 | tf_op jit(solution)/shard_map/ppermute | solution.py:250
  25.8 3.1 %collective-permute-done.1.refs_1_.refs_7_ = bf16[2,256,256]{2,1,0:T(8,128)(2,1)S(1)} collective-permute-done((bf16[2,256,256]{2,1,0:T(8,128)(2,1)S(1)}, bf16[2,256,256]{2,1,0:T(8,128)(2,1)S(1)}, u32[]{:S(2)}, u32[]{:S(2)}) %collective-permute-start.1) | collective-permute-done | bytes 262176 | tf_op jit(solution)/shard_map/ppermute | solution.py:250
  28.9 6.5 %collective-permute-done.2.refs_2_.refs_8_ = bf16[2,256,256]{2,1,0:T(8,128)(2,1)S(1)} collective-permute-done((bf16[2,256,256]{2,1,0:T(8,128)(2,1)S(1)}, bf16[2,256,256]{2,1,0:T(8,128)(2,1)S(1)}, u32[]{:S(2)}, u32[]{:S(2)}) %collective-permute-start.2) | collective-permute-done | bytes 262176 | tf_op jit(solution)/shard_map/ppermute | solution.py:250
  35.4 2.2 %collective-permute-start.4 = (bf16[4,256,256]{2,1,0:T(8,128)(2,1)S(1)}, bf16[4,256,256]{2,1,0:T(8,128)(2,1)S(1)}, u32[]{:S(2)}, u32[]{:S(2)}) collective-permute-start(bf16[4,256,256]{2,1,0:T(8,128)(2,1)S(1)} %shard_map.53), channel_id=1, source_target_pairs={{0,1},{1,0},{2,3},{3,2},{4,5},{5,4},{6,7},{7,6},{8,9},{9,8},{10,11... | collective-permute-start | bytes 1572872 | tf_op jit(solution)/shard_map/ppermute | solution.py:250
  37.6 0.5 shard_map.52
  38.1 1.0 %collective-permute-done.4.refs_5_ = bf16[4,256,256]{2,1,0:T(8,128)(2,1)S(1)} collective-permute-done((bf16[4,256,256]{2,1,0:T(8,128)(2,1)S(1)}, bf16[4,256,256]{2,1,0:T(8,128)(2,1)S(1)}, u32[]{:S(2)}, u32[]{:S(2)}) %collective-permute-start.4) | collective-permute-done | bytes 524320 | tf_op jit(solution)/shard_map/ppermute | solution.py:250
  39.2 4.8 %shard_map.54 = (f32[4,72,256]{2,1,0:T(8,128)S(1)}, f32[4,72,256]{2,1,0:T(8,128)S(1)}) custom-call(s32[4]{0:T(128)S(1)} %pad_add_fusion.place.refs_0_, bf16[16,64,256]{2,1,0:T(8,128)(2,1)S(1)} %all-to-all-done.bundles.refs_1_, bf16[4,256,256]{2,1,0:T(8,128)(2,1)S(1)} %get-tuple-element.16.refs_2_, bf16[4,256,256]{2,1,0:T(8,128)(2,1)S(1)} %get-tuple-element.17.refs_3_, ...), custom_call_target="tpu_custom_call" | custom-call | tf_op jit(solution)/shard_map/pallas_call | solution.py:208
  44.0 0.5 collective-permute-start.5
  44.5 1.2 %collective-permute-done.5.theirs = f32[4,72,256]{2,1,0:T(8,128)S(1)} collective-permute-done((f32[4,72,256]{2,1,0:T(8,128)S(1)}, f32[4,72,256]{2,1,0:T(8,128)S(1)}, u32[]{:S(2)}, u32[]{:S(2)}) %collective-permute-start.5) | collective-permute-done | bytes 294944 | tf_op jit(solution)/shard_map/ppermute | solution.py:250
  45.7 2.0 %collective-permute-start.6 = (f32[2,72,256]{2,1,0:T(8,128)S(1)}, f32[2,72,256]{2,1,0:T(8,128)S(1)}, u32[]{:S(2)}, u32[]{:S(2)}) collective-permute-start(f32[2,72,256]{2,1,0:T(8,128)S(1)} %pad_maximum_fusion), channel_id=1, source_target_pairs={{0,6},{1,7},{2,4},{3,5},{4,0},{5,1},{6,2},{7,3},{8,14},{9,15},{10,... | collective-permute-start | bytes 442376 | tf_op jit(solution)/shard_map/ppermute | solution.py:250
  47.7 0.9 %collective-permute-start.7 = (f32[2,72,256]{2,1,0:T(8,128)S(1)}, f32[2,72,256]{2,1,0:T(8,128)S(1)}, u32[]{:S(2)}, u32[]{:S(2)}) collective-permute-start(f32[2,72,256]{2,1,0:T(8,128)S(1)} %pad_maximum_fusion.1), channel_id=1, source_target_pairs={{0,2},{1,3},{2,0},{3,1},{4,6},{5,7},{6,4},{7,5},{8,10},{9,11},{10,... | collective-permute-start | bytes 442376 | tf_op jit(solution)/shard_map/ppermute | solution.py:250
  48.6 0.6 collective-permute-start.8
  49.2 1.6 %collective-permute-done.6.back1 = f32[2,72,256]{2,1,0:T(8,128)S(1)} collective-permute-done((f32[2,72,256]{2,1,0:T(8,128)S(1)}, f32[2,72,256]{2,1,0:T(8,128)S(1)}, u32[]{:S(2)}, u32[]{:S(2)}) %collective-permute-start.6) | collective-permute-done | bytes 147488 | tf_op jit(solution)/shard_map/ppermute | solution.py:250
  50.8 3.2 %collective-permute-done.7.back2 = f32[2,72,256]{2,1,0:T(8,128)S(1)} collective-permute-done((f32[2,72,256]{2,1,0:T(8,128)S(1)}, f32[2,72,256]{2,1,0:T(8,128)S(1)}, u32[]{:S(2)}, u32[]{:S(2)}) %collective-permute-start.7) | collective-permute-done | bytes 147488 | tf_op jit(solution)/shard_map/ppermute | solution.py:250
  54.0 4.2 %collective-permute-done.8.back3 = f32[2,72,256]{2,1,0:T(8,128)S(1)} collective-permute-done((f32[2,72,256]{2,1,0:T(8,128)S(1)}, f32[2,72,256]{2,1,0:T(8,128)S(1)}, u32[]{:S(2)}, u32[]{:S(2)}) %collective-permute-start.8) | collective-permute-done | bytes 147488 | tf_op jit(solution)/shard_map/ppermute | solution.py:250
  58.2 1.5 %shard_map.55 = (f32[64,1024]{1,0:T(8,128)}, f32[1,128]{1,0:T(1,128)}) custom-call(s32[1,1024]{1,0:T(1,128)S(1)} %get-tuple-element.14.code, f32[4,72,256]{2,1,0:T(8,128)S(1)} %get-tuple-element.22.mine, f32[4,72,256]{2,1,0:T(8,128)S(1)} %collective-permute-done.5.theirs, f32[2,72,256]{2,1,0:T(8,128)S(1)} %collective-permute-done.6.back1, ...), custom_call_target="tpu_custom_call" | custom-call | tf_op jit(solution)/shard_map/pallas_call | solution.py:208
  (12 shorter events, 0.2 us)
Async XLA Ops:
  0.6 5.8 %collective-permute-start = (bf16[2,64,224]{2,1,0:T(8,128)(2,1)}, bf16[2,64,224]{2,1,0:T(8,128)(2,1)S(1)}, u32[]{:S(2)}, u32[]{:S(2)}) collective-permute-start(bf16[2,64,224]{2,1,0:T(8,128)(2,1)} %bitcast.11), channel_id=1, source_target_pairs={{0,0},{1,1},{2,226},{3,227},{4,4},{5,5},{6,230},{7,231},{8,8},{9,9... | collective-permute-start | bytes 172040 | tf_op jit(solution)/shard_map/ppermute | solution.py:261
  2.1 0.7 %copy-start.1 = (s32[1024,1]{0,1:T(1,128)S(1)}, s32[1024,1]{0,1:T(1,128)}, u32[]{:S(2)}) copy-start(s32[1024,1]{0,1:T(1,128)} %param.5) | copy-start | bytes 12292
  2.8 1.0 %copy-start = (bf16[1024,224]{0,1:T(8,128)(2,1)S(1)}, bf16[1024,224]{0,1:T(8,128)(2,1)}, u32[]{:S(2)}) copy-start(bf16[1024,224]{0,1:T(8,128)(2,1)} %param.3) | copy-start | bytes 1376260
  8.0 29.7 %all-to-all-start = ((bf16[16,64,256]{2,1,0:T(8,128)(2,1)}), bf16[16,64,256]{2,1,0:T(8,128)(2,1)S(1)}, u32[]{:S(2)}, u32[]{:S(2)}) async-start(bf16[16,64,256]{2,1,0:T(8,128)(2,1)} %shard_map.51), calls=%async_computation | async-start | bytes 1048576 | tf_op jit(solution)/shard_map/all_to_all | solution.py:233
  17.2 11.7 %collective-permute-start.1 = (bf16[2,256,256]{2,1,0:T(8,128)(2,1)S(1)}, bf16[2,256,256]{2,1,0:T(8,128)(2,1)S(1)}, u32[]{:S(2)}, u32[]{:S(2)}) collective-permute-start(bf16[2,256,256]{2,1,0:T(8,128)(2,1)S(1)} %get-tuple-element.19), channel_id=1, source_target_pairs={{0,4},{1,5},{2,6},{3,7},{4,2},{5,3},{6,0},{7,1},{8,12},{9,13},{10,... | collective-permute-start | bytes 786440 | tf_op jit(solution)/shard_map/ppermute | solution.py:250
  18.5 16.9 %collective-permute-start.2 = (bf16[2,256,256]{2,1,0:T(8,128)(2,1)S(1)}, bf16[2,256,256]{2,1,0:T(8,128)(2,1)S(1)}, u32[]{:S(2)}, u32[]{:S(2)}) collective-permute-start(bf16[2,256,256]{2,1,0:T(8,128)(2,1)S(1)} %get-tuple-element.20), channel_id=1, source_target_pairs={{0,2},{1,3},{2,0},{3,1},{4,6},{5,7},{6,4},{7,5},{8,10},{9,11},{10,... | collective-permute-start | bytes 786440 | tf_op jit(solution)/shard_map/ppermute | solution.py:250
  24.6 10.8 %collective-permute-start.3 = (bf16[2,256,256]{2,1,0:T(8,128)(2,1)S(1)}, bf16[2,256,256]{2,1,0:T(8,128)(2,1)S(1)}, u32[]{:S(2)}, u32[]{:S(2)}) collective-permute-start(bf16[2,256,256]{2,1,0:T(8,128)(2,1)S(1)} %get-tuple-element.21), channel_id=1, source_target_pairs={{0,6},{1,7},{2,4},{3,5},{4,0},{5,1},{6,2},{7,3},{8,14},{9,15},{10,... | collective-permute-start | bytes 786440 | tf_op jit(solution)/shard_map/ppermute | solution.py:250
  35.4 3.7 %collective-permute-start.4 = (bf16[4,256,256]{2,1,0:T(8,128)(2,1)S(1)}, bf16[4,256,256]{2,1,0:T(8,128)(2,1)S(1)}, u32[]{:S(2)}, u32[]{:S(2)}) collective-permute-start(bf16[4,256,256]{2,1,0:T(8,128)(2,1)S(1)} %shard_map.53), channel_id=1, source_target_pairs={{0,1},{1,0},{2,3},{3,2},{4,5},{5,4},{6,7},{7,6},{8,9},{9,8},{10,11... | collective-permute-start | bytes 1572872 | tf_op jit(solution)/shard_map/ppermute | solution.py:250
  44.0 1.7 %collective-permute-start.5 = (f32[4,72,256]{2,1,0:T(8,128)S(1)}, f32[4,72,256]{2,1,0:T(8,128)S(1)}, u32[]{:S(2)}, u32[]{:S(2)}) collective-permute-start(f32[4,72,256]{2,1,0:T(8,128)S(1)} %get-tuple-element.23), channel_id=1, source_target_pairs={{0,1},{1,0},{2,3},{3,2},{4,5},{5,4},{6,7},{7,6},{8,9},{9,8},{10,11... | collective-permute-start | bytes 884744 | tf_op jit(solution)/shard_map/ppermute | solution.py:250
  45.7 5.1 %collective-permute-start.6 = (f32[2,72,256]{2,1,0:T(8,128)S(1)}, f32[2,72,256]{2,1,0:T(8,128)S(1)}, u32[]{:S(2)}, u32[]{:S(2)}) collective-permute-start(f32[2,72,256]{2,1,0:T(8,128)S(1)} %pad_maximum_fusion), channel_id=1, source_target_pairs={{0,6},{1,7},{2,4},{3,5},{4,0},{5,1},{6,2},{7,3},{8,14},{9,15},{10,... | collective-permute-start | bytes 442376 | tf_op jit(solution)/shard_map/ppermute | solution.py:250
  47.7 6.3 %collective-permute-start.7 = (f32[2,72,256]{2,1,0:T(8,128)S(1)}, f32[2,72,256]{2,1,0:T(8,128)S(1)}, u32[]{:S(2)}, u32[]{:S(2)}) collective-permute-start(f32[2,72,256]{2,1,0:T(8,128)S(1)} %pad_maximum_fusion.1), channel_id=1, source_target_pairs={{0,2},{1,3},{2,0},{3,1},{4,6},{5,7},{6,4},{7,5},{8,10},{9,11},{10,... | collective-permute-start | bytes 442376 | tf_op jit(solution)/shard_map/ppermute | solution.py:250
  48.6 9.6 %collective-permute-start.8 = (f32[2,72,256]{2,1,0:T(8,128)S(1)}, f32[2,72,256]{2,1,0:T(8,128)S(1)}, u32[]{:S(2)}, u32[]{:S(2)}) collective-permute-start(f32[2,72,256]{2,1,0:T(8,128)S(1)} %pad_maximum_fusion.2), channel_id=1, source_target_pairs={{0,4},{1,5},{2,6},{3,7},{4,2},{5,3},{6,0},{7,1},{8,12},{9,13},{10,... | collective-permute-start | bytes 442376 | tf_op jit(solution)/shard_map/ppermute | solution.py:250

commit v8 on v7

--- a/solution.py
+++ b/solution.py
@@ -35,31 +35,19 @@
     return lax.dot_general(a, b, (((1,), (1,)), ((), ())), preferred_element_type=f32)
 
 
-def spread_kernel(place, bundles, after, out, piece, wide, sems):
+def prep_kernel(place, bundles, *rest):
+    out = rest[-1]
     bands = bundles.shape[2]
-    count = out.shape[0]
-    fetch = pltpu.make_async_copy(bundles.at[place[0]], piece, sems.at[count])
-    fetch.start()
-    wide[...] = jnp.where(iota(wide.shape, 1) == bands, ROOT, 0.0).astype(bf16)
-    fetch.wait()
-    wide[:, :bands] = piece[...]
-    copies = [pltpu.make_async_copy(wide, out.at[i], sems.at[i]) for i in range(count)]
-    for copy in copies:
-        copy.start()
-    for copy in copies:
-        copy.wait()
-
-
-def slots_kernel(place, labels_from, pixels_from, *rest):
-    outs, (code, labels, wide, ranks, sems) = rest[:-5], rest[-5:]
-    bands, rows = pixels_from.shape
+    out[...] = jnp.where(iota(out.shape, 1) == bands, ROOT, 0.0).astype(bf16)
+    out[:, :bands] = bundles[place[0]]
+
+
+def slots_kernel(place, labels, pixels, *rest):
+    outs, (code, wide, ranks) = rest[:-3], rest[-3:]
+    bands, rows = pixels.shape
     count = rows // (CAP // 2)
-    fetch = pltpu.make_async_copy(labels_from, labels, sems.at[0])
-    fetch.start()
-    pixels = pltpu.make_async_copy(pixels_from, wide.at[:bands], sems.at[1])
-    pixels.start()
+    wide[:bands] = pixels[...]
     wide[bands:] = jnp.where(iota((LANES - bands, rows), 0) == 0, ROOT, 0.0).astype(bf16)
-    fetch.wait()
     label = labels[...]
     chunk = 256
     upper = one_hot(iota((chunk, chunk), 0) <= iota((chunk, chunk), 1))
@@ -71,13 +59,12 @@
         ranks[:, part] = jnp.sum(named * running, axis=0, keepdims=True) - 1.0
         carry = running[:, chunk - 1 :]
     rank = ranks[...].astype(jnp.int32)
-    other = (label >> 6) ^ place[2]
+    other = (label >> 6) ^ (place[2] >> 2)
     chip = other * 2 + (label >> 1 & 1)
     handler = (chip - place[3] & 3) * 2 + (label + place[0] & 1)
-    local = ((label >> 4 & 3) ^ other * 3) * PACK + (label >> 2 & 3)
+    local = (place[2] - ((label >> 4) ^ other * 3) & 3) * PACK + (place[4] - (label >> 2) & 3)
     slot = local * CAP + rank
     held = outs[0].shape[1]
-    pixels.wait()
     for d in range(2 * len(outs)):
         key = jnp.where(handler == d, slot, -1)
         outs[d // 2][d % 2] = dot_nt(one_hot(iota((held, rows), 0) == key), wide[...]).astype(bf16)
@@ -86,7 +73,7 @@
 
 
 def stack_kernel(*refs):
-    for r, m in enumerate(refs[:-1]):
+    for r, m in enumerate(refs[: refs[-1].shape[0]]):
         refs[-1][r] = m[1]
 
 
@@ -95,10 +82,11 @@
 
 
 def basis_of(bundles, g):
-    return jnp.concatenate([bundles[PACK * g + i] for i in range(PACK)], axis=0)
-
-
-def gram_kernel(bundles, high, low, steps, sums):
+    return jnp.concatenate([b[g] for b in bundles], axis=0)
+
+
+def gram_kernel(*refs):
+    bundles, (high, low, steps, sums) = refs[:-4], refs[-4:]
     groups = high.shape[0]
     wide = LANES // PACK
     block = blocks()
@@ -116,7 +104,8 @@
     steps[...] = 1.0 / largest
 
 
-def solve_kernel(place, bundles, high, low, steps, theirs, *rest, scale):
+def solve_kernel(place, *refs, scale):
+    bundles, (high, low, steps, theirs, *rest) = refs[:PACK], refs[PACK:]
     sources = [s for r, m in enumerate(rest[:-5]) for s in (m.at[0], theirs.at[r])]
     outs = rest[-5:-3]
     goal, state, parts = rest[-3:]
@@ -157,7 +146,8 @@
         for i in range(PACK):
             misfit = pixels_of(PACK * g + i).astype(f32) - fitted[i * slots : (i + 1) * slots]
             square = misfit * misfit
-            bundle = 16 * (4 * place[2] + g ^ 7 * place[1]) + 4 * i + 2 * (place[3] & 1) + place[0]
+            z, y = (place[2] & 4) + (place[2] - g & 3) ^ 7 * place[1], place[4] - i & 3
+            bundle = 16 * z + 4 * y + 2 * (place[3] & 1) + place[0]
             for half in range(2):
                 both = square[2 * half * CAP : 2 * (half + 1) * CAP]
                 both = both + square[2 * (half + 2) * CAP : 2 * (half + 3) * CAP]
@@ -201,36 +191,21 @@
     return pltpu.VMEM(shape, dtype)
 
 
-def call(kernel, place, args, outs, scratch, limit, after=(), stays=(), out_stays=False):
-    spec, lies = pl.BlockSpec(memory_space=pltpu.VMEM), pl.BlockSpec(memory_space=pl.ANY)
-    far = pl.BlockSpec(memory_space=pltpu.HBM)
+def call(kernel, place, args, outs, scratch, limit, after=()):
+    spec = pl.BlockSpec(memory_space=pltpu.VMEM)
     head = [] if place is None else [place]
     return pl.pallas_call(
         kernel,
         out_shape=outs,
-        in_specs=[pl.BlockSpec(memory_space=pltpu.SMEM)] * len(head)
-        + [spec] * len(args)
-        + [far] * len(stays)
-        + [lies] * len(after),
-        out_specs=jax.tree.map(lambda _: far if out_stays else spec, outs),
+        in_specs=[pl.BlockSpec(memory_space=pltpu.SMEM)] * len(head) + [spec] * len(args) + [pl.BlockSpec(memory_space=pl.ANY)] * len(after),
+        out_specs=jax.tree.map(lambda _: spec, outs),
         scratch_shapes=scratch,
         compiler_params=pltpu.CompilerParams(vmem_limit_bytes=limit << 20),
-    )(*head, *args, *stays, *after)
+    )(*head, *args, *after)
 
 
 def spots_of(n_blk, n_pix):
     return [(b // 8, b // 2 % 4, b % 2, p // 2, p % 2) for b in range(n_blk) for p in range(n_pix)]
-
-
-def grouped(spots, key):
-    groups = {}
-    for index, spot in enumerate(spots):
-        groups.setdefault(key(*spot), []).append(index)
-    return list(groups.values())
-
-
-def exchanged(array, groups):
-    return lax.all_to_all(array, ALL, 0, 0, tiled=True, axis_index_groups=groups)
 
 
 def per_device(pixels, bundles, assign):
@@ -238,50 +213,54 @@
     owned, _, width = bundles.shape
     n_blk, n_pix = lax.axis_size("blk"), lax.axis_size("pix")
     spots = spots_of(n_blk, n_pix)
-    column = grouped(spots, lambda z, y, xl, xh, c: (z // 4, xl, xh, c))
     there = {spot: index for index, spot in enumerate(spots)}
-    swap = [(there[s], there[(s[0] ^ 7 * s[3],) + s[1:]]) for s in spots]
-
-    def moved(array, r, other):
-        pairs = []
-        for z, y, xl, xh, c in spots:
-            x = (2 * xh + xl + r) % 4
-            pairs.append((there[z, y, xl, xh, c], there[z, y, x % 2, x // 2, c ^ other]))
-        return lax.ppermute(array, ALL, pairs) if r or other else array
+
+    def sent(array, target):
+        return lax.ppermute(array, ALL, [(there[s], there[target(*s)]) for s in spots])
+
+    def along_x(array, r):
+        def target(z, y, xl, xh, c):
+            x = 2 * xh + xl + r & 3
+            return z, y, x & 1, x >> 1, c
+
+        return sent(array, target) if r else array
+
+    def to_sibling(array):
+        return sent(array, lambda z, y, xl, xh, c: (z, y, xl, xh, c ^ 1))
 
     blk, pix = lax.axis_index("blk"), lax.axis_index("pix")
     z, x_hi = blk >> 3, pix >> 1
-    place = jnp.stack([pix & 1, x_hi, z >> 2, 2 * x_hi + (blk & 1)]).astype(jnp.int32)
+    place = jnp.stack([pix & 1, x_hi, z, 2 * x_hi + (blk & 1), blk >> 1 & 3]).astype(jnp.int32)
     sds = jax.ShapeDtypeStruct
-    n_col, chips = len(column[0]), 4
+    chips = 4
     count = n_blk * owned
-    groups = n_col // PACK
-    held = n_col * CAP
-
-    raw = lax.ppermute(bundles.transpose(0, 2, 1), ALL, swap)
+    groups = 4
+    held = groups * PACK * CAP
+
     *sends, code = call(
         slots_kernel,
         place,
-        [],
+        [assign.reshape(1, rows), pixels.T],
         (sds((2, held, LANES), bf16),) * chips + (sds((1, rows), jnp.int32),),
-        [vmem((1, rows), jnp.int32), vmem((LANES, rows), bf16), vmem((1, rows), f32), pltpu.SemaphoreType.DMA((2,))],
+        [vmem((LANES, rows), bf16), vmem((1, rows), f32)],
         16,
-        stays=[assign.reshape(1, rows), pixels.T],
     )
-    copies = call(
-        spread_kernel,
-        place,
-        [],
-        sds((n_col, width, LANES), bf16),
-        [vmem((width, bands), bf16), vmem((width, LANES), bf16), pltpu.SemaphoreType.DMA((n_col + 1,))],
-        4,
-        stays=[raw],
-        after=[sends[0]],
-        out_stays=True,
-    )
-    gathered = exchanged(copies, column)
-    received = [moved(send, r, 0) for r, send in enumerate(sends)]
-    theirs = moved(call(stack_kernel, None, received, sds((chips, held, LANES), bf16), [], 8), 0, 1)
+    received = [along_x(send, r) for r, send in enumerate(sends)]
+    basis = call(prep_kernel, place, [bundles.transpose(0, 2, 1)], sds((width, LANES), bf16), [], 4)
+    pieces = []
+    for q in range(groups):
+
+        def around(z, y, xl, xh, c):
+            held = z ^ 7 * xh
+            return held & 4 | held + q & 3, y, xl, xh, c
+
+        pieces.append(sent(basis, around))
+    levels = jnp.stack(pieces)
+    gathered = [levels]
+    for r in range(1, PACK):
+        gathered.append(sent(levels, lambda z, y, xl, xh, c: (z, y + r & 3, xl, xh, c)))
+    stacked = call(stack_kernel, None, received, sds((chips, held, LANES), bf16), [], 8, gathered[1:])
+    theirs = to_sibling(stacked)
 
     below = groups * CAP
     slots = 2 * chips * CAP
@@ -290,7 +269,7 @@
     grams = call(
         gram_kernel,
         None,
-        [gathered],
+        gathered,
         (square, square, sds((groups, LANES), f32)),
         [vmem((groups, LANES), f32)],
         16,
@@ -298,7 +277,7 @@
     solved = call(
         lambda *refs: solve_kernel(*refs, scale=scale),
         place,
-        [gathered, *grams, theirs, *received],
+        [*gathered, *grams, theirs, *received],
         (sds((chips, below + 8, LANES), f32),) * 2,
         [
             vmem((groups, slots, LANES), f32),
@@ -307,8 +286,8 @@
         ],
         16,
     )
-    mine, others = solved[0], moved(solved[1], 0, 1)
-    back = [moved(jnp.stack([mine[r], others[r]]), -r, 0) for r in range(1, chips)]
+    mine, others = solved[0], to_sibling(solved[1])
+    back = [along_x(jnp.stack([mine[r], others[r]]), -r) for r in range(1, chips)]
     outs = (sds((width, rows), f32), sds((1, count), f32))
     chosen, energy = call(return_kernel, None, [code, mine, others, *back], outs, [], 16)
     return chosen.T, energy

time: 60 us -> 62.4 us (1.040)
  starting transfers between devices: 25.5 us -> 31.9 us
  waiting for transfers between devices: 20.8 us -> 17.9 us
  Pallas kernels: 10.9 us -> 9.55 us
    ppermute x9 -> x15, starting transfers between devices: 16.3 us -> 31.9 us  [sent(): lax.ppermute(array, ALL, [(there[s], there[target(*s)]) for s in spots])]
    all_to_all x1 -> x0, starting transfers between devices: 9.2 us -> none  [exchanged(): lax.all_to_all(array, ALL, 0, 0, tiled=True, axis_index_groups=groups)]
    ppermute x9 -> x15, waiting for transfers between devices: 20.8 us -> 17.9 us  [sent(): lax.ppermute(array, ALL, [(there[s], there[target(*s)]) for s in spots])]
    pallas_call x6, Pallas kernels: 10.9 us -> 9.55 us  [call(): pl.pallas_call(kernel, out_shape=outs, in_specs=[pl.BlockSpec(memory_spac...]
    unnamed x4 -> x6, local copies, waits for them, and re-layouts: 1.63 us -> 1.86 us
  transfers between devices with their start and end apart: 10 -> 15, of which waited for: 7 -> 9; matrix products, arithmetic and copies ran while one was open for 0% -> 0% of each run, Pallas kernels for 5% -> 4%
where the time goes in v8:
time: 62.4 us; the launch traced here: 62.2 us
  starting transfers between devices  31.9 us (51%)
  waiting for transfers between devices  17.9 us (29%)
  Pallas kernels  9.55 us (15%)
  local copies, waits for them, and re-layouts  1.97 us (3%)
  between operations  0.74 us (1%)
    ppermute x15, starting transfers between devices, sent(): lax.ppermute(array, ALL, [(there[s], there[target(*s)]) for s in spots])  31.9 us
    ppermute x15, waiting for transfers between devices, sent(): lax.ppermute(array, ALL, [(there[s], there[target(*s)]) for s in spots])  17.9 us
    pallas_call x6, Pallas kernels, call(): pl.pallas_call(kernel, out_shape=outs, in_specs=[pl.BlockSpec(memory_spac...  9.55 us
    unnamed x6, local copies, waits for them, and re-layouts  1.86 us
  transfers between devices with their start and end apart: 15, of which 9 were waited for; matrix products, arithmetic and copies ran while one was open for 0% of the time, Pallas kernels for 4%

profile of v8, /device:TPU:1, one launch (start us, length us, event | category | flops | bytes accessed | tf_op | source)
XLA Modules:
  0.0 62.2 jit_solution(601607746074292690)
XLA Ops:
  0.7 0.8 %copy-done.1 = bf16[2,224,64]{1,2,0:T(8,128)(2,1)S(1)} copy-done((bf16[2,224,64]{1,2,0:T(8,128)(2,1)S(1)}, bf16[2,224,64]{1,2,0:T(8,128)(2,1)}, u32[]{:S(2)}) %copy-start.1) | copy-done | bytes 57368
  1.6 0.6 shard_map.51
  2.1 5.2 %collective-permute-start.3 = (bf16[64,256]{1,0:T(8,128)(2,1)S(1)}, bf16[64,256]{1,0:T(8,128)(2,1)S(1)}, u32[]{:S(2)}, u32[]{:S(2)}) collective-permute-start(bf16[64,256]{1,0:T(8,128)(2,1)S(1)} %shard_map.51), channel_id=1, source_target_pairs={{0,96},{1,97},{2,194},{3,195},{4,100},{5,101},{6,198},{7,199},{8,1... | collective-permute-start | bytes 98312 | tf_op jit(solution)/shard_map/ppermute | solution.py:219
  7.8 0.7 %collective-permute-start = (bf16[64,256]{1,0:T(8,128)(2,1)S(1)}, bf16[64,256]{1,0:T(8,128)(2,1)S(1)}, u32[]{:S(2)}, u32[]{:S(2)}) collective-permute-start(bf16[64,256]{1,0:T(8,128)(2,1)S(1)} %shard_map.51), channel_id=1, source_target_pairs={{0,0},{1,1},{2,226},{3,227},{4,4},{5,5},{6,230},{7,231},{8,8},{9,9... | collective-permute-start | bytes 98312 | tf_op jit(solution)/shard_map/ppermute | solution.py:219
  8.4 1.0 %copy-done = bf16[1024,224]{0,1:T(8,128)(2,1)S(1)} copy-done((bf16[1024,224]{0,1:T(8,128)(2,1)S(1)}, bf16[1024,224]{0,1:T(8,128)(2,1)}, u32[]{:S(2)}) %copy-start) | copy-done | bytes 458776
  9.4 2.2 %shard_map.50 = (bf16[2,256,256]{2,1,0:T(8,128)(2,1)S(1)}, bf16[2,256,256]{2,1,0:T(8,128)(2,1)S(1)}, bf16[2,256,256]{2,1,0:T(8,128)(2,1)S(1)}, bf16[2,256,256]{2,1,0:T(8,128)(2,1)S(1)}, s32[1,1024]{1,0:T(1,128)S(1)}) custom-call(s32[5]{0:T(128)S(1)} %stack.47.place.refs_0_, s32[1,1024]{1,0:T(1,128)S(1)} %bitcast.15, bf16[224,1024]{1,0:T(8,128)(2,1)S(1)} %bitcast.13), custom_call_target="tpu_custom_call" | custom-call | tf_op jit(solution)/shard_map/pallas_call | solution.py:197
  12.0 2.8 %collective-permute-start.6 = (bf16[4,64,256]{2,1,0:T(8,128)(2,1)S(1)}, bf16[4,64,256]{2,1,0:T(8,128)(2,1)S(1)}, u32[]{:S(2)}, u32[]{:S(2)}) collective-permute-start(bf16[4,64,256]{2,1,0:T(8,128)(2,1)S(1)} %pad_maximum_fusion.3.refs_0_.refs_1_), channel_id=1, source_target_pairs={{0,24},{1,25},{2,26},{3,27},{4,28},{5,29},{6,30},{7,31},{8,0},{9,1... | collective-permute-start | bytes 393224 | tf_op jit(solution)/shard_map/ppermute | solution.py:219
  14.8 1.2 %collective-permute-start.7 = (bf16[2,256,256]{2,1,0:T(8,128)(2,1)S(1)}, bf16[2,256,256]{2,1,0:T(8,128)(2,1)S(1)}, u32[]{:S(2)}, u32[]{:S(2)}) collective-permute-start(bf16[2,256,256]{2,1,0:T(8,128)(2,1)S(1)} %get-tuple-element.19), channel_id=1, source_target_pairs={{0,4},{1,5},{2,6},{3,7},{4,2},{5,3},{6,0},{7,1},{8,12},{9,13},{10,... | collective-permute-start | bytes 786440 | tf_op jit(solution)/shard_map/ppermute | solution.py:219
  16.0 11.2 %collective-permute-start.8 = (bf16[2,256,256]{2,1,0:T(8,128)(2,1)S(1)}, bf16[2,256,256]{2,1,0:T(8,128)(2,1)S(1)}, u32[]{:S(2)}, u32[]{:S(2)}) collective-permute-start(bf16[2,256,256]{2,1,0:T(8,128)(2,1)S(1)} %get-tuple-element.20), channel_id=1, source_target_pairs={{0,2},{1,3},{2,0},{3,1},{4,6},{5,7},{6,4},{7,5},{8,10},{9,11},{10,... | collective-permute-start | bytes 786440 | tf_op jit(solution)/shard_map/ppermute | solution.py:219
  27.2 1.2 %collective-permute-start.9 = (bf16[2,256,256]{2,1,0:T(8,128)(2,1)S(1)}, bf16[2,256,256]{2,1,0:T(8,128)(2,1)S(1)}, u32[]{:S(2)}, u32[]{:S(2)}) collective-permute-start(bf16[2,256,256]{2,1,0:T(8,128)(2,1)S(1)} %get-tuple-element.21), channel_id=1, source_target_pairs={{0,6},{1,7},{2,4},{3,5},{4,0},{5,1},{6,2},{7,3},{8,14},{9,15},{10,... | collective-permute-start | bytes 786440 | tf_op jit(solution)/shard_map/ppermute | solution.py:219
  28.7 0.7 %collective-permute-start.4 = (bf16[4,64,256]{2,1,0:T(8,128)(2,1)S(1)}, bf16[4,64,256]{2,1,0:T(8,128)(2,1)S(1)}, u32[]{:S(2)}, u32[]{:S(2)}) collective-permute-start(bf16[4,64,256]{2,1,0:T(8,128)(2,1)S(1)} %pad_maximum_fusion.3.refs_0_.refs_1_), channel_id=1, source_target_pairs={{0,8},{1,9},{2,10},{3,11},{4,12},{5,13},{6,14},{7,15},{8,16},{9,17... | collective-permute-start | bytes 393224 | tf_op jit(solution)/shard_map/ppermute | solution.py:219
  29.4 4.4 %collective-permute-done.5.refs_2_.refs_5_.refs_3_ = bf16[4,64,256]{2,1,0:T(8,128)(2,1)S(1)} collective-permute-done((bf16[4,64,256]{2,1,0:T(8,128)(2,1)S(1)}, bf16[4,64,256]{2,1,0:T(8,128)(2,1)S(1)}, u32[]{:S(2)}, u32[]{:S(2)}) %collective-permute-start.5) | collective-permute-done | bytes 131104 | tf_op jit(solution)/shard_map/ppermute | solution.py:219
  33.8 1.6 %collective-permute-done.4.refs_1_.refs_4_.refs_2_ = bf16[4,64,256]{2,1,0:T(8,128)(2,1)S(1)} collective-permute-done((bf16[4,64,256]{2,1,0:T(8,128)(2,1)S(1)}, bf16[4,64,256]{2,1,0:T(8,128)(2,1)S(1)}, u32[]{:S(2)}, u32[]{:S(2)}) %collective-permute-start.4) | collective-permute-done | bytes 131104 | tf_op jit(solution)/shard_map/ppermute | solution.py:219
  36.0 4.2 %collective-permute-start.10 = (bf16[4,256,256]{2,1,0:T(8,128)(2,1)S(1)}, bf16[4,256,256]{2,1,0:T(8,128)(2,1)S(1)}, u32[]{:S(2)}, u32[]{:S(2)}) collective-permute-start(bf16[4,256,256]{2,1,0:T(8,128)(2,1)S(1)} %shard_map.53), channel_id=1, source_target_pairs={{0,1},{1,0},{2,3},{3,2},{4,5},{5,4},{6,7},{7,6},{8,9},{9,8},{10,11... | collective-permute-start | bytes 1572872 | tf_op jit(solution)/shard_map/ppermute | solution.py:219
  40.7 1.0 %collective-permute-done.10.refs_8_ = bf16[4,256,256]{2,1,0:T(8,128)(2,1)S(1)} collective-permute-done((bf16[4,256,256]{2,1,0:T(8,128)(2,1)S(1)}, bf16[4,256,256]{2,1,0:T(8,128)(2,1)S(1)}, u32[]{:S(2)}, u32[]{:S(2)}) %collective-permute-start.10) | collective-permute-done | bytes 524320 | tf_op jit(solution)/shard_map/ppermute | solution.py:219
  41.8 4.8 %shard_map.54 = (f32[4,72,256]{2,1,0:T(8,128)S(1)}, f32[4,72,256]{2,1,0:T(8,128)S(1)}) custom-call(s32[5]{0:T(128)S(1)} %stack.47.place.refs_0_, bf16[4,64,256]{2,1,0:T(8,128)(2,1)S(1)} %pad_maximum_fusion.3.refs_0_.refs_1_, bf16[4,64,256]{2,1,0:T(8,128)(2,1)S(1)} %collective-permute-done.4.refs_1_.refs_4_.refs_2_, ...), custom_call_target="tpu_custom_call" | custom-call | tf_op jit(solution)/shard_map/pallas_call | solution.py:197
  47.1 1.2 %collective-permute-done.11.theirs = f32[4,72,256]{2,1,0:T(8,128)S(1)} collective-permute-done((f32[4,72,256]{2,1,0:T(8,128)S(1)}, f32[4,72,256]{2,1,0:T(8,128)S(1)}, u32[]{:S(2)}, u32[]{:S(2)}) %collective-permute-start.11) | collective-permute-done | bytes 294944 | tf_op jit(solution)/shard_map/ppermute | solution.py:219
  48.3 1.9 %collective-permute-start.12 = (f32[2,72,256]{2,1,0:T(8,128)S(1)}, f32[2,72,256]{2,1,0:T(8,128)S(1)}, u32[]{:S(2)}, u32[]{:S(2)}) collective-permute-start(f32[2,72,256]{2,1,0:T(8,128)S(1)} %pad_maximum_fusion), channel_id=1, source_target_pairs={{0,6},{1,7},{2,4},{3,5},{4,0},{5,1},{6,2},{7,3},{8,14},{9,15},{10,... | collective-permute-start | bytes 442376 | tf_op jit(solution)/shard_map/ppermute | solution.py:219
  50.2 0.9 %collective-permute-start.13 = (f32[2,72,256]{2,1,0:T(8,128)S(1)}, f32[2,72,256]{2,1,0:T(8,128)S(1)}, u32[]{:S(2)}, u32[]{:S(2)}) collective-permute-start(f32[2,72,256]{2,1,0:T(8,128)S(1)} %pad_maximum_fusion.1), channel_id=1, source_target_pairs={{0,2},{1,3},{2,0},{3,1},{4,6},{5,7},{6,4},{7,5},{8,10},{9,11},{10,... | collective-permute-start | bytes 442376 | tf_op jit(solution)/shard_map/ppermute | solution.py:219
  51.1 0.7 %collective-permute-start.14 = (f32[2,72,256]{2,1,0:T(8,128)S(1)}, f32[2,72,256]{2,1,0:T(8,128)S(1)}, u32[]{:S(2)}, u32[]{:S(2)}) collective-permute-start(f32[2,72,256]{2,1,0:T(8,128)S(1)} %pad_maximum_fusion.2), channel_id=1, source_target_pairs={{0,4},{1,5},{2,6},{3,7},{4,2},{5,3},{6,0},{7,1},{8,12},{9,13},{10,... | collective-permute-start | bytes 442376 | tf_op jit(solution)/shard_map/ppermute | solution.py:219
  51.8 1.6 %collective-permute-done.12.back1 = f32[2,72,256]{2,1,0:T(8,128)S(1)} collective-permute-done((f32[2,72,256]{2,1,0:T(8,128)S(1)}, f32[2,72,256]{2,1,0:T(8,128)S(1)}, u32[]{:S(2)}, u32[]{:S(2)}) %collective-permute-start.12) | collective-permute-done | bytes 147488 | tf_op jit(solution)/shard_map/ppermute | solution.py:219
  53.4 3.1 %collective-permute-done.13.back2 = f32[2,72,256]{2,1,0:T(8,128)S(1)} collective-permute-done((f32[2,72,256]{2,1,0:T(8,128)S(1)}, f32[2,72,256]{2,1,0:T(8,128)S(1)}, u32[]{:S(2)}, u32[]{:S(2)}) %collective-permute-start.13) | collective-permute-done | bytes 147488 | tf_op jit(solution)/shard_map/ppermute | solution.py:219
  56.5 4.2 %collective-permute-done.14.back3 = f32[2,72,256]{2,1,0:T(8,128)S(1)} collective-permute-done((f32[2,72,256]{2,1,0:T(8,128)S(1)}, f32[2,72,256]{2,1,0:T(8,128)S(1)}, u32[]{:S(2)}, u32[]{:S(2)}) %collective-permute-start.14) | collective-permute-done | bytes 147488 | tf_op jit(solution)/shard_map/ppermute | solution.py:219
  60.7 1.5 %shard_map.55 = (f32[64,1024]{1,0:T(8,128)}, f32[1,128]{1,0:T(1,128)}) custom-call(s32[1,1024]{1,0:T(1,128)S(1)} %get-tuple-element.14.code, f32[4,72,256]{2,1,0:T(8,128)S(1)} %get-tuple-element.22.mine, f32[4,72,256]{2,1,0:T(8,128)S(1)} %collective-permute-done.11.theirs, f32[2,72,256]{2,1,0:T(8,128)S(1)} %collective-permute-done.12.back1, ...), custom_call_target="tpu_custom_call" | custom-call | tf_op jit(solution)/shard_map/pallas_call | solution.py:197
  (25 shorter events, 2.7 us)
Async XLA Ops:
  0.7 0.8 %copy-start.1 = (bf16[2,224,64]{1,2,0:T(8,128)(2,1)S(1)}, bf16[2,224,64]{1,2,0:T(8,128)(2,1)}, u32[]{:S(2)}) copy-start(bf16[2,224,64]{1,2,0:T(8,128)(2,1)} %param.4) | copy-start | bytes 172036
  1.6 6.9 %copy-start.2 = (s32[1024,1]{0,1:T(1,128)S(1)}, s32[1024,1]{0,1:T(1,128)}, u32[]{:S(2)}) copy-start(s32[1024,1]{0,1:T(1,128)} %param.5) | copy-start | bytes 12292
  2.1 9.5 %collective-permute-start.3 = (bf16[64,256]{1,0:T(8,128)(2,1)S(1)}, bf16[64,256]{1,0:T(8,128)(2,1)S(1)}, u32[]{:S(2)}, u32[]{:S(2)}) collective-permute-start(bf16[64,256]{1,0:T(8,128)(2,1)S(1)} %shard_map.51), channel_id=1, source_target_pairs={{0,96},{1,97},{2,194},{3,195},{4,100},{5,101},{6,198},{7,199},{8,1... | collective-permute-start | bytes 98312 | tf_op jit(solution)/shard_map/ppermute | solution.py:219
  7.4 4.3 %collective-permute-start.2 = (bf16[64,256]{1,0:T(8,128)(2,1)S(1)}, bf16[64,256]{1,0:T(8,128)(2,1)S(1)}, u32[]{:S(2)}, u32[]{:S(2)}) collective-permute-start(bf16[64,256]{1,0:T(8,128)(2,1)S(1)} %shard_map.51), channel_id=1, source_target_pairs={{0,64},{1,65},{2,162},{3,163},{4,68},{5,69},{6,166},{7,167},{8,72}... | collective-permute-start | bytes 98312 | tf_op jit(solution)/shard_map/ppermute | solution.py:219
  7.4 4.6 %collective-permute-start.1 = (bf16[64,256]{1,0:T(8,128)(2,1)S(1)}, bf16[64,256]{1,0:T(8,128)(2,1)S(1)}, u32[]{:S(2)}, u32[]{:S(2)}) collective-permute-start(bf16[64,256]{1,0:T(8,128)(2,1)S(1)} %shard_map.51), channel_id=1, source_target_pairs={{0,32},{1,33},{2,130},{3,131},{4,36},{5,37},{6,134},{7,135},{8,40}... | collective-permute-start | bytes 98312 | tf_op jit(solution)/shard_map/ppermute | solution.py:219
  7.8 4.2 %collective-permute-start = (bf16[64,256]{1,0:T(8,128)(2,1)S(1)}, bf16[64,256]{1,0:T(8,128)(2,1)S(1)}, u32[]{:S(2)}, u32[]{:S(2)}) collective-permute-start(bf16[64,256]{1,0:T(8,128)(2,1)S(1)} %shard_map.51), channel_id=1, source_target_pairs={{0,0},{1,1},{2,226},{3,227},{4,4},{5,5},{6,230},{7,231},{8,8},{9,9... | collective-permute-start | bytes 98312 | tf_op jit(solution)/shard_map/ppermute | solution.py:219
  8.4 1.0 %copy-start = (bf16[1024,224]{0,1:T(8,128)(2,1)S(1)}, bf16[1024,224]{0,1:T(8,128)(2,1)}, u32[]{:S(2)}) copy-start(bf16[1024,224]{0,1:T(8,128)(2,1)} %param.3) | copy-start | bytes 1376260
  12.0 16.8 %collective-permute-start.6 = (bf16[4,64,256]{2,1,0:T(8,128)(2,1)S(1)}, bf16[4,64,256]{2,1,0:T(8,128)(2,1)S(1)}, u32[]{:S(2)}, u32[]{:S(2)}) collective-permute-start(bf16[4,64,256]{2,1,0:T(8,128)(2,1)S(1)} %pad_maximum_fusion.3.refs_0_.refs_1_), channel_id=1, source_target_pairs={{0,24},{1,25},{2,26},{3,27},{4,28},{5,29},{6,30},{7,31},{8,0},{9,1... | collective-permute-start | bytes 393224 | tf_op jit(solution)/shard_map/ppermute | solution.py:219
  14.8 20.6 %collective-permute-start.7 = (bf16[2,256,256]{2,1,0:T(8,128)(2,1)S(1)}, bf16[2,256,256]{2,1,0:T(8,128)(2,1)S(1)}, u32[]{:S(2)}, u32[]{:S(2)}) collective-permute-start(bf16[2,256,256]{2,1,0:T(8,128)(2,1)S(1)} %get-tuple-element.19), channel_id=1, source_target_pairs={{0,4},{1,5},{2,6},{3,7},{4,2},{5,3},{6,0},{7,1},{8,12},{9,13},{10,... | collective-permute-start | bytes 786440 | tf_op jit(solution)/shard_map/ppermute | solution.py:219
  16.0 19.9 %collective-permute-start.8 = (bf16[2,256,256]{2,1,0:T(8,128)(2,1)S(1)}, bf16[2,256,256]{2,1,0:T(8,128)(2,1)S(1)}, u32[]{:S(2)}, u32[]{:S(2)}) collective-permute-start(bf16[2,256,256]{2,1,0:T(8,128)(2,1)S(1)} %get-tuple-element.20), channel_id=1, source_target_pairs={{0,2},{1,3},{2,0},{3,1},{4,6},{5,7},{6,4},{7,5},{8,10},{9,11},{10,... | collective-permute-start | bytes 786440 | tf_op jit(solution)/shard_map/ppermute | solution.py:219
  27.2 8.7 %collective-permute-start.9 = (bf16[2,256,256]{2,1,0:T(8,128)(2,1)S(1)}, bf16[2,256,256]{2,1,0:T(8,128)(2,1)S(1)}, u32[]{:S(2)}, u32[]{:S(2)}) collective-permute-start(bf16[2,256,256]{2,1,0:T(8,128)(2,1)S(1)} %get-tuple-element.21), channel_id=1, source_target_pairs={{0,6},{1,7},{2,4},{3,5},{4,0},{5,1},{6,2},{7,3},{8,14},{9,15},{10,... | collective-permute-start | bytes 786440 | tf_op jit(solution)/shard_map/ppermute | solution.py:219
  28.4 5.4 %collective-permute-start.5 = (bf16[4,64,256]{2,1,0:T(8,128)(2,1)S(1)}, bf16[4,64,256]{2,1,0:T(8,128)(2,1)S(1)}, u32[]{:S(2)}, u32[]{:S(2)}) collective-permute-start(bf16[4,64,256]{2,1,0:T(8,128)(2,1)S(1)} %pad_maximum_fusion.3.refs_0_.refs_1_), channel_id=1, source_target_pairs={{0,16},{1,17},{2,18},{3,19},{4,20},{5,21},{6,22},{7,23},{8,24},{9,... | collective-permute-start | bytes 393224 | tf_op jit(solution)/shard_map/ppermute | solution.py:219
  28.7 6.7 %collective-permute-start.4 = (bf16[4,64,256]{2,1,0:T(8,128)(2,1)S(1)}, bf16[4,64,256]{2,1,0:T(8,128)(2,1)S(1)}, u32[]{:S(2)}, u32[]{:S(2)}) collective-permute-start(bf16[4,64,256]{2,1,0:T(8,128)(2,1)S(1)} %pad_maximum_fusion.3.refs_0_.refs_1_), channel_id=1, source_target_pairs={{0,8},{1,9},{2,10},{3,11},{4,12},{5,13},{6,14},{7,15},{8,16},{9,17... | collective-permute-start | bytes 393224 | tf_op jit(solution)/shard_map/ppermute | solution.py:219
  36.0 5.8 %collective-permute-start.10 = (bf16[4,256,256]{2,1,0:T(8,128)(2,1)S(1)}, bf16[4,256,256]{2,1,0:T(8,128)(2,1)S(1)}, u32[]{:S(2)}, u32[]{:S(2)}) collective-permute-start(bf16[4,256,256]{2,1,0:T(8,128)(2,1)S(1)} %shard_map.53), channel_id=1, source_target_pairs={{0,1},{1,0},{2,3},{3,2},{4,5},{5,4},{6,7},{7,6},{8,9},{9,8},{10,11... | collective-permute-start | bytes 1572872 | tf_op jit(solution)/shard_map/ppermute | solution.py:219
  46.6 1.7 %collective-permute-start.11 = (f32[4,72,256]{2,1,0:T(8,128)S(1)}, f32[4,72,256]{2,1,0:T(8,128)S(1)}, u32[]{:S(2)}, u32[]{:S(2)}) collective-permute-start(f32[4,72,256]{2,1,0:T(8,128)S(1)} %get-tuple-element.23), channel_id=1, source_target_pairs={{0,1},{1,0},{2,3},{3,2},{4,5},{5,4},{6,7},{7,6},{8,9},{9,8},{10,11... | collective-permute-start | bytes 884744 | tf_op jit(solution)/shard_map/ppermute | solution.py:219
  48.3 5.1 %collective-permute-start.12 = (f32[2,72,256]{2,1,0:T(8,128)S(1)}, f32[2,72,256]{2,1,0:T(8,128)S(1)}, u32[]{:S(2)}, u32[]{:S(2)}) collective-permute-start(f32[2,72,256]{2,1,0:T(8,128)S(1)} %pad_maximum_fusion), channel_id=1, source_target_pairs={{0,6},{1,7},{2,4},{3,5},{4,0},{5,1},{6,2},{7,3},{8,14},{9,15},{10,... | collective-permute-start | bytes 442376 | tf_op jit(solution)/shard_map/ppermute | solution.py:219
  50.2 6.3 %collective-permute-start.13 = (f32[2,72,256]{2,1,0:T(8,128)S(1)}, f32[2,72,256]{2,1,0:T(8,128)S(1)}, u32[]{:S(2)}, u32[]{:S(2)}) collective-permute-start(f32[2,72,256]{2,1,0:T(8,128)S(1)} %pad_maximum_fusion.1), channel_id=1, source_target_pairs={{0,2},{1,3},{2,0},{3,1},{4,6},{5,7},{6,4},{7,5},{8,10},{9,11},{10,... | collective-permute-start | bytes 442376 | tf_op jit(solution)/shard_map/ppermute | solution.py:219
  51.1 9.6 %collective-permute-start.14 = (f32[2,72,256]{2,1,0:T(8,128)S(1)}, f32[2,72,256]{2,1,0:T(8,128)S(1)}, u32[]{:S(2)}, u32[]{:S(2)}) collective-permute-start(f32[2,72,256]{2,1,0:T(8,128)S(1)} %pad_maximum_fusion.2), channel_id=1, source_target_pairs={{0,4},{1,5},{2,6},{3,7},{4,2},{5,3},{6,0},{7,1},{8,12},{9,13},{10,... | collective-permute-start | bytes 442376 | tf_op jit(solution)/shard_map/ppermute | solution.py:219

commit v9 on v8

--- a/solution.py
+++ b/solution.py
@@ -134,7 +134,7 @@
             state[g] = jnp.maximum(a - steps[g : g + 1] * (grad - goal[g]), 0.0)
         return carry
 
-    lax.fori_loop(1, ITERS, sweep, 0)
+    lax.fori_loop(1, ITERS, sweep, 0, unroll=True)
     parts[...] = jnp.zeros(parts.shape, f32)
     for g in range(groups):
         a = state[g]
@@ -246,7 +246,7 @@
         16,
     )
     received = [along_x(send, r) for r, send in enumerate(sends)]
-    basis = call(prep_kernel, place, [bundles.transpose(0, 2, 1)], sds((width, LANES), bf16), [], 4)
+    basis = call(prep_kernel, place, [bundles.transpose(0, 2, 1)], sds((width, LANES), bf16), [], 4, [sends[0]])
     pieces = []
     for q in range(groups):
 

time: 62.4 us -> 63.9 us (1.024)
  waiting for transfers between devices: 17.9 us -> 21.2 us
  Pallas kernels: 9.55 us -> 8.16 us
    ppermute x15, waiting for transfers between devices: 17.9 us -> 21.2 us  [sent(): lax.ppermute(array, ALL, [(there[s], there[target(*s)]) for s in spots])]
    pallas_call x6, Pallas kernels: 9.55 us -> 8.16 us  [call(): pl.pallas_call(kernel, out_shape=outs, in_specs=[pl.BlockSpec(memory_spac...]
  transfers between devices with their start and end apart: 15 -> 15, of which waited for: 9 -> 10; matrix products, arithmetic and copies ran while one was open for 0% -> 0% of each run, Pallas kernels for 4% -> 1%
where the time goes in v9:
time: 63.9 us; the launch traced here: 63.8 us
  starting transfers between devices  31.9 us (50%)
  waiting for transfers between devices  21.2 us (33%)
  Pallas kernels  8.16 us (13%)
  local copies, waits for them, and re-layouts  1.73 us (3%)
  between operations  0.73 us (1%)
    ppermute x15, starting transfers between devices, sent(): lax.ppermute(array, ALL, [(there[s], there[target(*s)]) for s in spots])  31.9 us
    ppermute x15, waiting for transfers between devices, sent(): lax.ppermute(array, ALL, [(there[s], there[target(*s)]) for s in spots])  21.2 us
    pallas_call x6, Pallas kernels, call(): pl.pallas_call(kernel, out_shape=outs, in_specs=[pl.BlockSpec(memory_spac...  8.16 us
    unnamed x6, local copies, waits for them, and re-layouts  1.62 us
  transfers between devices with their start and end apart: 15, of which 10 were waited for; matrix products, arithmetic and copies ran while one was open for 0% of the time, Pallas kernels for 1%

profile of v9, /device:TPU:1, one launch (start us, length us, event | category | flops | bytes accessed | tf_op | source)
XLA Modules:
  0.0 63.8 jit_solution(15392905820848784347)
XLA Ops:
  0.7 0.6 copy-done.2
  1.3 1.0 %copy-done = bf16[1024,224]{0,1:T(8,128)(2,1)S(1)} copy-done((bf16[1024,224]{0,1:T(8,128)(2,1)S(1)}, bf16[1024,224]{0,1:T(8,128)(2,1)}, u32[]{:S(2)}) %copy-start) | copy-done | bytes 458776
  2.3 2.2 %shard_map.50 = (bf16[2,256,256]{2,1,0:T(8,128)(2,1)S(1)}, bf16[2,256,256]{2,1,0:T(8,128)(2,1)S(1)}, bf16[2,256,256]{2,1,0:T(8,128)(2,1)S(1)}, bf16[2,256,256]{2,1,0:T(8,128)(2,1)S(1)}, s32[1,1024]{1,0:T(1,128)S(1)}) custom-call(s32[5]{0:T(128)S(1)} %stack.47.place.refs_0_, s32[1,1024]{1,0:T(1,128)S(1)} %bitcast.15, bf16[224,1024]{1,0:T(8,128)(2,1)S(1)} %bitcast.13), custom_call_target="tpu_custom_call" | custom-call | tf_op jit(solution)/shard_map/pallas_call | solution.py:197
  5.1 5.2 %collective-permute-start.3 = (bf16[64,256]{1,0:T(8,128)(2,1)S(1)}, bf16[64,256]{1,0:T(8,128)(2,1)S(1)}, u32[]{:S(2)}, u32[]{:S(2)}) collective-permute-start(bf16[64,256]{1,0:T(8,128)(2,1)S(1)} %shard_map.51), channel_id=1, source_target_pairs={{0,96},{1,97},{2,194},{3,195},{4,100},{5,101},{6,198},{7,199},{8,1... | collective-permute-start | bytes 98312 | tf_op jit(solution)/shard_map/ppermute | solution.py:219
  10.7 0.7 %collective-permute-start = (bf16[64,256]{1,0:T(8,128)(2,1)S(1)}, bf16[64,256]{1,0:T(8,128)(2,1)S(1)}, u32[]{:S(2)}, u32[]{:S(2)}) collective-permute-start(bf16[64,256]{1,0:T(8,128)(2,1)S(1)} %shard_map.51), channel_id=1, source_target_pairs={{0,0},{1,1},{2,226},{3,227},{4,4},{5,5},{6,230},{7,231},{8,8},{9,9... | collective-permute-start | bytes 98312 | tf_op jit(solution)/shard_map/ppermute | solution.py:219
  11.4 3.0 %collective-permute-done.2 = bf16[64,256]{1,0:T(8,128)(2,1)S(1)} collective-permute-done((bf16[64,256]{1,0:T(8,128)(2,1)S(1)}, bf16[64,256]{1,0:T(8,128)(2,1)S(1)}, u32[]{:S(2)}, u32[]{:S(2)}) %collective-permute-start.2) | collective-permute-done | bytes 32800 | tf_op jit(solution)/shard_map/ppermute | solution.py:219
  14.9 2.8 %collective-permute-start.6 = (bf16[4,64,256]{2,1,0:T(8,128)(2,1)S(1)}, bf16[4,64,256]{2,1,0:T(8,128)(2,1)S(1)}, u32[]{:S(2)}, u32[]{:S(2)}) collective-permute-start(bf16[4,64,256]{2,1,0:T(8,128)(2,1)S(1)} %pad_maximum_fusion.3.refs_0_.refs_1_), channel_id=1, source_target_pairs={{0,24},{1,25},{2,26},{3,27},{4,28},{5,29},{6,30},{7,31},{8,0},{9,1... | collective-permute-start | bytes 393224 | tf_op jit(solution)/shard_map/ppermute | solution.py:219
  17.8 1.2 %collective-permute-start.7 = (bf16[2,256,256]{2,1,0:T(8,128)(2,1)S(1)}, bf16[2,256,256]{2,1,0:T(8,128)(2,1)S(1)}, u32[]{:S(2)}, u32[]{:S(2)}) collective-permute-start(bf16[2,256,256]{2,1,0:T(8,128)(2,1)S(1)} %get-tuple-element.19), channel_id=1, source_target_pairs={{0,4},{1,5},{2,6},{3,7},{4,2},{5,3},{6,0},{7,1},{8,12},{9,13},{10,... | collective-permute-start | bytes 786440 | tf_op jit(solution)/shard_map/ppermute | solution.py:219
  19.0 11.2 %collective-permute-start.8 = (bf16[2,256,256]{2,1,0:T(8,128)(2,1)S(1)}, bf16[2,256,256]{2,1,0:T(8,128)(2,1)S(1)}, u32[]{:S(2)}, u32[]{:S(2)}) collective-permute-start(bf16[2,256,256]{2,1,0:T(8,128)(2,1)S(1)} %get-tuple-element.20), channel_id=1, source_target_pairs={{0,2},{1,3},{2,0},{3,1},{4,6},{5,7},{6,4},{7,5},{8,10},{9,11},{10,... | collective-permute-start | bytes 786440 | tf_op jit(solution)/shard_map/ppermute | solution.py:219
  30.2 1.1 %collective-permute-start.9 = (bf16[2,256,256]{2,1,0:T(8,128)(2,1)S(1)}, bf16[2,256,256]{2,1,0:T(8,128)(2,1)S(1)}, u32[]{:S(2)}, u32[]{:S(2)}) collective-permute-start(bf16[2,256,256]{2,1,0:T(8,128)(2,1)S(1)} %get-tuple-element.21), channel_id=1, source_target_pairs={{0,6},{1,7},{2,4},{3,5},{4,0},{5,1},{6,2},{7,3},{8,14},{9,15},{10,... | collective-permute-start | bytes 786440 | tf_op jit(solution)/shard_map/ppermute | solution.py:219
  31.7 0.7 %collective-permute-start.4 = (bf16[4,64,256]{2,1,0:T(8,128)(2,1)S(1)}, bf16[4,64,256]{2,1,0:T(8,128)(2,1)S(1)}, u32[]{:S(2)}, u32[]{:S(2)}) collective-permute-start(bf16[4,64,256]{2,1,0:T(8,128)(2,1)S(1)} %pad_maximum_fusion.3.refs_0_.refs_1_), channel_id=1, source_target_pairs={{0,8},{1,9},{2,10},{3,11},{4,12},{5,13},{6,14},{7,15},{8,16},{9,17... | collective-permute-start | bytes 393224 | tf_op jit(solution)/shard_map/ppermute | solution.py:219
  32.4 4.4 %collective-permute-done.5.refs_2_.refs_5_.refs_3_ = bf16[4,64,256]{2,1,0:T(8,128)(2,1)S(1)} collective-permute-done((bf16[4,64,256]{2,1,0:T(8,128)(2,1)S(1)}, bf16[4,64,256]{2,1,0:T(8,128)(2,1)S(1)}, u32[]{:S(2)}, u32[]{:S(2)}) %collective-permute-start.5) | collective-permute-done | bytes 131104 | tf_op jit(solution)/shard_map/ppermute | solution.py:219
  36.8 1.6 %collective-permute-done.4.refs_1_.refs_4_.refs_2_ = bf16[4,64,256]{2,1,0:T(8,128)(2,1)S(1)} collective-permute-done((bf16[4,64,256]{2,1,0:T(8,128)(2,1)S(1)}, bf16[4,64,256]{2,1,0:T(8,128)(2,1)S(1)}, u32[]{:S(2)}, u32[]{:S(2)}) %collective-permute-start.4) | collective-permute-done | bytes 131104 | tf_op jit(solution)/shard_map/ppermute | solution.py:219
  39.0 4.2 %collective-permute-start.10 = (bf16[4,256,256]{2,1,0:T(8,128)(2,1)S(1)}, bf16[4,256,256]{2,1,0:T(8,128)(2,1)S(1)}, u32[]{:S(2)}, u32[]{:S(2)}) collective-permute-start(bf16[4,256,256]{2,1,0:T(8,128)(2,1)S(1)} %shard_map.53), channel_id=1, source_target_pairs={{0,1},{1,0},{2,3},{3,2},{4,5},{5,4},{6,7},{7,6},{8,9},{9,8},{10,11... | collective-permute-start | bytes 1572872 | tf_op jit(solution)/shard_map/ppermute | solution.py:219
  43.7 1.1 %collective-permute-done.10.refs_8_ = bf16[4,256,256]{2,1,0:T(8,128)(2,1)S(1)} collective-permute-done((bf16[4,256,256]{2,1,0:T(8,128)(2,1)S(1)}, bf16[4,256,256]{2,1,0:T(8,128)(2,1)S(1)}, u32[]{:S(2)}, u32[]{:S(2)}) %collective-permute-start.10) | collective-permute-done | bytes 524320 | tf_op jit(solution)/shard_map/ppermute | solution.py:219
  44.7 3.4 %shard_map.54 = (f32[4,72,256]{2,1,0:T(8,128)S(1)}, f32[4,72,256]{2,1,0:T(8,128)S(1)}) custom-call(s32[5]{0:T(128)S(1)} %stack.47.place.refs_0_, bf16[4,64,256]{2,1,0:T(8,128)(2,1)S(1)} %pad_maximum_fusion.3.refs_0_.refs_1_, bf16[4,64,256]{2,1,0:T(8,128)(2,1)S(1)} %collective-permute-done.4.refs_1_.refs_4_.refs_2_, ...), custom_call_target="tpu_custom_call" | custom-call | tf_op jit(solution)/shard_map/pallas_call | solution.py:197
  48.7 1.2 %collective-permute-done.11.theirs = f32[4,72,256]{2,1,0:T(8,128)S(1)} collective-permute-done((f32[4,72,256]{2,1,0:T(8,128)S(1)}, f32[4,72,256]{2,1,0:T(8,128)S(1)}, u32[]{:S(2)}, u32[]{:S(2)}) %collective-permute-start.11) | collective-permute-done | bytes 294944 | tf_op jit(solution)/shard_map/ppermute | solution.py:219
  49.9 1.9 %collective-permute-start.12 = (f32[2,72,256]{2,1,0:T(8,128)S(1)}, f32[2,72,256]{2,1,0:T(8,128)S(1)}, u32[]{:S(2)}, u32[]{:S(2)}) collective-permute-start(f32[2,72,256]{2,1,0:T(8,128)S(1)} %pad_maximum_fusion), channel_id=1, source_target_pairs={{0,6},{1,7},{2,4},{3,5},{4,0},{5,1},{6,2},{7,3},{8,14},{9,15},{10,... | collective-permute-start | bytes 442376 | tf_op jit(solution)/shard_map/ppermute | solution.py:219
  51.8 0.9 %collective-permute-start.13 = (f32[2,72,256]{2,1,0:T(8,128)S(1)}, f32[2,72,256]{2,1,0:T(8,128)S(1)}, u32[]{:S(2)}, u32[]{:S(2)}) collective-permute-start(f32[2,72,256]{2,1,0:T(8,128)S(1)} %pad_maximum_fusion.1), channel_id=1, source_target_pairs={{0,2},{1,3},{2,0},{3,1},{4,6},{5,7},{6,4},{7,5},{8,10},{9,11},{10,... | collective-permute-start | bytes 442376 | tf_op jit(solution)/shard_map/ppermute | solution.py:219
  52.7 0.7 %collective-permute-start.14 = (f32[2,72,256]{2,1,0:T(8,128)S(1)}, f32[2,72,256]{2,1,0:T(8,128)S(1)}, u32[]{:S(2)}, u32[]{:S(2)}) collective-permute-start(f32[2,72,256]{2,1,0:T(8,128)S(1)} %pad_maximum_fusion.2), channel_id=1, source_target_pairs={{0,4},{1,5},{2,6},{3,7},{4,2},{5,3},{6,0},{7,1},{8,12},{9,13},{10,... | collective-permute-start | bytes 442376 | tf_op jit(solution)/shard_map/ppermute | solution.py:219
  53.4 1.6 %collective-permute-done.12.back1 = f32[2,72,256]{2,1,0:T(8,128)S(1)} collective-permute-done((f32[2,72,256]{2,1,0:T(8,128)S(1)}, f32[2,72,256]{2,1,0:T(8,128)S(1)}, u32[]{:S(2)}, u32[]{:S(2)}) %collective-permute-start.12) | collective-permute-done | bytes 147488 | tf_op jit(solution)/shard_map/ppermute | solution.py:219
  55.0 3.1 %collective-permute-done.13.back2 = f32[2,72,256]{2,1,0:T(8,128)S(1)} collective-permute-done((f32[2,72,256]{2,1,0:T(8,128)S(1)}, f32[2,72,256]{2,1,0:T(8,128)S(1)}, u32[]{:S(2)}, u32[]{:S(2)}) %collective-permute-start.13) | collective-permute-done | bytes 147488 | tf_op jit(solution)/shard_map/ppermute | solution.py:219
  58.1 4.2 %collective-permute-done.14.back3 = f32[2,72,256]{2,1,0:T(8,128)S(1)} collective-permute-done((f32[2,72,256]{2,1,0:T(8,128)S(1)}, f32[2,72,256]{2,1,0:T(8,128)S(1)}, u32[]{:S(2)}, u32[]{:S(2)}) %collective-permute-start.14) | collective-permute-done | bytes 147488 | tf_op jit(solution)/shard_map/ppermute | solution.py:219
  62.3 1.5 %shard_map.55 = (f32[64,1024]{1,0:T(8,128)}, f32[1,128]{1,0:T(1,128)}) custom-call(s32[1,1024]{1,0:T(1,128)S(1)} %get-tuple-element.14.code, f32[4,72,256]{2,1,0:T(8,128)S(1)} %get-tuple-element.22.mine, f32[4,72,256]{2,1,0:T(8,128)S(1)} %collective-permute-done.11.theirs, f32[2,72,256]{2,1,0:T(8,128)S(1)} %collective-permute-done.12.back1, ...), custom_call_target="tpu_custom_call" | custom-call | tf_op jit(solution)/shard_map/pallas_call | solution.py:197
  (25 shorter events, 3.6 us)
Async XLA Ops:
  0.6 0.7 %copy-start.2 = (s32[1024,1]{0,1:T(1,128)S(1)}, s32[1024,1]{0,1:T(1,128)}, u32[]{:S(2)}) copy-start(s32[1024,1]{0,1:T(1,128)} %param.5) | copy-start | bytes 12292
  1.3 1.0 %copy-start = (bf16[1024,224]{0,1:T(8,128)(2,1)S(1)}, bf16[1024,224]{0,1:T(8,128)(2,1)}, u32[]{:S(2)}) copy-start(bf16[1024,224]{0,1:T(8,128)(2,1)} %param.3) | copy-start | bytes 1376260
  2.3 2.2 %copy-start.1 = (bf16[2,224,64]{1,2,0:T(8,128)(2,1)S(1)}, bf16[2,224,64]{1,2,0:T(8,128)(2,1)}, u32[]{:S(2)}) copy-start(bf16[2,224,64]{1,2,0:T(8,128)(2,1)} %param.4) | copy-start | bytes 172036
  5.1 6.3 %collective-permute-start.3 = (bf16[64,256]{1,0:T(8,128)(2,1)S(1)}, bf16[64,256]{1,0:T(8,128)(2,1)S(1)}, u32[]{:S(2)}, u32[]{:S(2)}) collective-permute-start(bf16[64,256]{1,0:T(8,128)(2,1)S(1)} %shard_map.51), channel_id=1, source_target_pairs={{0,96},{1,97},{2,194},{3,195},{4,100},{5,101},{6,198},{7,199},{8,1... | collective-permute-start | bytes 98312 | tf_op jit(solution)/shard_map/ppermute | solution.py:219
  10.4 4.0 %collective-permute-start.2 = (bf16[64,256]{1,0:T(8,128)(2,1)S(1)}, bf16[64,256]{1,0:T(8,128)(2,1)S(1)}, u32[]{:S(2)}, u32[]{:S(2)}) collective-permute-start(bf16[64,256]{1,0:T(8,128)(2,1)S(1)} %shard_map.51), channel_id=1, source_target_pairs={{0,64},{1,65},{2,162},{3,163},{4,68},{5,69},{6,166},{7,167},{8,72}... | collective-permute-start | bytes 98312 | tf_op jit(solution)/shard_map/ppermute | solution.py:219
  10.4 4.6 %collective-permute-start.1 = (bf16[64,256]{1,0:T(8,128)(2,1)S(1)}, bf16[64,256]{1,0:T(8,128)(2,1)S(1)}, u32[]{:S(2)}, u32[]{:S(2)}) collective-permute-start(bf16[64,256]{1,0:T(8,128)(2,1)S(1)} %shard_map.51), channel_id=1, source_target_pairs={{0,32},{1,33},{2,130},{3,131},{4,36},{5,37},{6,134},{7,135},{8,40}... | collective-permute-start | bytes 98312 | tf_op jit(solution)/shard_map/ppermute | solution.py:219
  10.7 4.2 %collective-permute-start = (bf16[64,256]{1,0:T(8,128)(2,1)S(1)}, bf16[64,256]{1,0:T(8,128)(2,1)S(1)}, u32[]{:S(2)}, u32[]{:S(2)}) collective-permute-start(bf16[64,256]{1,0:T(8,128)(2,1)S(1)} %shard_map.51), channel_id=1, source_target_pairs={{0,0},{1,1},{2,226},{3,227},{4,4},{5,5},{6,230},{7,231},{8,8},{9,9... | collective-permute-start | bytes 98312 | tf_op jit(solution)/shard_map/ppermute | solution.py:219
  14.9 16.8 %collective-permute-start.6 = (bf16[4,64,256]{2,1,0:T(8,128)(2,1)S(1)}, bf16[4,64,256]{2,1,0:T(8,128)(2,1)S(1)}, u32[]{:S(2)}, u32[]{:S(2)}) collective-permute-start(bf16[4,64,256]{2,1,0:T(8,128)(2,1)S(1)} %pad_maximum_fusion.3.refs_0_.refs_1_), channel_id=1, source_target_pairs={{0,24},{1,25},{2,26},{3,27},{4,28},{5,29},{6,30},{7,31},{8,0},{9,1... | collective-permute-start | bytes 393224 | tf_op jit(solution)/shard_map/ppermute | solution.py:219
  17.8 20.6 %collective-permute-start.7 = (bf16[2,256,256]{2,1,0:T(8,128)(2,1)S(1)}, bf16[2,256,256]{2,1,0:T(8,128)(2,1)S(1)}, u32[]{:S(2)}, u32[]{:S(2)}) collective-permute-start(bf16[2,256,256]{2,1,0:T(8,128)(2,1)S(1)} %get-tuple-element.19), channel_id=1, source_target_pairs={{0,4},{1,5},{2,6},{3,7},{4,2},{5,3},{6,0},{7,1},{8,12},{9,13},{10,... | collective-permute-start | bytes 786440 | tf_op jit(solution)/shard_map/ppermute | solution.py:219
  19.0 19.9 %collective-permute-start.8 = (bf16[2,256,256]{2,1,0:T(8,128)(2,1)S(1)}, bf16[2,256,256]{2,1,0:T(8,128)(2,1)S(1)}, u32[]{:S(2)}, u32[]{:S(2)}) collective-permute-start(bf16[2,256,256]{2,1,0:T(8,128)(2,1)S(1)} %get-tuple-element.20), channel_id=1, source_target_pairs={{0,2},{1,3},{2,0},{3,1},{4,6},{5,7},{6,4},{7,5},{8,10},{9,11},{10,... | collective-permute-start | bytes 786440 | tf_op jit(solution)/shard_map/ppermute | solution.py:219
  30.2 8.7 %collective-permute-start.9 = (bf16[2,256,256]{2,1,0:T(8,128)(2,1)S(1)}, bf16[2,256,256]{2,1,0:T(8,128)(2,1)S(1)}, u32[]{:S(2)}, u32[]{:S(2)}) collective-permute-start(bf16[2,256,256]{2,1,0:T(8,128)(2,1)S(1)} %get-tuple-element.21), channel_id=1, source_target_pairs={{0,6},{1,7},{2,4},{3,5},{4,0},{5,1},{6,2},{7,3},{8,14},{9,15},{10,... | collective-permute-start | bytes 786440 | tf_op jit(solution)/shard_map/ppermute | solution.py:219
  31.4 5.4 %collective-permute-start.5 = (bf16[4,64,256]{2,1,0:T(8,128)(2,1)S(1)}, bf16[4,64,256]{2,1,0:T(8,128)(2,1)S(1)}, u32[]{:S(2)}, u32[]{:S(2)}) collective-permute-start(bf16[4,64,256]{2,1,0:T(8,128)(2,1)S(1)} %pad_maximum_fusion.3.refs_0_.refs_1_), channel_id=1, source_target_pairs={{0,16},{1,17},{2,18},{3,19},{4,20},{5,21},{6,22},{7,23},{8,24},{9,... | collective-permute-start | bytes 393224 | tf_op jit(solution)/shard_map/ppermute | solution.py:219
  31.7 6.7 %collective-permute-start.4 = (bf16[4,64,256]{2,1,0:T(8,128)(2,1)S(1)}, bf16[4,64,256]{2,1,0:T(8,128)(2,1)S(1)}, u32[]{:S(2)}, u32[]{:S(2)}) collective-permute-start(bf16[4,64,256]{2,1,0:T(8,128)(2,1)S(1)} %pad_maximum_fusion.3.refs_0_.refs_1_), channel_id=1, source_target_pairs={{0,8},{1,9},{2,10},{3,11},{4,12},{5,13},{6,14},{7,15},{8,16},{9,17... | collective-permute-start | bytes 393224 | tf_op jit(solution)/shard_map/ppermute | solution.py:219
  39.0 5.8 %collective-permute-start.10 = (bf16[4,256,256]{2,1,0:T(8,128)(2,1)S(1)}, bf16[4,256,256]{2,1,0:T(8,128)(2,1)S(1)}, u32[]{:S(2)}, u32[]{:S(2)}) collective-permute-start(bf16[4,256,256]{2,1,0:T(8,128)(2,1)S(1)} %shard_map.53), channel_id=1, source_target_pairs={{0,1},{1,0},{2,3},{3,2},{4,5},{5,4},{6,7},{7,6},{8,9},{9,8},{10,11... | collective-permute-start | bytes 1572872 | tf_op jit(solution)/shard_map/ppermute | solution.py:219
  48.2 1.7 %collective-permute-start.11 = (f32[4,72,256]{2,1,0:T(8,128)S(1)}, f32[4,72,256]{2,1,0:T(8,128)S(1)}, u32[]{:S(2)}, u32[]{:S(2)}) collective-permute-start(f32[4,72,256]{2,1,0:T(8,128)S(1)} %get-tuple-element.23), channel_id=1, source_target_pairs={{0,1},{1,0},{2,3},{3,2},{4,5},{5,4},{6,7},{7,6},{8,9},{9,8},{10,11... | collective-permute-start | bytes 884744 | tf_op jit(solution)/shard_map/ppermute | solution.py:219
  49.9 5.1 %collective-permute-start.12 = (f32[2,72,256]{2,1,0:T(8,128)S(1)}, f32[2,72,256]{2,1,0:T(8,128)S(1)}, u32[]{:S(2)}, u32[]{:S(2)}) collective-permute-start(f32[2,72,256]{2,1,0:T(8,128)S(1)} %pad_maximum_fusion), channel_id=1, source_target_pairs={{0,6},{1,7},{2,4},{3,5},{4,0},{5,1},{6,2},{7,3},{8,14},{9,15},{10,... | collective-permute-start | bytes 442376 | tf_op jit(solution)/shard_map/ppermute | solution.py:219
  51.8 6.3 %collective-permute-start.13 = (f32[2,72,256]{2,1,0:T(8,128)S(1)}, f32[2,72,256]{2,1,0:T(8,128)S(1)}, u32[]{:S(2)}, u32[]{:S(2)}) collective-permute-start(f32[2,72,256]{2,1,0:T(8,128)S(1)} %pad_maximum_fusion.1), channel_id=1, source_target_pairs={{0,2},{1,3},{2,0},{3,1},{4,6},{5,7},{6,4},{7,5},{8,10},{9,11},{10,... | collective-permute-start | bytes 442376 | tf_op jit(solution)/shard_map/ppermute | solution.py:219
  52.7 9.6 %collective-permute-start.14 = (f32[2,72,256]{2,1,0:T(8,128)S(1)}, f32[2,72,256]{2,1,0:T(8,128)S(1)}, u32[]{:S(2)}, u32[]{:S(2)}) collective-permute-start(f32[2,72,256]{2,1,0:T(8,128)S(1)} %pad_maximum_fusion.2), channel_id=1, source_target_pairs={{0,4},{1,5},{2,6},{3,7},{4,2},{5,3},{6,0},{7,1},{8,12},{9,13},{10,... | collective-permute-start | bytes 442376 | tf_op jit(solution)/shard_map/ppermute | solution.py:219

commit v10 on v6

--- a/solution.py
+++ b/solution.py
@@ -79,38 +79,49 @@
         refs[-1][r] = m[1]
 
 
-def solve_kernel(place, bundles, theirs, *rest, scale):
-    sources = [s for r, m in enumerate(rest[:-9]) for s in (m.at[0], theirs.at[r])]
-    outs = rest[-9:-7]
-    high, low, goal, state, steps, sums, parts = rest[-7:]
-    groups = state.shape[0]
-    slots = len(sources) * CAP
+def blocks():
+    return iota((1, LANES), 1) // (LANES // PACK)
+
+
+def basis_of(bundles, g):
+    return jnp.concatenate([bundles[PACK * g + i] for i in range(PACK)], axis=0)
+
+
+def gram_kernel(bundles, high, low, steps, sums):
+    groups = high.shape[0]
     wide = LANES // PACK
-    block = iota((1, LANES), 1) // wide
+    block = blocks()
     same = iota((LANES, LANES), 0) // wide == iota((LANES, LANES), 1) // wide
-
-    def basis_of(g):
-        return jnp.concatenate([bundles[PACK * g + i] for i in range(PACK)], axis=0)
-
-    def pixels_of(local):
-        return jnp.concatenate([s[local * CAP : (local + 1) * CAP] for s in sources], axis=0)
-
     for g in range(groups):
-        basis = basis_of(g)
+        basis = basis_of(bundles, g)
         gram = jnp.where(same, dot_nt(basis, basis), 0.0)
         sums[g : g + 1] = jnp.sum(jnp.abs(gram), axis=0, keepdims=True)
         high[g], low[g] = split(gram)
-        found = dot_nt(jnp.concatenate([pixels_of(PACK * g + i) for i in range(PACK)], axis=0), basis)
-        aim = found[:slots]
-        for i in range(1, PACK):
-            aim = jnp.where(block == i, found[i * slots : (i + 1) * slots], aim)
-        goal[g] = aim
     total = sums[...]
     largest = jnp.zeros_like(total)
     for i in range(PACK):
         inside = block == i
         largest = jnp.where(inside, jnp.max(jnp.where(inside, total, 0.0), axis=1, keepdims=True), largest)
     steps[...] = 1.0 / largest
+
+
+def solve_kernel(place, bundles, high, low, steps, theirs, *rest, scale):
+    sources = [s for r, m in enumerate(rest[:-5]) for s in (m.at[0], theirs.at[r])]
+    outs = rest[-5:-3]
+    goal, state, parts = rest[-3:]
+    groups = state.shape[0]
+    slots = len(sources) * CAP
+    block = blocks()
+
+    def pixels_of(local):
+        return jnp.concatenate([s[local * CAP : (local + 1) * CAP] for s in sources], axis=0)
+
+    for g in range(groups):
+        found = dot_nt(jnp.concatenate([pixels_of(PACK * g + i) for i in range(PACK)], axis=0), basis_of(bundles, g))
+        aim = found[:slots]
+        for i in range(1, PACK):
+            aim = jnp.where(block == i, found[i * slots : (i + 1) * slots], aim)
+        goal[g] = aim
     for g in range(groups):
         state[g] = jnp.maximum(steps[g : g + 1] * goal[g], 0.0)
 
@@ -123,14 +134,14 @@
             state[g] = jnp.maximum(a - steps[g : g + 1] * (grad - goal[g]), 0.0)
         return carry
 
-    lax.fori_loop(1, ITERS, sweep, 0)
+    lax.fori_loop(1, ITERS, sweep, 0, unroll=True)
     parts[...] = jnp.zeros(parts.shape, f32)
     for g in range(groups):
         a = state[g]
         for s in range(len(sources)):
             outs[s % 2][s // 2, g * CAP : (g + 1) * CAP] = a[s * CAP : (s + 1) * CAP]
         spread = jnp.concatenate([jnp.where(block == i, a, 0.0) for i in range(PACK)], axis=0)
-        both = dot(jnp.concatenate(split(spread), axis=0), basis_of(g))
+        both = dot(jnp.concatenate(split(spread), axis=0), basis_of(bundles, g))
         fitted = both[: PACK * slots] + both[PACK * slots :]
         for i in range(PACK):
             misfit = pixels_of(PACK * g + i).astype(f32) - fitted[i * slots : (i + 1) * slots]
@@ -251,18 +262,23 @@
     below = groups * CAP
     slots = 2 * chips * CAP
     scale = bands * rows * n_pix / count
+    square = sds((groups, LANES, LANES), bf16)
+    grams = call(
+        gram_kernel,
+        None,
+        [gathered],
+        (square, square, sds((groups, LANES), f32)),
+        [vmem((groups, LANES), f32)],
+        16,
+    )
     solved = call(
         lambda *refs: solve_kernel(*refs, scale=scale),
         place,
-        [gathered, theirs, *received],
+        [gathered, *grams, theirs, *received],
         (sds((chips, below + 8, LANES), f32),) * 2,
         [
-            vmem((groups, LANES, LANES), bf16),
-            vmem((groups, LANES, LANES), bf16),
             vmem((groups, slots, LANES), f32),
             vmem((groups, slots, LANES), f32),
-            vmem((groups, LANES), f32),
-            vmem((groups, LANES), f32),
             vmem((2, count, LANES), f32),
         ],
         16,

time: 59.5 us -> 58.2 us (0.978)
  Pallas kernels: 9.88 us -> 9.14 us
    pallas_call x5 -> x6, Pallas kernels: 9.88 us -> 9.14 us  [call(): pl.pallas_call(kernel, out_shape=outs, in_specs=[pl.BlockSpec(memory_spac...]
  transfers between devices with their start and end apart: 10 -> 10, of which waited for: 7 -> 7; matrix products, arithmetic and copies ran while one was open for 0% -> 0% of each run, Pallas kernels for 4% -> 5%
where the time goes in v10:
time: 58.2 us; the launch traced here: 57.9 us
  starting transfers between devices  25.4 us (44%)
  waiting for transfers between devices  20.8 us (36%)
  Pallas kernels  9.14 us (16%)
  local copies, waits for them, and re-layouts  1.66 us (3%)
  between operations  0.7 us (1%)
    ppermute x8, waiting for transfers between devices, moved(): return lax.ppermute(array, ALL, pairs) if r or other else array  20.8 us
    ppermute x8, starting transfers between devices, moved(): return lax.ppermute(array, ALL, pairs) if r or other else array  14.8 us
    all_to_all x1, starting transfers between devices, exchanged(): lax.all_to_all(array, ALL, 0, 0, tiled=True, axis_index_groups=groups)  9.19 us
    pallas_call x6, Pallas kernels, call(): pl.pallas_call(kernel, out_shape=outs, in_specs=[pl.BlockSpec(memory_spac...  9.14 us
    unnamed x4, local copies, waits for them, and re-layouts  1.63 us
    ppermute x1, starting transfers between devices, per_device(): raw = lax.ppermute(bundles.transpose(0, 2, 1), ALL, swap)  1.5 us
  transfers between devices with their start and end apart: 10, of which 7 were waited for; matrix products, arithmetic and copies ran while one was open for 0% of the time, Pallas kernels for 5%

profile of v10, /device:TPU:1, one launch (start us, length us, event | category | flops | bytes accessed | tf_op | source)
XLA Modules:
  0.0 57.9 jit_solution(4044887596274019208)
XLA Ops:
  0.6 1.5 %collective-permute-start = (bf16[2,64,224]{2,1,0:T(8,128)(2,1)}, bf16[2,64,224]{2,1,0:T(8,128)(2,1)S(1)}, u32[]{:S(2)}, u32[]{:S(2)}) collective-permute-start(bf16[2,64,224]{2,1,0:T(8,128)(2,1)} %bitcast.11), channel_id=1, source_target_pairs={{0,0},{1,1},{2,226},{3,227},{4,4},{5,5},{6,230},{7,231},{8,8},{9,9... | collective-permute-start | bytes 172040 | tf_op jit(solution)/shard_map/ppermute | solution.py:246
  2.2 0.6 %copy-done.1 = s32[1024,1]{0,1:T(1,128)S(1)} copy-done((s32[1024,1]{0,1:T(1,128)S(1)}, s32[1024,1]{0,1:T(1,128)}, u32[]{:S(2)}) %copy-start.1) | copy-done | bytes 4120
  2.8 1.0 %copy-done = bf16[1024,224]{0,1:T(8,128)(2,1)S(1)} copy-done((bf16[1024,224]{0,1:T(8,128)(2,1)S(1)}, bf16[1024,224]{0,1:T(8,128)(2,1)}, u32[]{:S(2)}) %copy-start) | copy-done | bytes 458776
  3.8 2.2 %shard_map.50 = (bf16[2,256,256]{2,1,0:T(8,128)(2,1)S(1)}, bf16[2,256,256]{2,1,0:T(8,128)(2,1)S(1)}, bf16[2,256,256]{2,1,0:T(8,128)(2,1)S(1)}, bf16[2,256,256]{2,1,0:T(8,128)(2,1)S(1)}, s32[1,1024]{1,0:T(1,128)S(1)}) custom-call(s32[4]{0:T(128)S(1)} %pad_add_fusion.place.refs_0_, s32[1,1024]{1,0:T(1,128)S(1)} %bitcast.9, bf16[224,1024]{1,0:T(8,128)(2,1)S(1)} %bitcast.8), custom_call_target="tpu_custom_call" | custom-call | tf_op jit(solution)/shard_map/pallas_call | solution.py:196
  6.0 1.4 %shard_map.51 = bf16[16,64,256]{2,1,0:T(8,128)(2,1)} custom-call(s32[4]{0:T(128)S(1)} %pad_add_fusion.place.refs_0_, bf16[2,64,224]{2,1,0:T(8,128)(2,1)S(1)} %collective-permute-done.bundles, bf16[2,256,256]{2,1,0:T(8,128)(2,1)S(1)} %get-tuple-element.15.rest_0_.refs_0_.refs_6_), custom_call_target="tpu_custom_call" | custom-call | tf_op jit(solution)/shard_map/pallas_call | solution.py:196
  7.4 9.2 %all-to-all-start = ((bf16[16,64,256]{2,1,0:T(8,128)(2,1)}), bf16[16,64,256]{2,1,0:T(8,128)(2,1)S(1)}, u32[]{:S(2)}, u32[]{:S(2)}) async-start(bf16[16,64,256]{2,1,0:T(8,128)(2,1)} %shard_map.51), calls=%async_computation | async-start | bytes 1048576 | tf_op jit(solution)/shard_map/all_to_all | solution.py:218
  16.6 1.3 %collective-permute-start.1 = (bf16[2,256,256]{2,1,0:T(8,128)(2,1)S(1)}, bf16[2,256,256]{2,1,0:T(8,128)(2,1)S(1)}, u32[]{:S(2)}, u32[]{:S(2)}) collective-permute-start(bf16[2,256,256]{2,1,0:T(8,128)(2,1)S(1)} %get-tuple-element.19), channel_id=1, source_target_pairs={{0,4},{1,5},{2,6},{3,7},{4,2},{5,3},{6,0},{7,1},{8,12},{9,13},{10,... | collective-permute-start | bytes 786440 | tf_op jit(solution)/shard_map/ppermute | solution.py:235
  17.9 6.2 %collective-permute-start.2 = (bf16[2,256,256]{2,1,0:T(8,128)(2,1)S(1)}, bf16[2,256,256]{2,1,0:T(8,128)(2,1)S(1)}, u32[]{:S(2)}, u32[]{:S(2)}) collective-permute-start(bf16[2,256,256]{2,1,0:T(8,128)(2,1)S(1)} %get-tuple-element.20), channel_id=1, source_target_pairs={{0,2},{1,3},{2,0},{3,1},{4,6},{5,7},{6,4},{7,5},{8,10},{9,11},{10,... | collective-permute-start | bytes 786440 | tf_op jit(solution)/shard_map/ppermute | solution.py:235
  24.1 1.1 %collective-permute-start.3 = (bf16[2,256,256]{2,1,0:T(8,128)(2,1)S(1)}, bf16[2,256,256]{2,1,0:T(8,128)(2,1)S(1)}, u32[]{:S(2)}, u32[]{:S(2)}) collective-permute-start(bf16[2,256,256]{2,1,0:T(8,128)(2,1)S(1)} %get-tuple-element.21), channel_id=1, source_target_pairs={{0,6},{1,7},{2,4},{3,5},{4,0},{5,1},{6,2},{7,3},{8,14},{9,15},{10,... | collective-permute-start | bytes 786440 | tf_op jit(solution)/shard_map/ppermute | solution.py:235
  25.2 3.1 %collective-permute-done.1.refs_1_.refs_7_ = bf16[2,256,256]{2,1,0:T(8,128)(2,1)S(1)} collective-permute-done((bf16[2,256,256]{2,1,0:T(8,128)(2,1)S(1)}, bf16[2,256,256]{2,1,0:T(8,128)(2,1)S(1)}, u32[]{:S(2)}, u32[]{:S(2)}) %collective-permute-start.1) | collective-permute-done | bytes 262176 | tf_op jit(solution)/shard_map/ppermute | solution.py:235
  28.3 6.5 %collective-permute-done.2.refs_2_.refs_8_ = bf16[2,256,256]{2,1,0:T(8,128)(2,1)S(1)} collective-permute-done((bf16[2,256,256]{2,1,0:T(8,128)(2,1)S(1)}, bf16[2,256,256]{2,1,0:T(8,128)(2,1)S(1)}, u32[]{:S(2)}, u32[]{:S(2)}) %collective-permute-start.2) | collective-permute-done | bytes 262176 | tf_op jit(solution)/shard_map/ppermute | solution.py:235
  34.9 2.2 %collective-permute-start.4 = (bf16[4,256,256]{2,1,0:T(8,128)(2,1)S(1)}, bf16[4,256,256]{2,1,0:T(8,128)(2,1)S(1)}, u32[]{:S(2)}, u32[]{:S(2)}) collective-permute-start(bf16[4,256,256]{2,1,0:T(8,128)(2,1)S(1)} %shard_map.53), channel_id=1, source_target_pairs={{0,1},{1,0},{2,3},{3,2},{4,5},{5,4},{6,7},{7,6},{8,9},{9,8},{10,11... | collective-permute-start | bytes 1572872 | tf_op jit(solution)/shard_map/ppermute | solution.py:235
  37.1 0.5 shard_map.52
  37.6 1.0 %collective-permute-done.4.refs_5_ = bf16[4,256,256]{2,1,0:T(8,128)(2,1)S(1)} collective-permute-done((bf16[4,256,256]{2,1,0:T(8,128)(2,1)S(1)}, bf16[4,256,256]{2,1,0:T(8,128)(2,1)S(1)}, u32[]{:S(2)}, u32[]{:S(2)}) %collective-permute-start.4) | collective-permute-done | bytes 524320 | tf_op jit(solution)/shard_map/ppermute | solution.py:235
  38.6 3.6 %shard_map.54 = (f32[4,72,256]{2,1,0:T(8,128)S(1)}, f32[4,72,256]{2,1,0:T(8,128)S(1)}) custom-call(s32[4]{0:T(128)S(1)} %pad_add_fusion.place.refs_0_, bf16[16,64,256]{2,1,0:T(8,128)(2,1)S(1)} %all-to-all-done.bundles.refs_1_, bf16[4,256,256]{2,1,0:T(8,128)(2,1)S(1)} %get-tuple-element.16.refs_2_, bf16[4,256,256]{2,1,0:T(8,128)(2,1)S(1)} %get-tuple-element.17.refs_3_, ...), custom_call_target="tpu_custom_call" | custom-call | tf_op jit(solution)/shard_map/pallas_call | solution.py:196
  42.2 0.5 collective-permute-start.5
  42.7 1.2 %collective-permute-done.5.theirs = f32[4,72,256]{2,1,0:T(8,128)S(1)} collective-permute-done((f32[4,72,256]{2,1,0:T(8,128)S(1)}, f32[4,72,256]{2,1,0:T(8,128)S(1)}, u32[]{:S(2)}, u32[]{:S(2)}) %collective-permute-start.5) | collective-permute-done | bytes 294944 | tf_op jit(solution)/shard_map/ppermute | solution.py:235
  43.9 2.0 %collective-permute-start.6 = (f32[2,72,256]{2,1,0:T(8,128)S(1)}, f32[2,72,256]{2,1,0:T(8,128)S(1)}, u32[]{:S(2)}, u32[]{:S(2)}) collective-permute-start(f32[2,72,256]{2,1,0:T(8,128)S(1)} %pad_maximum_fusion), channel_id=1, source_target_pairs={{0,6},{1,7},{2,4},{3,5},{4,0},{5,1},{6,2},{7,3},{8,14},{9,15},{10,... | collective-permute-start | bytes 442376 | tf_op jit(solution)/shard_map/ppermute | solution.py:235
  45.9 0.9 %collective-permute-start.7 = (f32[2,72,256]{2,1,0:T(8,128)S(1)}, f32[2,72,256]{2,1,0:T(8,128)S(1)}, u32[]{:S(2)}, u32[]{:S(2)}) collective-permute-start(f32[2,72,256]{2,1,0:T(8,128)S(1)} %pad_maximum_fusion.1), channel_id=1, source_target_pairs={{0,2},{1,3},{2,0},{3,1},{4,6},{5,7},{6,4},{7,5},{8,10},{9,11},{10,... | collective-permute-start | bytes 442376 | tf_op jit(solution)/shard_map/ppermute | solution.py:235
  46.9 0.6 collective-permute-start.8
  47.4 1.6 %collective-permute-done.6.back1 = f32[2,72,256]{2,1,0:T(8,128)S(1)} collective-permute-done((f32[2,72,256]{2,1,0:T(8,128)S(1)}, f32[2,72,256]{2,1,0:T(8,128)S(1)}, u32[]{:S(2)}, u32[]{:S(2)}) %collective-permute-start.6) | collective-permute-done | bytes 147488 | tf_op jit(solution)/shard_map/ppermute | solution.py:235
  49.1 3.2 %collective-permute-done.7.back2 = f32[2,72,256]{2,1,0:T(8,128)S(1)} collective-permute-done((f32[2,72,256]{2,1,0:T(8,128)S(1)}, f32[2,72,256]{2,1,0:T(8,128)S(1)}, u32[]{:S(2)}, u32[]{:S(2)}) %collective-permute-start.7) | collective-permute-done | bytes 147488 | tf_op jit(solution)/shard_map/ppermute | solution.py:235
  52.2 4.2 %collective-permute-done.8.back3 = f32[2,72,256]{2,1,0:T(8,128)S(1)} collective-permute-done((f32[2,72,256]{2,1,0:T(8,128)S(1)}, f32[2,72,256]{2,1,0:T(8,128)S(1)}, u32[]{:S(2)}, u32[]{:S(2)}) %collective-permute-start.8) | collective-permute-done | bytes 147488 | tf_op jit(solution)/shard_map/ppermute | solution.py:235
  56.4 1.5 %shard_map.55 = (f32[64,1024]{1,0:T(8,128)}, f32[1,128]{1,0:T(1,128)}) custom-call(s32[1,1024]{1,0:T(1,128)S(1)} %get-tuple-element.14.code, f32[4,72,256]{2,1,0:T(8,128)S(1)} %get-tuple-element.22.mine, f32[4,72,256]{2,1,0:T(8,128)S(1)} %collective-permute-done.5.theirs, f32[2,72,256]{2,1,0:T(8,128)S(1)} %collective-permute-done.6.back1, ...), custom_call_target="tpu_custom_call" | custom-call | tf_op jit(solution)/shard_map/pallas_call | solution.py:196
  (12 shorter events, 0.2 us)
Async XLA Ops:
  0.6 5.4 %collective-permute-start = (bf16[2,64,224]{2,1,0:T(8,128)(2,1)}, bf16[2,64,224]{2,1,0:T(8,128)(2,1)S(1)}, u32[]{:S(2)}, u32[]{:S(2)}) collective-permute-start(bf16[2,64,224]{2,1,0:T(8,128)(2,1)} %bitcast.11), channel_id=1, source_target_pairs={{0,0},{1,1},{2,226},{3,227},{4,4},{5,5},{6,230},{7,231},{8,8},{9,9... | collective-permute-start | bytes 172040 | tf_op jit(solution)/shard_map/ppermute | solution.py:246
  2.1 0.7 %copy-start.1 = (s32[1024,1]{0,1:T(1,128)S(1)}, s32[1024,1]{0,1:T(1,128)}, u32[]{:S(2)}) copy-start(s32[1024,1]{0,1:T(1,128)} %param.5) | copy-start | bytes 12292
  2.8 1.0 %copy-start = (bf16[1024,224]{0,1:T(8,128)(2,1)S(1)}, bf16[1024,224]{0,1:T(8,128)(2,1)}, u32[]{:S(2)}) copy-start(bf16[1024,224]{0,1:T(8,128)(2,1)} %param.3) | copy-start | bytes 1376260
  7.4 29.7 %all-to-all-start = ((bf16[16,64,256]{2,1,0:T(8,128)(2,1)}), bf16[16,64,256]{2,1,0:T(8,128)(2,1)S(1)}, u32[]{:S(2)}, u32[]{:S(2)}) async-start(bf16[16,64,256]{2,1,0:T(8,128)(2,1)} %shard_map.51), calls=%async_computation | async-start | bytes 1048576 | tf_op jit(solution)/shard_map/all_to_all | solution.py:218
  16.6 11.7 %collective-permute-start.1 = (bf16[2,256,256]{2,1,0:T(8,128)(2,1)S(1)}, bf16[2,256,256]{2,1,0:T(8,128)(2,1)S(1)}, u32[]{:S(2)}, u32[]{:S(2)}) collective-permute-start(bf16[2,256,256]{2,1,0:T(8,128)(2,1)S(1)} %get-tuple-element.19), channel_id=1, source_target_pairs={{0,4},{1,5},{2,6},{3,7},{4,2},{5,3},{6,0},{7,1},{8,12},{9,13},{10,... | collective-permute-start | bytes 786440 | tf_op jit(solution)/shard_map/ppermute | solution.py:235
  17.9 16.9 %collective-permute-start.2 = (bf16[2,256,256]{2,1,0:T(8,128)(2,1)S(1)}, bf16[2,256,256]{2,1,0:T(8,128)(2,1)S(1)}, u32[]{:S(2)}, u32[]{:S(2)}) collective-permute-start(bf16[2,256,256]{2,1,0:T(8,128)(2,1)S(1)} %get-tuple-element.20), channel_id=1, source_target_pairs={{0,2},{1,3},{2,0},{3,1},{4,6},{5,7},{6,4},{7,5},{8,10},{9,11},{10,... | collective-permute-start | bytes 786440 | tf_op jit(solution)/shard_map/ppermute | solution.py:235
  24.1 10.8 %collective-permute-start.3 = (bf16[2,256,256]{2,1,0:T(8,128)(2,1)S(1)}, bf16[2,256,256]{2,1,0:T(8,128)(2,1)S(1)}, u32[]{:S(2)}, u32[]{:S(2)}) collective-permute-start(bf16[2,256,256]{2,1,0:T(8,128)(2,1)S(1)} %get-tuple-element.21), channel_id=1, source_target_pairs={{0,6},{1,7},{2,4},{3,5},{4,0},{5,1},{6,2},{7,3},{8,14},{9,15},{10,... | collective-permute-start | bytes 786440 | tf_op jit(solution)/shard_map/ppermute | solution.py:235
  34.9 3.7 %collective-permute-start.4 = (bf16[4,256,256]{2,1,0:T(8,128)(2,1)S(1)}, bf16[4,256,256]{2,1,0:T(8,128)(2,1)S(1)}, u32[]{:S(2)}, u32[]{:S(2)}) collective-permute-start(bf16[4,256,256]{2,1,0:T(8,128)(2,1)S(1)} %shard_map.53), channel_id=1, source_target_pairs={{0,1},{1,0},{2,3},{3,2},{4,5},{5,4},{6,7},{7,6},{8,9},{9,8},{10,11... | collective-permute-start | bytes 1572872 | tf_op jit(solution)/shard_map/ppermute | solution.py:235
  42.2 1.7 %collective-permute-start.5 = (f32[4,72,256]{2,1,0:T(8,128)S(1)}, f32[4,72,256]{2,1,0:T(8,128)S(1)}, u32[]{:S(2)}, u32[]{:S(2)}) collective-permute-start(f32[4,72,256]{2,1,0:T(8,128)S(1)} %get-tuple-element.23), channel_id=1, source_target_pairs={{0,1},{1,0},{2,3},{3,2},{4,5},{5,4},{6,7},{7,6},{8,9},{9,8},{10,11... | collective-permute-start | bytes 884744 | tf_op jit(solution)/shard_map/ppermute | solution.py:235
  43.9 5.1 %collective-permute-start.6 = (f32[2,72,256]{2,1,0:T(8,128)S(1)}, f32[2,72,256]{2,1,0:T(8,128)S(1)}, u32[]{:S(2)}, u32[]{:S(2)}) collective-permute-start(f32[2,72,256]{2,1,0:T(8,128)S(1)} %pad_maximum_fusion), channel_id=1, source_target_pairs={{0,6},{1,7},{2,4},{3,5},{4,0},{5,1},{6,2},{7,3},{8,14},{9,15},{10,... | collective-permute-start | bytes 442376 | tf_op jit(solution)/shard_map/ppermute | solution.py:235
  45.9 6.3 %collective-permute-start.7 = (f32[2,72,256]{2,1,0:T(8,128)S(1)}, f32[2,72,256]{2,1,0:T(8,128)S(1)}, u32[]{:S(2)}, u32[]{:S(2)}) collective-permute-start(f32[2,72,256]{2,1,0:T(8,128)S(1)} %pad_maximum_fusion.1), channel_id=1, source_target_pairs={{0,2},{1,3},{2,0},{3,1},{4,6},{5,7},{6,4},{7,5},{8,10},{9,11},{10,... | collective-permute-start | bytes 442376 | tf_op jit(solution)/shard_map/ppermute | solution.py:235
  46.9 9.6 %collective-permute-start.8 = (f32[2,72,256]{2,1,0:T(8,128)S(1)}, f32[2,72,256]{2,1,0:T(8,128)S(1)}, u32[]{:S(2)}, u32[]{:S(2)}) collective-permute-start(f32[2,72,256]{2,1,0:T(8,128)S(1)} %pad_maximum_fusion.2), channel_id=1, source_target_pairs={{0,4},{1,5},{2,6},{3,7},{4,2},{5,3},{6,0},{7,1},{8,12},{9,13},{10,... | collective-permute-start | bytes 442376 | tf_op jit(solution)/shard_map/ppermute | solution.py:235

commit v11 on v9

--- a/solution.py
+++ b/solution.py
@@ -42,8 +42,7 @@
     out[:, :bands] = bundles[place[0]]
 
 
-def slots_kernel(place, labels, pixels, *rest):
-    outs, (code, wide, ranks) = rest[:-3], rest[-3:]
+def slots_kernel(place, labels, pixels, send, code, wide, ranks):
     bands, rows = pixels.shape
     count = rows // (CAP // 2)
     wide[:bands] = pixels[...]
@@ -60,21 +59,21 @@
         carry = running[:, chunk - 1 :]
     rank = ranks[...].astype(jnp.int32)
     other = (label >> 6) ^ (place[2] >> 2)
-    chip = other * 2 + (label >> 1 & 1)
-    handler = (chip - place[3] & 3) * 2 + (label + place[0] & 1)
+    handler = (label >> 1 & 1) * 4 + other * 2 + (label + place[0] & 1)
     local = (place[2] - ((label >> 4) ^ other * 3) & 3) * PACK + (place[4] - (label >> 2) & 3)
     slot = local * CAP + rank
-    held = outs[0].shape[1]
-    for d in range(2 * len(outs)):
+    chips, _, held = send.shape[:3]
+    for d in range(2 * chips):
         key = jnp.where(handler == d, slot, -1)
-        outs[d // 2][d % 2] = dot_nt(one_hot(iota((held, rows), 0) == key), wide[...]).astype(bf16)
+        send[d // 2, d % 2] = dot_nt(one_hot(iota((held, rows), 0) == key), wide[...]).astype(bf16)
     table_row = handler * (held // PACK) + (local >> 2) * CAP + rank
     code[...] = (local & 3) * 1024 + table_row
 
 
-def stack_kernel(*refs):
-    for r, m in enumerate(refs[: refs[-1].shape[0]]):
-        refs[-1][r] = m[1]
+def stack_kernel(received, *rest):
+    out = rest[-1]
+    for j in range(out.shape[0]):
+        out[j] = received[j, 1]
 
 
 def blocks():
@@ -105,10 +104,9 @@
 
 
 def solve_kernel(place, *refs, scale):
-    bundles, (high, low, steps, theirs, *rest) = refs[:PACK], refs[PACK:]
-    sources = [s for r, m in enumerate(rest[:-5]) for s in (m.at[0], theirs.at[r])]
-    outs = rest[-5:-3]
-    goal, state, parts = rest[-3:]
+    bundles, (high, low, steps, received, theirs, mine_out, theirs_out, goal, state, parts) = refs[:-10], refs[-10:]
+    sources = [s for j in range(theirs.shape[0]) for s in (received.at[j, 0], theirs.at[j])]
+    outs = (mine_out, theirs_out)
     groups = state.shape[0]
     slots = len(sources) * CAP
     block = blocks()
@@ -147,11 +145,10 @@
             misfit = pixels_of(PACK * g + i).astype(f32) - fitted[i * slots : (i + 1) * slots]
             square = misfit * misfit
             z, y = (place[2] & 4) + (place[2] - g & 3) ^ 7 * place[1], place[4] - i & 3
-            bundle = 16 * z + 4 * y + 2 * (place[3] & 1) + place[0]
+            bundle = 16 * z + 4 * y + 2 * place[3] + place[0]
             for half in range(2):
-                both = square[2 * half * CAP : 2 * (half + 1) * CAP]
-                both = both + square[2 * (half + 2) * CAP : 2 * (half + 3) * CAP]
-                parts[half, pl.ds(bundle, 1), :] = jnp.sum(both, axis=0, keepdims=True)
+                rows = slice(half * slots // 2, (half + 1) * slots // 2)
+                parts[half, pl.ds(bundle, 1), :] = jnp.sum(square[rows], axis=0, keepdims=True)
     bands = LANES - 32
     below = groups * CAP
     for half in range(2):
@@ -159,16 +156,15 @@
         lines = jnp.where(iota(lines.shape, 0) < bands, lines, 0.0)
         energy = jnp.sum(lines, axis=0, keepdims=True) / scale
         energy = jnp.concatenate([energy, jnp.zeros_like(energy)], axis=1)
-        for r in (half, half + 2):
+        for j in (2 * half, 2 * half + 1):
             for i in range(2):
-                outs[i][r, below:] = jnp.broadcast_to(energy, (8, LANES))
-
-
-def return_kernel(code, mine, theirs, back1, back2, back3, chosen, energy):
+                outs[i][j, below:] = jnp.broadcast_to(energy, (8, LANES))
+
+
+def return_kernel(code, back, chosen, energy):
     rows = code.shape[1]
-    held, lanes = mine.shape[1] - 8, mine.shape[2]
-    backs = (back1, back2, back3)
-    tables = [mine.at[0], theirs.at[0]] + [b.at[i] for b in backs for i in range(2)]
+    held, lanes = back.shape[2] - 8, back.shape[3]
+    tables = [back.at[j, i] for j in range(back.shape[0]) for i in range(2)]
     handlers = len(tables)
     wide = lanes // PACK
     codes = code[...]
@@ -208,6 +204,17 @@
     return [(b // 8, b // 2 % 4, b % 2, p // 2, p % 2) for b in range(n_blk) for p in range(n_pix)]
 
 
+def grouped(spots, key):
+    groups = {}
+    for index, spot in enumerate(spots):
+        groups.setdefault(key(*spot), []).append(index)
+    return list(groups.values())
+
+
+def exchanged(array, groups):
+    return lax.all_to_all(array, ALL, 0, 0, tiled=True, axis_index_groups=groups)
+
+
 def per_device(pixels, bundles, assign):
     rows, bands = pixels.shape
     owned, _, width = bundles.shape
@@ -218,35 +225,29 @@
     def sent(array, target):
         return lax.ppermute(array, ALL, [(there[s], there[target(*s)]) for s in spots])
 
-    def along_x(array, r):
-        def target(z, y, xl, xh, c):
-            x = 2 * xh + xl + r & 3
-            return z, y, x & 1, x >> 1, c
-
-        return sent(array, target) if r else array
+    row = grouped(spots, lambda z, y, xl, xh, c: (z, y, c))
 
     def to_sibling(array):
         return sent(array, lambda z, y, xl, xh, c: (z, y, xl, xh, c ^ 1))
 
     blk, pix = lax.axis_index("blk"), lax.axis_index("pix")
     z, x_hi = blk >> 3, pix >> 1
-    place = jnp.stack([pix & 1, x_hi, z, 2 * x_hi + (blk & 1), blk >> 1 & 3]).astype(jnp.int32)
+    place = jnp.stack([pix & 1, x_hi, z, blk & 1, blk >> 1 & 3]).astype(jnp.int32)
     sds = jax.ShapeDtypeStruct
-    chips = 4
+    chips = len(row[0])
     count = n_blk * owned
     groups = 4
     held = groups * PACK * CAP
 
-    *sends, code = call(
+    send, code = call(
         slots_kernel,
         place,
         [assign.reshape(1, rows), pixels.T],
-        (sds((2, held, LANES), bf16),) * chips + (sds((1, rows), jnp.int32),),
+        (sds((chips, 2, held, LANES), bf16), sds((1, rows), jnp.int32)),
         [vmem((LANES, rows), bf16), vmem((1, rows), f32)],
         16,
     )
-    received = [along_x(send, r) for r, send in enumerate(sends)]
-    basis = call(prep_kernel, place, [bundles.transpose(0, 2, 1)], sds((width, LANES), bf16), [], 4, [sends[0]])
+    basis = call(prep_kernel, place, [bundles.transpose(0, 2, 1)], sds((width, LANES), bf16), [], 4, [send])
     pieces = []
     for q in range(groups):
 
@@ -259,8 +260,8 @@
     gathered = [levels]
     for r in range(1, PACK):
         gathered.append(sent(levels, lambda z, y, xl, xh, c: (z, y + r & 3, xl, xh, c)))
-    stacked = call(stack_kernel, None, received, sds((chips, held, LANES), bf16), [], 8, gathered[1:])
-    theirs = to_sibling(stacked)
+    received = exchanged(send, row)
+    theirs = to_sibling(call(stack_kernel, None, [received], sds((chips, held, LANES), bf16), [], 8, gathered[1:]))
 
     below = groups * CAP
     slots = 2 * chips * CAP
@@ -277,7 +278,7 @@
     solved = call(
         lambda *refs: solve_kernel(*refs, scale=scale),
         place,
-        [*gathered, *grams, theirs, *received],
+        [*gathered, *grams, received, theirs],
         (sds((chips, below + 8, LANES), f32),) * 2,
         [
             vmem((groups, slots, LANES), f32),
@@ -286,10 +287,9 @@
         ],
         16,
     )
-    mine, others = solved[0], to_sibling(solved[1])
-    back = [along_x(jnp.stack([mine[r], others[r]]), -r) for r in range(1, chips)]
+    back = exchanged(jnp.stack([solved[0], to_sibling(solved[1])], axis=1), row)
     outs = (sds((width, rows), f32), sds((1, count), f32))
-    chosen, energy = call(return_kernel, None, [code, mine, others, *back], outs, [], 16)
+    chosen, energy = call(return_kernel, None, [code, back], outs, [], 16)
     return chosen.T, energy
 
 

time: 63.9 us -> 65.3 us (1.022)
  blocking collectives: 0 us -> 22.9 us
  starting transfers between devices: 31.9 us -> 18.4 us
  waiting for transfers between devices: 21.2 us -> 11.8 us
  Pallas kernels: 8.16 us -> 9.28 us
    all_to_all x0 -> x1, blocking collectives: none -> 22.9 us  [exchanged(): lax.all_to_all(array, ALL, 0, 0, tiled=True, axis_index_groups=groups)]
    ppermute x15 -> x9, starting transfers between devices: 31.9 us -> 13.4 us  [sent(): lax.ppermute(array, ALL, [(there[s], there[target(*s)]) for s in spots])]
    ppermute x15 -> x9, waiting for transfers between devices: 21.2 us -> 11.8 us  [sent(): lax.ppermute(array, ALL, [(there[s], there[target(*s)]) for s in spots])]
    all_to_all x0 -> x1, starting transfers between devices: none -> 4.97 us  [exchanged(): lax.all_to_all(array, ALL, 0, 0, tiled=True, axis_index_groups=groups)]
    pallas_call x6, Pallas kernels: 8.16 us -> 9.28 us  [call(): pl.pallas_call(kernel, out_shape=outs, in_specs=[pl.BlockSpec(memory_spac...]
  transfers between devices with their start and end apart: 15 -> 10, of which waited for: 10 -> 7; matrix products, arithmetic and copies ran while one was open for 0% -> 0% of each run, Pallas kernels for 1% -> 2%
where the time goes in v11:
time: 65.3 us; the launch traced here: 64.7 us
  blocking collectives  22.9 us (35%)
  starting transfers between devices  18.4 us (28%)
  waiting for transfers between devices  11.8 us (18%)
  Pallas kernels  9.28 us (14%)
  local copies, waits for them, and re-layouts  1.7 us (3%)
  between operations  0.71 us (1%)
    all_to_all x1, blocking collectives, exchanged(): lax.all_to_all(array, ALL, 0, 0, tiled=True, axis_index_groups=groups)  22.9 us
    ppermute x9, starting transfers between devices, sent(): lax.ppermute(array, ALL, [(there[s], there[target(*s)]) for s in spots])  13.4 us
    ppermute x9, waiting for transfers between devices, sent(): lax.ppermute(array, ALL, [(there[s], there[target(*s)]) for s in spots])  11.8 us
    pallas_call x6, Pallas kernels, call(): pl.pallas_call(kernel, out_shape=outs, in_specs=[pl.BlockSpec(memory_spac...  9.28 us
    all_to_all x1, starting transfers between devices, exchanged(): lax.all_to_all(array, ALL, 0, 0, tiled=True, axis_index_groups=groups)  4.97 us
    unnamed x6, local copies, waits for them, and re-layouts  1.62 us
  transfers between devices with their start and end apart: 10, of which 7 were waited for; matrix products, arithmetic and copies ran while one was open for 0% of the time, Pallas kernels for 2%

profile of v11, /device:TPU:1, one launch (start us, length us, event | category | flops | bytes accessed | tf_op | source)
XLA Modules:
  0.0 64.7 jit_solution(115558502584193408)
XLA Ops:
  0.7 0.6 copy-done.2
  1.3 1.0 %copy-done = bf16[1024,224]{0,1:T(8,128)(2,1)S(1)} copy-done((bf16[1024,224]{0,1:T(8,128)(2,1)S(1)}, bf16[1024,224]{0,1:T(8,128)(2,1)}, u32[]{:S(2)}) %copy-start) | copy-done | bytes 458776
  2.3 3.2 %shard_map.50 = (bf16[4,2,256,256]{3,2,1,0:T(8,128)(2,1)}, s32[1,1024]{1,0:T(1,128)S(1)}) custom-call(s32[5]{0:T(128)S(1)} %stack.47.place.refs_0_, s32[1,1024]{1,0:T(1,128)S(1)} %bitcast.18, bf16[224,1024]{1,0:T(8,128)(2,1)S(1)} %bitcast.15), custom_call_target="tpu_custom_call" | custom-call | tf_op jit(solution)/shard_map/pallas_call | solution.py:193
  5.5 5.0 %all-to-all-start = ((bf16[4,2,256,256]{3,2,1,0:T(8,128)(2,1)}), bf16[4,2,256,256]{3,2,1,0:T(8,128)(2,1)S(1)}, u32[]{:S(2)}, u32[]{:S(2)}) async-start(bf16[4,2,256,256]{3,2,1,0:T(8,128)(2,1)} %get-tuple-element.12.rest_0_), calls=%async_computation | async-start | bytes 2097152 | tf_op jit(solution)/shard_map/all_to_all | solution.py:215
  10.5 0.6 shard_map.51
  11.1 4.4 %collective-permute-start.3 = (bf16[64,256]{1,0:T(8,128)(2,1)S(1)}, bf16[64,256]{1,0:T(8,128)(2,1)S(1)}, u32[]{:S(2)}, u32[]{:S(2)}) collective-permute-start(bf16[64,256]{1,0:T(8,128)(2,1)S(1)} %shard_map.51), channel_id=1, source_target_pairs={{0,96},{1,97},{2,194},{3,195},{4,100},{5,101},{6,198},{7,199},{8,1... | collective-permute-start | bytes 98312 | tf_op jit(solution)/shard_map/ppermute | solution.py:226
  15.5 0.4 collective-permute-start.1
  15.9 0.7 %collective-permute-start = (bf16[64,256]{1,0:T(8,128)(2,1)S(1)}, bf16[64,256]{1,0:T(8,128)(2,1)S(1)}, u32[]{:S(2)}, u32[]{:S(2)}) collective-permute-start(bf16[64,256]{1,0:T(8,128)(2,1)S(1)} %shard_map.51), channel_id=1, source_target_pairs={{0,0},{1,1},{2,226},{3,227},{4,4},{5,5},{6,230},{7,231},{8,8},{9,9... | collective-permute-start | bytes 98312 | tf_op jit(solution)/shard_map/ppermute | solution.py:226
  16.5 2.9 %collective-permute-done.2 = bf16[64,256]{1,0:T(8,128)(2,1)S(1)} collective-permute-done((bf16[64,256]{1,0:T(8,128)(2,1)S(1)}, bf16[64,256]{1,0:T(8,128)(2,1)S(1)}, u32[]{:S(2)}, u32[]{:S(2)}) %collective-permute-start.2) | collective-permute-done | bytes 32800 | tf_op jit(solution)/shard_map/ppermute | solution.py:226
  19.4 0.9 %collective-permute-done.1 = bf16[64,256]{1,0:T(8,128)(2,1)S(1)} collective-permute-done((bf16[64,256]{1,0:T(8,128)(2,1)S(1)}, bf16[64,256]{1,0:T(8,128)(2,1)S(1)}, u32[]{:S(2)}, u32[]{:S(2)}) %collective-permute-start.1) | collective-permute-done | bytes 32800 | tf_op jit(solution)/shard_map/ppermute | solution.py:226
  20.4 2.8 %collective-permute-start.6 = (bf16[4,64,256]{2,1,0:T(8,128)(2,1)S(1)}, bf16[4,64,256]{2,1,0:T(8,128)(2,1)S(1)}, u32[]{:S(2)}, u32[]{:S(2)}) collective-permute-start(bf16[4,64,256]{2,1,0:T(8,128)(2,1)S(1)} %pad_maximum_fusion.1.refs_0_.refs_1_), channel_id=1, source_target_pairs={{0,24},{1,25},{2,26},{3,27},{4,28},{5,29},{6,30},{7,31},{8,0},{9,1... | collective-permute-start | bytes 393224 | tf_op jit(solution)/shard_map/ppermute | solution.py:226
  23.2 0.3 collective-permute-start.5
  23.5 0.7 %collective-permute-start.4 = (bf16[4,64,256]{2,1,0:T(8,128)(2,1)S(1)}, bf16[4,64,256]{2,1,0:T(8,128)(2,1)S(1)}, u32[]{:S(2)}, u32[]{:S(2)}) collective-permute-start(bf16[4,64,256]{2,1,0:T(8,128)(2,1)S(1)} %pad_maximum_fusion.1.refs_0_.refs_1_), channel_id=1, source_target_pairs={{0,8},{1,9},{2,10},{3,11},{4,12},{5,13},{6,14},{7,15},{8,16},{9,17... | collective-permute-start | bytes 393224 | tf_op jit(solution)/shard_map/ppermute | solution.py:226
  24.2 1.6 %collective-permute-done.6.refs_3_.rest_2_.refs_4_ = bf16[4,64,256]{2,1,0:T(8,128)(2,1)S(1)} collective-permute-done((bf16[4,64,256]{2,1,0:T(8,128)(2,1)S(1)}, bf16[4,64,256]{2,1,0:T(8,128)(2,1)S(1)}, u32[]{:S(2)}, u32[]{:S(2)}) %collective-permute-start.6) | collective-permute-done | bytes 131104 | tf_op jit(solution)/shard_map/ppermute | solution.py:226
  25.8 2.8 %collective-permute-done.5.refs_2_.rest_1_.refs_3_ = bf16[4,64,256]{2,1,0:T(8,128)(2,1)S(1)} collective-permute-done((bf16[4,64,256]{2,1,0:T(8,128)(2,1)S(1)}, bf16[4,64,256]{2,1,0:T(8,128)(2,1)S(1)}, u32[]{:S(2)}, u32[]{:S(2)}) %collective-permute-start.5) | collective-permute-done | bytes 131104 | tf_op jit(solution)/shard_map/ppermute | solution.py:226
  28.6 1.3 %collective-permute-done.4.refs_1_.rest_0_.refs_2_ = bf16[4,64,256]{2,1,0:T(8,128)(2,1)S(1)} collective-permute-done((bf16[4,64,256]{2,1,0:T(8,128)(2,1)S(1)}, bf16[4,64,256]{2,1,0:T(8,128)(2,1)S(1)}, u32[]{:S(2)}, u32[]{:S(2)}) %collective-permute-start.4) | collective-permute-done | bytes 131104 | tf_op jit(solution)/shard_map/ppermute | solution.py:226
  29.9 3.6 %collective-permute-start.7 = (bf16[4,256,256]{2,1,0:T(8,128)(2,1)S(1)}, bf16[4,256,256]{2,1,0:T(8,128)(2,1)S(1)}, u32[]{:S(2)}, u32[]{:S(2)}) collective-permute-start(bf16[4,256,256]{2,1,0:T(8,128)(2,1)S(1)} %shard_map.53), channel_id=1, source_target_pairs={{0,1},{1,0},{2,3},{3,2},{4,5},{5,4},{6,7},{7,6},{8,9},{9,8},{10,11... | collective-permute-start | bytes 1572872 | tf_op jit(solution)/shard_map/ppermute | solution.py:226
  33.6 0.5 shard_map.52
  34.0 1.0 %collective-permute-done.7.refs_9_ = bf16[4,256,256]{2,1,0:T(8,128)(2,1)S(1)} collective-permute-done((bf16[4,256,256]{2,1,0:T(8,128)(2,1)S(1)}, bf16[4,256,256]{2,1,0:T(8,128)(2,1)S(1)}, u32[]{:S(2)}, u32[]{:S(2)}) %collective-permute-start.7) | collective-permute-done | bytes 524320 | tf_op jit(solution)/shard_map/ppermute | solution.py:226
  35.1 3.6 %shard_map.54 = (f32[4,72,256]{2,1,0:T(8,128)S(1)}, f32[4,72,256]{2,1,0:T(8,128)S(1)}) custom-call(s32[5]{0:T(128)S(1)} %stack.47.place.refs_0_, bf16[4,64,256]{2,1,0:T(8,128)(2,1)S(1)} %pad_maximum_fusion.1.refs_0_.refs_1_, bf16[4,64,256]{2,1,0:T(8,128)(2,1)S(1)} %collective-permute-done.4.refs_1_.rest_0_.refs_2_, ...), custom_call_target="tpu_custom_call" | custom-call | tf_op jit(solution)/shard_map/pallas_call | solution.py:193
  38.7 0.5 collective-permute-start.8
  39.1 1.2 %collective-permute-done.8 = f32[4,72,256]{2,1,0:T(8,128)S(1)} collective-permute-done((f32[4,72,256]{2,1,0:T(8,128)S(1)}, f32[4,72,256]{2,1,0:T(8,128)S(1)}, u32[]{:S(2)}, u32[]{:S(2)}) %collective-permute-start.8) | collective-permute-done | bytes 294944 | tf_op jit(solution)/shard_map/ppermute | solution.py:226
  40.4 22.9 %all_to_all.10.back = f32[4,2,72,256]{3,2,1,0:T(8,128)S(1)} all-to-all(f32[4,2,72,256]{3,2,1,0:T(8,128)S(1)} %pad_maximum_fusion), channel_id=1, replica_groups={{0,2,4,6},{1,3,5,7},{8,10,12,14},{9,11,13,15},{16,18,20,22},{17,19,21,2..., dimensions={0} | all-to-all | bytes 1179648 | tf_op jit(solution)/shard_map/all_to_all | solution.py:215
  63.3 1.5 %shard_map.55 = (f32[64,1024]{1,0:T(8,128)}, f32[1,128]{1,0:T(1,128)}) custom-call(s32[1,1024]{1,0:T(1,128)S(1)} %get-tuple-element.11.code, f32[4,2,72,256]{3,2,1,0:T(8,128)S(1)} %all_to_all.10.back), custom_call_target="tpu_custom_call" | custom-call | tf_op jit(solution)/shard_map/pallas_call | solution.py:193
  (12 shorter events, 0.2 us)
Async XLA Ops:
  0.6 0.7 %copy-start.2 = (s32[1024,1]{0,1:T(1,128)S(1)}, s32[1024,1]{0,1:T(1,128)}, u32[]{:S(2)}) copy-start(s32[1024,1]{0,1:T(1,128)} %param.5) | copy-start | bytes 12292
  1.3 1.0 %copy-start = (bf16[1024,224]{0,1:T(8,128)(2,1)S(1)}, bf16[1024,224]{0,1:T(8,128)(2,1)}, u32[]{:S(2)}) copy-start(bf16[1024,224]{0,1:T(8,128)(2,1)} %param.3) | copy-start | bytes 1376260
  5.5 5.0 %copy-start.1 = (bf16[2,224,64]{1,2,0:T(8,128)(2,1)S(1)}, bf16[2,224,64]{1,2,0:T(8,128)(2,1)}, u32[]{:S(2)}) copy-start(bf16[2,224,64]{1,2,0:T(8,128)(2,1)} %param.4) | copy-start | bytes 172036
  5.5 24.4 %all-to-all-start = ((bf16[4,2,256,256]{3,2,1,0:T(8,128)(2,1)}), bf16[4,2,256,256]{3,2,1,0:T(8,128)(2,1)S(1)}, u32[]{:S(2)}, u32[]{:S(2)}) async-start(bf16[4,2,256,256]{3,2,1,0:T(8,128)(2,1)} %get-tuple-element.12.rest_0_), calls=%async_computation | async-start | bytes 2097152 | tf_op jit(solution)/shard_map/all_to_all | solution.py:215
  11.1 5.5 %collective-permute-start.3 = (bf16[64,256]{1,0:T(8,128)(2,1)S(1)}, bf16[64,256]{1,0:T(8,128)(2,1)S(1)}, u32[]{:S(2)}, u32[]{:S(2)}) collective-permute-start(bf16[64,256]{1,0:T(8,128)(2,1)S(1)} %shard_map.51), channel_id=1, source_target_pairs={{0,96},{1,97},{2,194},{3,195},{4,100},{5,101},{6,198},{7,199},{8,1... | collective-permute-start | bytes 98312 | tf_op jit(solution)/shard_map/ppermute | solution.py:226
  15.5 4.0 %collective-permute-start.2 = (bf16[64,256]{1,0:T(8,128)(2,1)S(1)}, bf16[64,256]{1,0:T(8,128)(2,1)S(1)}, u32[]{:S(2)}, u32[]{:S(2)}) collective-permute-start(bf16[64,256]{1,0:T(8,128)(2,1)S(1)} %shard_map.51), channel_id=1, source_target_pairs={{0,64},{1,65},{2,162},{3,163},{4,68},{5,69},{6,166},{7,167},{8,72}... | collective-permute-start | bytes 98312 | tf_op jit(solution)/shard_map/ppermute | solution.py:226
  15.5 4.9 %collective-permute-start.1 = (bf16[64,256]{1,0:T(8,128)(2,1)S(1)}, bf16[64,256]{1,0:T(8,128)(2,1)S(1)}, u32[]{:S(2)}, u32[]{:S(2)}) collective-permute-start(bf16[64,256]{1,0:T(8,128)(2,1)S(1)} %shard_map.51), channel_id=1, source_target_pairs={{0,32},{1,33},{2,130},{3,131},{4,36},{5,37},{6,134},{7,135},{8,40}... | collective-permute-start | bytes 98312 | tf_op jit(solution)/shard_map/ppermute | solution.py:226
  15.9 4.5 %collective-permute-start = (bf16[64,256]{1,0:T(8,128)(2,1)S(1)}, bf16[64,256]{1,0:T(8,128)(2,1)S(1)}, u32[]{:S(2)}, u32[]{:S(2)}) collective-permute-start(bf16[64,256]{1,0:T(8,128)(2,1)S(1)} %shard_map.51), channel_id=1, source_target_pairs={{0,0},{1,1},{2,226},{3,227},{4,4},{5,5},{6,230},{7,231},{8,8},{9,9... | collective-permute-start | bytes 98312 | tf_op jit(solution)/shard_map/ppermute | solution.py:226
  20.4 5.5 %collective-permute-start.6 = (bf16[4,64,256]{2,1,0:T(8,128)(2,1)S(1)}, bf16[4,64,256]{2,1,0:T(8,128)(2,1)S(1)}, u32[]{:S(2)}, u32[]{:S(2)}) collective-permute-start(bf16[4,64,256]{2,1,0:T(8,128)(2,1)S(1)} %pad_maximum_fusion.1.refs_0_.refs_1_), channel_id=1, source_target_pairs={{0,24},{1,25},{2,26},{3,27},{4,28},{5,29},{6,30},{7,31},{8,0},{9,1... | collective-permute-start | bytes 393224 | tf_op jit(solution)/shard_map/ppermute | solution.py:226
  23.2 5.4 %collective-permute-start.5 = (bf16[4,64,256]{2,1,0:T(8,128)(2,1)S(1)}, bf16[4,64,256]{2,1,0:T(8,128)(2,1)S(1)}, u32[]{:S(2)}, u32[]{:S(2)}) collective-permute-start(bf16[4,64,256]{2,1,0:T(8,128)(2,1)S(1)} %pad_maximum_fusion.1.refs_0_.refs_1_), channel_id=1, source_target_pairs={{0,16},{1,17},{2,18},{3,19},{4,20},{5,21},{6,22},{7,23},{8,24},{9,... | collective-permute-start | bytes 393224 | tf_op jit(solution)/shard_map/ppermute | solution.py:226
  23.5 6.4 %collective-permute-start.4 = (bf16[4,64,256]{2,1,0:T(8,128)(2,1)S(1)}, bf16[4,64,256]{2,1,0:T(8,128)(2,1)S(1)}, u32[]{:S(2)}, u32[]{:S(2)}) collective-permute-start(bf16[4,64,256]{2,1,0:T(8,128)(2,1)S(1)} %pad_maximum_fusion.1.refs_0_.refs_1_), channel_id=1, source_target_pairs={{0,8},{1,9},{2,10},{3,11},{4,12},{5,13},{6,14},{7,15},{8,16},{9,17... | collective-permute-start | bytes 393224 | tf_op jit(solution)/shard_map/ppermute | solution.py:226
  29.9 5.1 %collective-permute-start.7 = (bf16[4,256,256]{2,1,0:T(8,128)(2,1)S(1)}, bf16[4,256,256]{2,1,0:T(8,128)(2,1)S(1)}, u32[]{:S(2)}, u32[]{:S(2)}) collective-permute-start(bf16[4,256,256]{2,1,0:T(8,128)(2,1)S(1)} %shard_map.53), channel_id=1, source_target_pairs={{0,1},{1,0},{2,3},{3,2},{4,5},{5,4},{6,7},{7,6},{8,9},{9,8},{10,11... | collective-permute-start | bytes 1572872 | tf_op jit(solution)/shard_map/ppermute | solution.py:226
  38.7 1.7 %collective-permute-start.8 = (f32[4,72,256]{2,1,0:T(8,128)S(1)}, f32[4,72,256]{2,1,0:T(8,128)S(1)}, u32[]{:S(2)}, u32[]{:S(2)}) collective-permute-start(f32[4,72,256]{2,1,0:T(8,128)S(1)} %get-tuple-element.17), channel_id=1, source_target_pairs={{0,1},{1,0},{2,3},{3,2},{4,5},{5,4},{6,7},{7,6},{8,9},{9,8},{10,11... | collective-permute-start | bytes 884744 | tf_op jit(solution)/shard_map/ppermute | solution.py:226

commit v12 on v10

--- a/solution.py
+++ b/solution.py
@@ -163,17 +163,20 @@
                 outs[i][r, below:] = jnp.broadcast_to(energy, (8, LANES))
 
 
-def return_kernel(code, mine, theirs, back1, back2, back3, chosen, energy):
+def pick_kernel(code, *rest):
+    pick = rest[-1]
+    pick[...] = one_hot(iota(pick.shape, 0) == code[...] & 1023)
+
+
+def return_kernel(code, pick, mine, theirs, back1, back2, back3, chosen, energy):
     rows = code.shape[1]
     held, lanes = mine.shape[1] - 8, mine.shape[2]
     backs = (back1, back2, back3)
     tables = [mine.at[0], theirs.at[0]] + [b.at[i] for b in backs for i in range(2)]
-    handlers = len(tables)
     wide = lanes // PACK
     codes = code[...]
-    pick = one_hot(iota((handlers * held, rows), 0) == codes & 1023)
     table = jnp.concatenate([t[:held] for t in tables], axis=0).T
-    found = dot(jnp.concatenate(split(table), axis=0), pick)
+    found = dot(jnp.concatenate(split(table), axis=0), pick[...])
     found = found[:lanes] + found[lanes:]
     which = codes >> 10
     result = found[:wide]
@@ -285,8 +288,9 @@
     )
     mine, others = solved[0], moved(solved[1], 0, 1)
     back = [moved(jnp.stack([mine[r], others[r]]), -r, 0) for r in range(1, chips)]
+    pick = call(pick_kernel, None, [code], sds((2 * chips * below, rows), bf16), [], 8, [solved[0]])
     outs = (sds((width, rows), f32), sds((1, count), f32))
-    chosen, energy = call(return_kernel, None, [code, mine, others, *back], outs, [], 16)
+    chosen, energy = call(return_kernel, None, [code, pick, mine, others, *back], outs, [], 16)
     return chosen.T, energy
 
 

time: 58.2 us -> 58.2 us (level)
    pallas_call x6 -> x7, Pallas kernels: 9.14 us -> 9.32 us  [call(): pl.pallas_call(kernel, out_shape=outs, in_specs=[pl.BlockSpec(memory_spac...]
where the time goes in v12:
time: 58.2 us; the launch traced here: 57.9 us
  starting transfers between devices  25.4 us (44%)
  waiting for transfers between devices  20.7 us (36%)
  Pallas kernels  9.32 us (16%)
  local copies, waits for them, and re-layouts  1.66 us (3%)
  between operations  0.7 us (1%)
    ppermute x8, waiting for transfers between devices, moved(): return lax.ppermute(array, ALL, pairs) if r or other else array  20.7 us
    ppermute x8, starting transfers between devices, moved(): return lax.ppermute(array, ALL, pairs) if r or other else array  14.8 us
    pallas_call x7, Pallas kernels, call(): pl.pallas_call(kernel, out_shape=outs, in_specs=[pl.BlockSpec(memory_spac...  9.32 us
    all_to_all x1, starting transfers between devices, exchanged(): lax.all_to_all(array, ALL, 0, 0, tiled=True, axis_index_groups=groups)  9.19 us
    unnamed x4, local copies, waits for them, and re-layouts  1.63 us
    ppermute x1, starting transfers between devices, per_device(): raw = lax.ppermute(bundles.transpose(0, 2, 1), ALL, swap)  1.5 us
  transfers between devices with their start and end apart: 10, of which 7 were waited for; matrix products, arithmetic and copies ran while one was open for 0% of the time, Pallas kernels for 5%

profile of v12, /device:TPU:1, one launch (start us, length us, event | category | flops | bytes accessed | tf_op | source)
XLA Modules:
  0.0 57.9 jit_solution(7878505910368580988)
XLA Ops:
  0.6 1.5 %collective-permute-start = (bf16[2,64,224]{2,1,0:T(8,128)(2,1)}, bf16[2,64,224]{2,1,0:T(8,128)(2,1)S(1)}, u32[]{:S(2)}, u32[]{:S(2)}) collective-permute-start(bf16[2,64,224]{2,1,0:T(8,128)(2,1)} %bitcast.11), channel_id=1, source_target_pairs={{0,0},{1,1},{2,226},{3,227},{4,4},{5,5},{6,230},{7,231},{8,8},{9,9... | collective-permute-start | bytes 172040 | tf_op jit(solution)/shard_map/ppermute | solution.py:249
  2.2 0.6 %copy-done.1 = s32[1024,1]{0,1:T(1,128)S(1)} copy-done((s32[1024,1]{0,1:T(1,128)S(1)}, s32[1024,1]{0,1:T(1,128)}, u32[]{:S(2)}) %copy-start.1) | copy-done | bytes 4120
  2.8 1.0 %copy-done = bf16[1024,224]{0,1:T(8,128)(2,1)S(1)} copy-done((bf16[1024,224]{0,1:T(8,128)(2,1)S(1)}, bf16[1024,224]{0,1:T(8,128)(2,1)}, u32[]{:S(2)}) %copy-start) | copy-done | bytes 458776
  3.8 2.2 %shard_map.50 = (bf16[2,256,256]{2,1,0:T(8,128)(2,1)S(1)}, bf16[2,256,256]{2,1,0:T(8,128)(2,1)S(1)}, bf16[2,256,256]{2,1,0:T(8,128)(2,1)S(1)}, bf16[2,256,256]{2,1,0:T(8,128)(2,1)S(1)}, s32[1,1024]{1,0:T(1,128)S(1)}) custom-call(s32[4]{0:T(128)S(1)} %pad_add_fusion.place.refs_0_, s32[1,1024]{1,0:T(1,128)S(1)} %bitcast.9, bf16[224,1024]{1,0:T(8,128)(2,1)S(1)} %bitcast.8), custom_call_target="tpu_custom_call" | custom-call | tf_op jit(solution)/shard_map/pallas_call | solution.py:199
  6.0 1.4 %shard_map.51 = bf16[16,64,256]{2,1,0:T(8,128)(2,1)} custom-call(s32[4]{0:T(128)S(1)} %pad_add_fusion.place.refs_0_, bf16[2,64,224]{2,1,0:T(8,128)(2,1)S(1)} %collective-permute-done.bundles, bf16[2,256,256]{2,1,0:T(8,128)(2,1)S(1)} %get-tuple-element.15.rest_0_.refs_0_.refs_6_), custom_call_target="tpu_custom_call" | custom-call | tf_op jit(solution)/shard_map/pallas_call | solution.py:199
  7.4 9.2 %all-to-all-start = ((bf16[16,64,256]{2,1,0:T(8,128)(2,1)}), bf16[16,64,256]{2,1,0:T(8,128)(2,1)S(1)}, u32[]{:S(2)}, u32[]{:S(2)}) async-start(bf16[16,64,256]{2,1,0:T(8,128)(2,1)} %shard_map.51), calls=%async_computation | async-start | bytes 1048576 | tf_op jit(solution)/shard_map/all_to_all | solution.py:221
  16.6 1.3 %collective-permute-start.1 = (bf16[2,256,256]{2,1,0:T(8,128)(2,1)S(1)}, bf16[2,256,256]{2,1,0:T(8,128)(2,1)S(1)}, u32[]{:S(2)}, u32[]{:S(2)}) collective-permute-start(bf16[2,256,256]{2,1,0:T(8,128)(2,1)S(1)} %get-tuple-element.19), channel_id=1, source_target_pairs={{0,4},{1,5},{2,6},{3,7},{4,2},{5,3},{6,0},{7,1},{8,12},{9,13},{10,... | collective-permute-start | bytes 786440 | tf_op jit(solution)/shard_map/ppermute | solution.py:238
  17.9 6.2 %collective-permute-start.2 = (bf16[2,256,256]{2,1,0:T(8,128)(2,1)S(1)}, bf16[2,256,256]{2,1,0:T(8,128)(2,1)S(1)}, u32[]{:S(2)}, u32[]{:S(2)}) collective-permute-start(bf16[2,256,256]{2,1,0:T(8,128)(2,1)S(1)} %get-tuple-element.20), channel_id=1, source_target_pairs={{0,2},{1,3},{2,0},{3,1},{4,6},{5,7},{6,4},{7,5},{8,10},{9,11},{10,... | collective-permute-start | bytes 786440 | tf_op jit(solution)/shard_map/ppermute | solution.py:238
  24.1 1.1 %collective-permute-start.3 = (bf16[2,256,256]{2,1,0:T(8,128)(2,1)S(1)}, bf16[2,256,256]{2,1,0:T(8,128)(2,1)S(1)}, u32[]{:S(2)}, u32[]{:S(2)}) collective-permute-start(bf16[2,256,256]{2,1,0:T(8,128)(2,1)S(1)} %get-tuple-element.21), channel_id=1, source_target_pairs={{0,6},{1,7},{2,4},{3,5},{4,0},{5,1},{6,2},{7,3},{8,14},{9,15},{10,... | collective-permute-start | bytes 786440 | tf_op jit(solution)/shard_map/ppermute | solution.py:238
  25.2 3.1 %collective-permute-done.1.refs_1_.refs_7_ = bf16[2,256,256]{2,1,0:T(8,128)(2,1)S(1)} collective-permute-done((bf16[2,256,256]{2,1,0:T(8,128)(2,1)S(1)}, bf16[2,256,256]{2,1,0:T(8,128)(2,1)S(1)}, u32[]{:S(2)}, u32[]{:S(2)}) %collective-permute-start.1) | collective-permute-done | bytes 262176 | tf_op jit(solution)/shard_map/ppermute | solution.py:238
  28.3 6.5 %collective-permute-done.2.refs_2_.refs_8_ = bf16[2,256,256]{2,1,0:T(8,128)(2,1)S(1)} collective-permute-done((bf16[2,256,256]{2,1,0:T(8,128)(2,1)S(1)}, bf16[2,256,256]{2,1,0:T(8,128)(2,1)S(1)}, u32[]{:S(2)}, u32[]{:S(2)}) %collective-permute-start.2) | collective-permute-done | bytes 262176 | tf_op jit(solution)/shard_map/ppermute | solution.py:238
  34.9 2.2 %collective-permute-start.4 = (bf16[4,256,256]{2,1,0:T(8,128)(2,1)S(1)}, bf16[4,256,256]{2,1,0:T(8,128)(2,1)S(1)}, u32[]{:S(2)}, u32[]{:S(2)}) collective-permute-start(bf16[4,256,256]{2,1,0:T(8,128)(2,1)S(1)} %shard_map.53), channel_id=1, source_target_pairs={{0,1},{1,0},{2,3},{3,2},{4,5},{5,4},{6,7},{7,6},{8,9},{9,8},{10,11... | collective-permute-start | bytes 1572872 | tf_op jit(solution)/shard_map/ppermute | solution.py:238
  37.1 0.5 shard_map.52
  37.6 1.0 %collective-permute-done.4.refs_5_ = bf16[4,256,256]{2,1,0:T(8,128)(2,1)S(1)} collective-permute-done((bf16[4,256,256]{2,1,0:T(8,128)(2,1)S(1)}, bf16[4,256,256]{2,1,0:T(8,128)(2,1)S(1)}, u32[]{:S(2)}, u32[]{:S(2)}) %collective-permute-start.4) | collective-permute-done | bytes 524320 | tf_op jit(solution)/shard_map/ppermute | solution.py:238
  38.6 3.6 %shard_map.54 = (f32[4,72,256]{2,1,0:T(8,128)S(1)}, f32[4,72,256]{2,1,0:T(8,128)S(1)}) custom-call(s32[4]{0:T(128)S(1)} %pad_add_fusion.place.refs_0_, bf16[16,64,256]{2,1,0:T(8,128)(2,1)S(1)} %all-to-all-done.bundles.refs_1_, bf16[4,256,256]{2,1,0:T(8,128)(2,1)S(1)} %get-tuple-element.16.refs_2_, bf16[4,256,256]{2,1,0:T(8,128)(2,1)S(1)} %get-tuple-element.17.refs_3_, ...), custom_call_target="tpu_custom_call" | custom-call | tf_op jit(solution)/shard_map/pallas_call | solution.py:199
  42.2 0.5 collective-permute-start.5
  42.7 1.2 %collective-permute-done.5.theirs = f32[4,72,256]{2,1,0:T(8,128)S(1)} collective-permute-done((f32[4,72,256]{2,1,0:T(8,128)S(1)}, f32[4,72,256]{2,1,0:T(8,128)S(1)}, u32[]{:S(2)}, u32[]{:S(2)}) %collective-permute-start.5) | collective-permute-done | bytes 294944 | tf_op jit(solution)/shard_map/ppermute | solution.py:238
  43.9 2.0 %collective-permute-start.6 = (f32[2,72,256]{2,1,0:T(8,128)S(1)}, f32[2,72,256]{2,1,0:T(8,128)S(1)}, u32[]{:S(2)}, u32[]{:S(2)}) collective-permute-start(f32[2,72,256]{2,1,0:T(8,128)S(1)} %pad_maximum_fusion), channel_id=1, source_target_pairs={{0,6},{1,7},{2,4},{3,5},{4,0},{5,1},{6,2},{7,3},{8,14},{9,15},{10,... | collective-permute-start | bytes 442376 | tf_op jit(solution)/shard_map/ppermute | solution.py:238
  45.9 0.9 %collective-permute-start.7 = (f32[2,72,256]{2,1,0:T(8,128)S(1)}, f32[2,72,256]{2,1,0:T(8,128)S(1)}, u32[]{:S(2)}, u32[]{:S(2)}) collective-permute-start(f32[2,72,256]{2,1,0:T(8,128)S(1)} %pad_maximum_fusion.1), channel_id=1, source_target_pairs={{0,2},{1,3},{2,0},{3,1},{4,6},{5,7},{6,4},{7,5},{8,10},{9,11},{10,... | collective-permute-start | bytes 442376 | tf_op jit(solution)/shard_map/ppermute | solution.py:238
  46.9 0.6 collective-permute-start.8
  47.6 1.5 %collective-permute-done.6.back1 = f32[2,72,256]{2,1,0:T(8,128)S(1)} collective-permute-done((f32[2,72,256]{2,1,0:T(8,128)S(1)}, f32[2,72,256]{2,1,0:T(8,128)S(1)}, u32[]{:S(2)}, u32[]{:S(2)}) %collective-permute-start.6) | collective-permute-done | bytes 147488 | tf_op jit(solution)/shard_map/ppermute | solution.py:238
  49.1 3.2 %collective-permute-done.7.back2 = f32[2,72,256]{2,1,0:T(8,128)S(1)} collective-permute-done((f32[2,72,256]{2,1,0:T(8,128)S(1)}, f32[2,72,256]{2,1,0:T(8,128)S(1)}, u32[]{:S(2)}, u32[]{:S(2)}) %collective-permute-start.7) | collective-permute-done | bytes 147488 | tf_op jit(solution)/shard_map/ppermute | solution.py:238
  52.2 4.2 %collective-permute-done.8.back3 = f32[2,72,256]{2,1,0:T(8,128)S(1)} collective-permute-done((f32[2,72,256]{2,1,0:T(8,128)S(1)}, f32[2,72,256]{2,1,0:T(8,128)S(1)}, u32[]{:S(2)}, u32[]{:S(2)}) %collective-permute-start.8) | collective-permute-done | bytes 147488 | tf_op jit(solution)/shard_map/ppermute | solution.py:238
  56.4 1.5 %shard_map.56 = (f32[64,1024]{1,0:T(8,128)}, f32[1,128]{1,0:T(1,128)}) custom-call(s32[1,1024]{1,0:T(1,128)S(1)} %get-tuple-element.14.code, bf16[512,1024]{1,0:T(8,128)(2,1)S(1)} %shard_map.55.pick, f32[4,72,256]{2,1,0:T(8,128)S(1)} %get-tuple-element.22.rest_0_.mine, f32[4,72,256]{2,1,0:T(8,128)S(1)} %collective-permute-done.5.theirs, ...), custom_call_target="tpu_custom_call" | custom-call | tf_op jit(solution)/shard_map/pallas_call | solution.py:199
  (13 shorter events, 0.4 us)
Async XLA Ops:
  0.6 5.4 %collective-permute-start = (bf16[2,64,224]{2,1,0:T(8,128)(2,1)}, bf16[2,64,224]{2,1,0:T(8,128)(2,1)S(1)}, u32[]{:S(2)}, u32[]{:S(2)}) collective-permute-start(bf16[2,64,224]{2,1,0:T(8,128)(2,1)} %bitcast.11), channel_id=1, source_target_pairs={{0,0},{1,1},{2,226},{3,227},{4,4},{5,5},{6,230},{7,231},{8,8},{9,9... | collective-permute-start | bytes 172040 | tf_op jit(solution)/shard_map/ppermute | solution.py:249
  2.1 0.7 %copy-start.1 = (s32[1024,1]{0,1:T(1,128)S(1)}, s32[1024,1]{0,1:T(1,128)}, u32[]{:S(2)}) copy-start(s32[1024,1]{0,1:T(1,128)} %param.5) | copy-start | bytes 12292
  2.8 1.0 %copy-start = (bf16[1024,224]{0,1:T(8,128)(2,1)S(1)}, bf16[1024,224]{0,1:T(8,128)(2,1)}, u32[]{:S(2)}) copy-start(bf16[1024,224]{0,1:T(8,128)(2,1)} %param.3) | copy-start | bytes 1376260
  7.4 29.7 %all-to-all-start = ((bf16[16,64,256]{2,1,0:T(8,128)(2,1)}), bf16[16,64,256]{2,1,0:T(8,128)(2,1)S(1)}, u32[]{:S(2)}, u32[]{:S(2)}) async-start(bf16[16,64,256]{2,1,0:T(8,128)(2,1)} %shard_map.51), calls=%async_computation | async-start | bytes 1048576 | tf_op jit(solution)/shard_map/all_to_all | solution.py:221
  16.6 11.7 %collective-permute-start.1 = (bf16[2,256,256]{2,1,0:T(8,128)(2,1)S(1)}, bf16[2,256,256]{2,1,0:T(8,128)(2,1)S(1)}, u32[]{:S(2)}, u32[]{:S(2)}) collective-permute-start(bf16[2,256,256]{2,1,0:T(8,128)(2,1)S(1)} %get-tuple-element.19), channel_id=1, source_target_pairs={{0,4},{1,5},{2,6},{3,7},{4,2},{5,3},{6,0},{7,1},{8,12},{9,13},{10,... | collective-permute-start | bytes 786440 | tf_op jit(solution)/shard_map/ppermute | solution.py:238
  17.9 16.9 %collective-permute-start.2 = (bf16[2,256,256]{2,1,0:T(8,128)(2,1)S(1)}, bf16[2,256,256]{2,1,0:T(8,128)(2,1)S(1)}, u32[]{:S(2)}, u32[]{:S(2)}) collective-permute-start(bf16[2,256,256]{2,1,0:T(8,128)(2,1)S(1)} %get-tuple-element.20), channel_id=1, source_target_pairs={{0,2},{1,3},{2,0},{3,1},{4,6},{5,7},{6,4},{7,5},{8,10},{9,11},{10,... | collective-permute-start | bytes 786440 | tf_op jit(solution)/shard_map/ppermute | solution.py:238
  24.1 10.8 %collective-permute-start.3 = (bf16[2,256,256]{2,1,0:T(8,128)(2,1)S(1)}, bf16[2,256,256]{2,1,0:T(8,128)(2,1)S(1)}, u32[]{:S(2)}, u32[]{:S(2)}) collective-permute-start(bf16[2,256,256]{2,1,0:T(8,128)(2,1)S(1)} %get-tuple-element.21), channel_id=1, source_target_pairs={{0,6},{1,7},{2,4},{3,5},{4,0},{5,1},{6,2},{7,3},{8,14},{9,15},{10,... | collective-permute-start | bytes 786440 | tf_op jit(solution)/shard_map/ppermute | solution.py:238
  34.9 3.7 %collective-permute-start.4 = (bf16[4,256,256]{2,1,0:T(8,128)(2,1)S(1)}, bf16[4,256,256]{2,1,0:T(8,128)(2,1)S(1)}, u32[]{:S(2)}, u32[]{:S(2)}) collective-permute-start(bf16[4,256,256]{2,1,0:T(8,128)(2,1)S(1)} %shard_map.53), channel_id=1, source_target_pairs={{0,1},{1,0},{2,3},{3,2},{4,5},{5,4},{6,7},{7,6},{8,9},{9,8},{10,11... | collective-permute-start | bytes 1572872 | tf_op jit(solution)/shard_map/ppermute | solution.py:238
  42.2 1.7 %collective-permute-start.5 = (f32[4,72,256]{2,1,0:T(8,128)S(1)}, f32[4,72,256]{2,1,0:T(8,128)S(1)}, u32[]{:S(2)}, u32[]{:S(2)}) collective-permute-start(f32[4,72,256]{2,1,0:T(8,128)S(1)} %get-tuple-element.23), channel_id=1, source_target_pairs={{0,1},{1,0},{2,3},{3,2},{4,5},{5,4},{6,7},{7,6},{8,9},{9,8},{10,11... | collective-permute-start | bytes 884744 | tf_op jit(solution)/shard_map/ppermute | solution.py:238
  43.9 5.1 %collective-permute-start.6 = (f32[2,72,256]{2,1,0:T(8,128)S(1)}, f32[2,72,256]{2,1,0:T(8,128)S(1)}, u32[]{:S(2)}, u32[]{:S(2)}) collective-permute-start(f32[2,72,256]{2,1,0:T(8,128)S(1)} %pad_maximum_fusion), channel_id=1, source_target_pairs={{0,6},{1,7},{2,4},{3,5},{4,0},{5,1},{6,2},{7,3},{8,14},{9,15},{10,... | collective-permute-start | bytes 442376 | tf_op jit(solution)/shard_map/ppermute | solution.py:238
  45.9 6.3 %collective-permute-start.7 = (f32[2,72,256]{2,1,0:T(8,128)S(1)}, f32[2,72,256]{2,1,0:T(8,128)S(1)}, u32[]{:S(2)}, u32[]{:S(2)}) collective-permute-start(f32[2,72,256]{2,1,0:T(8,128)S(1)} %pad_maximum_fusion.1), channel_id=1, source_target_pairs={{0,2},{1,3},{2,0},{3,1},{4,6},{5,7},{6,4},{7,5},{8,10},{9,11},{10,... | collective-permute-start | bytes 442376 | tf_op jit(solution)/shard_map/ppermute | solution.py:238
  46.9 9.6 %collective-permute-start.8 = (f32[2,72,256]{2,1,0:T(8,128)S(1)}, f32[2,72,256]{2,1,0:T(8,128)S(1)}, u32[]{:S(2)}, u32[]{:S(2)}) collective-permute-start(f32[2,72,256]{2,1,0:T(8,128)S(1)} %pad_maximum_fusion.2), channel_id=1, source_target_pairs={{0,4},{1,5},{2,6},{3,7},{4,2},{5,3},{6,0},{7,1},{8,12},{9,13},{10,... | collective-permute-start | bytes 442376 | tf_op jit(solution)/shard_map/ppermute | solution.py:238
